TPU v7x, 512 devices: a whole 4x8x8 slice. The times are simulated.
512 devices in a mesh: grp: 32 (over z, x), sub: 16 (over y, core).
Axes of the slice: x: 4, y: 8, z: 8, core: 2. Of those that a mesh axis runs over, the one named last changes fastest.
Arguments:
- field: float32 [2048, 2, 16, 256], P(('grp', 'sub')), may hold values from -6 to 6
- source: float32 [2048, 2, 16, 256], P(('grp', 'sub')), may hold values from -6 to 6
- patch_of_slot: int32 [2048], P(('grp', 'sub')), may hold values from -1 to 47, as said below
- neighbour: int32 [2048, 6], P(('grp', 'sub')), may hold values from -1 to 63, as said below
- wave_index: int32 [2048], P(('grp', 'sub')), may hold values from 0 to 15
- wave_table: float32 [16], replicated, may hold values from 0.02 to 0.2
Outputs:
- corrected: float32 [2048, 2, 16, 256], P(('grp', 'sub'))
Inputs may be any that keep to these rules, and one draw needn't show every extreme that they name: `patch_of_slot`: in each slab every patch 0 to 47 is held by exactly one slot; each device holds 2 to 4 patches in its first slots, the rest -1; in every slab some device holds 4 and some 2. `neighbour`: consistent with patch_of_slot and the slab grid: -1 exactly for empty slots, for faces on the grid's boundary.
All inputs are finite; a program needn't handle non-finite values.
Results may differ from a plain program's by a relative error of at most 0.0003.
Values sent between devices are 32-bit elements; how exact they have to be, the bound alone decides.
No kernel may reach another device: no remote copies, remote signals or barrier semaphores. Data moves between devices by JAX's collectives and lax.ppermute only.
A program may use at most 64 MiB of HBM per device.

v0:
```python
import jax
import jax.numpy as jnp
from jax import lax
from jax.experimental import pallas as pl
from jax.experimental.pallas import tpu as pltpu
from jax.sharding import PartitionSpec as P

PZ = 4
PY = 12
PATCHES = PY * PZ
EDGE = 16
CELLS = EDGE * EDGE
SLOTS = 4
NS = 16
LIVE = NS * SLOTS
LANES = 128

omega_fine = 0.7
omega_coarse = 0.6
shift_imag = 0.5

HI = lax.Precision.HIGHEST
F32 = jnp.float32
VM = pl.BlockSpec(memory_space=pltpu.VMEM)
SM = pl.BlockSpec(memory_space=pltpu.SMEM)


def call(body, outs, ins, scratch=()):
    return pl.pallas_call(
        body,
        out_shape=[jax.ShapeDtypeStruct(shape, F32) for shape in outs],
        in_specs=[SM if a.dtype == jnp.int32 or a.ndim == 1 else VM for a in ins],
        out_specs=[VM] * len(outs),
        scratch_shapes=[pltpu.VMEM(shape, F32) for shape in scratch],
    )(*ins)


def iota(shape, dim):
    return lax.broadcasted_iota(jnp.int32, shape, dim)


def lane_roll(x, shift):
    return pltpu.roll(x, shift % x.shape[1], 1)


def row_roll(x, shift):
    return pltpu.roll(x, shift % x.shape[0], 0)


def in_plane(u):
    shape = u[0].shape
    lane = iota(shape, 1)
    patch = iota(shape, 0)
    k = lane % EDGE
    col = patch % PZ
    not_last, not_first = k < EDGE - 1, k > 0
    has_next, has_prev = col < PZ - 1, col > 0
    out = []
    ahead = [lane_roll(t, -EDGE) for t in u]
    behind = [lane_roll(t, EDGE) for t in u]
    low, high = lane >= EDGE, lane < LANES - EDGE
    y_next = [
        jnp.where(high, ahead[0], ahead[1]),
        jnp.where(high, ahead[1], jnp.where(patch < PATCHES - PZ, row_roll(ahead[0], -PZ), 0.0)),
    ]
    y_prev = [
        jnp.where(low, behind[0], jnp.where(patch >= PZ, row_roll(behind[1], PZ), 0.0)),
        jnp.where(low, behind[1], behind[0]),
    ]
    for h in range(2):
        t = u[h]
        z_next = jnp.where(
            not_last,
            lane_roll(t, -1),
            jnp.where(has_next, row_roll(lane_roll(t, EDGE - 1), -1), 0.0),
        )
        z_prev = jnp.where(
            not_first,
            lane_roll(t, 1),
            jnp.where(has_prev, row_roll(lane_roll(t, 1 - EDGE), 1), 0.0),
        )
        out.append((z_next + z_prev) + (y_next[h] + y_prev[h]))
    return out


def halves(ref, index):
    return [ref[index, :, :LANES], ref[index, :, LANES:]]


def put(ref, index, pair):
    ref[index, :, :LANES] = pair[0]
    ref[index, :, LANES:] = pair[1]


def field_of(ref, first):
    return [halves(ref, first), halves(ref, first + 1)]


def choose(flag, a, b):
    return [[jnp.where(flag, x, y) for x, y in zip(p, q)] for p, q in zip(a, b)]


def around(u, before, after):
    return [
        [n + (x + y) for n, x, y in zip(in_plane(u[part]), before[part], after[part])]
        for part in range(2)
    ]


def diagonal(wave):
    real, imag = 6.0 - wave, shift_imag * wave
    return real, imag


def smooth(u, total, rights, wave):
    real, imag = diagonal(wave)
    scale = omega_fine / (real * real + imag * imag)
    real, imag = real * scale, imag * scale
    keep = 1.0 - omega_fine
    out_re, out_im = [], []
    for h in range(2):
        a = rights[0][h] + total[0][h]
        b = rights[1][h] + total[1][h]
        out_re.append(keep * u[0][h] + (a * real - b * imag))
        out_im.append(keep * u[1][h] + (a * imag + b * real))
    return [out_re, out_im]


def residual(u, total, rights, wave):
    real, imag = diagonal(wave)
    out_re, out_im = [], []
    for h in range(2):
        out_re.append(rights[0][h] + total[0][h] - (real * u[0][h] + imag * u[1][h]))
        out_im.append(rights[1][h] + total[1][h] - (real * u[1][h] - imag * u[0][h]))
    return [out_re, out_im]


def position():
    return lax.axis_index("grp"), lax.axis_index("sub")


def low_side_open(g):
    last = lax.axis_size("grp") - 1
    beyond = jnp.where(g % 2 == 0, g - 1, g + 1)
    return (beyond >= 0) & (beyond <= last)


def pack_body(field_ref, source_ref, patch_ref, index_ref, table_ref, out_ref):
    g, _ = position()
    odd = g % 2 == 1
    for q in range(SLOTS):
        patch = jnp.full((1, LANES), patch_ref[q].astype(F32), F32)
        wave = jnp.full((1, LANES), table_ref[index_ref[q]], F32)
        for s in range(NS):
            out_ref[s, 10 * q + 8 : 10 * q + 9, :] = patch
            out_ref[s, 10 * q + 9 : 10 * q + 10, :] = wave
    for s in range(NS):
        layer = jnp.where(odd, EDGE - 1 - s, s)
        for q in range(SLOTS):
            for a, ref in enumerate((field_ref, source_ref)):
                for part in range(2):
                    row = 10 * q + 4 * a + 2 * part
                    cells = ref[q, part, pl.ds(layer, 1), :]
                    out_ref[s, row : row + 1, :] = cells[:, :LANES]
                    out_ref[s, row + 1 : row + 2, :] = cells[:, LANES:]


def place_body(raw_ref, plane_ref, field_ref, slot_ref):
    patches = raw_ref[pl.ds(8, LIVE, stride=10), :]
    held = (patches == iota((LIVE, LANES), 1).astype(F32)).astype(F32)
    slot_ref[...] = held
    pick = held.T[:PATCHES]
    order = (0, 1, 2, 3, 4, 5, 6, 7, 9)
    rows = jnp.concatenate([raw_ref[pl.ds(c, LIVE, stride=10), :] for c in order], 1)
    placed = jnp.dot(pick, rows, precision=HI, preferred_element_type=F32)
    for c in range(4):
        put(plane_ref, c, [placed[:, 256 * c : 256 * c + 128], placed[:, 256 * c + 128 : 256 * c + 256]])
    for c in range(2):
        put(field_ref, c, [placed[:, 256 * c : 256 * c + 128], placed[:, 256 * c + 128 : 256 * c + 256]])
    put(plane_ref, 4, [placed[:, 1024:], placed[:, 1024:]])


def first_body(own_ref, before_ref, after_ref, far_ref, out_ref):
    _, s = position()
    u = field_of(own_ref, 0)
    v = field_of(far_ref, 0)
    before = choose(s == 0, v, field_of(before_ref, 0))
    after = choose(s == NS - 1, v, field_of(after_ref, 0))
    new = smooth(u, around(u, before, after), field_of(own_ref, 2), own_ref[4, :, :LANES])
    for part in range(2):
        put(out_ref, part, new[part])
        put(out_ref, 2 + part, v[part])


def open_factor():
    g, s = position()
    return jnp.where((s >= NS // 2) | low_side_open(g), 1.0, 0.0)


def second_body(own_ref, far_ref, before_ref, after_ref, mine_ref, slot_ref, out_ref, sent_ref):
    _, s = position()
    first, last = s == 0, s == NS - 1
    u = field_of(own_ref, 0)
    v = field_of(far_ref, 0)
    one = field_of(mine_ref, 0)
    v_before = choose(first, u, field_of(before_ref, 2))
    v_after = choose(last, u, field_of(after_ref, 2))
    v_one = smooth(v, around(v, v_before, v_after), field_of(far_ref, 2), far_ref[4, :, :LANES])
    factor = open_factor()
    v_one = [[x * factor for x in pair] for pair in v_one]
    before = choose(first, v_one, field_of(before_ref, 0))
    after = choose(last, v_one, field_of(after_ref, 0))
    two = smooth(one, around(one, before, after), field_of(own_ref, 2), own_ref[4, :, :LANES])
    for part in range(2):
        put(out_ref, part, two[part])
        put(out_ref, 2 + part, v_one[part])
    rows = jnp.concatenate(two[0] + two[1], 1)
    slots = jnp.dot(slot_ref[:, :PATCHES], rows, precision=HI, preferred_element_type=F32)
    for c in range(4):
        sent_ref[pl.ds(c, LIVE, stride=4), :] = slots[:, LANES * c : LANES * (c + 1)]


def coarse_lane(shape, dim):
    cell = iota(shape, dim)
    part, inside = cell // CELLS, cell % CELLS
    return part * 64 + (inside // (4 * EDGE)) * EDGE + (inside % EDGE) // 4


def restrict_body(own_ref, far_ref, before_ref, after_ref, two_ref, one_ref, out_ref):
    _, s = position()
    first, last = s == 0, s == NS - 1
    one = field_of(one_ref, 0)
    two = field_of(two_ref, 0)
    v_one = field_of(two_ref, 2)
    wave = own_ref[4, :, :LANES]
    v_before = choose(first, one, field_of(before_ref, 2))
    v_after = choose(last, one, field_of(after_ref, 2))
    v_two = smooth(v_one, around(v_one, v_before, v_after), field_of(far_ref, 2), far_ref[4, :, :LANES])
    factor = open_factor()
    v_two = [[x * factor for x in pair] for pair in v_two]
    before = choose(first, v_two, field_of(before_ref, 0))
    after = choose(last, v_two, field_of(after_ref, 0))
    r = residual(two, around(two, before, after), field_of(own_ref, 2), wave)
    rows = jnp.concatenate(r[0] + r[1], 1)
    shape = (2 * CELLS, LANES)
    gather = (coarse_lane(shape, 0) == iota(shape, 1)).astype(F32)
    sums = jnp.dot(rows, gather, precision=HI, preferred_element_type=F32)
    col = iota(sums.shape, 0) % PZ
    spread = jnp.where(col == 0, sums, 0.0)
    for c in range(1, PZ):
        spread = jnp.where(col == c, lane_roll(sums, 4 * c), spread)
    group = (iota((16, PATCHES), 1) // PZ == iota((16, PATCHES), 0)).astype(F32)
    block = jnp.dot(group, spread, precision=HI, preferred_element_type=F32)
    diag = jnp.where(iota(wave.shape, 0) == iota(wave.shape, 1), wave, 0.0)
    wave_row = jnp.sum(diag, 0, keepdims=True)
    out_ref[...] = jnp.where(iota(block.shape, 0) == PY, wave_row, block)


def bundle_body(sent_ref, block_ref, far_ref, out_ref):
    out_ref[:, 0:16, :] = sent_ref[...]
    for d in range(NS):
        out_ref[d, 16:32, :] = block_ref[...]
        out_ref[d, 32:48, :] = far_ref[...]


def coarse_sum(e):
    lane = iota(e.shape, 1)
    z = lane % EDGE
    j = (lane // EDGE) % 4
    z_next = jnp.where(z < EDGE - 1, lane_roll(e, -1), 0.0)
    z_prev = jnp.where(z > 0, lane_roll(e, 1), 0.0)
    y_next = jnp.where(j < 3, lane_roll(e, -EDGE), row_roll(lane_roll(e, 3 * EDGE), -1))
    y_prev = jnp.where(j > 0, lane_roll(e, EDGE), row_roll(lane_roll(e, -3 * EDGE), 1))
    return (z_next + z_prev) + (y_next + y_prev)


def correct_body(raw_ref, patch_ref, out_ref, coarse_ref, smooth_ref):
    g, _ = position()
    odd = g % 2 == 1
    shape = (16, LANES)
    row, lane = iota(shape, 0), iota(shape, 1)
    live = row < PY
    spread = (iota((LANES, LANES), 0) % PZ == (iota((LANES, LANES), 1) % EDGE) // 4).astype(F32)
    sign = jnp.where(lane < 64, -1.0, 1.0)

    def inverse(wave_row):
        own = jnp.where((lane // PZ == row) & live, jnp.broadcast_to(wave_row, shape), 0.0)
        wave = jnp.dot(own, spread, precision=HI, preferred_element_type=F32)
        real, imag = 6.0 / 16.0 - wave, shift_imag * wave
        scale = omega_coarse / (real * real + imag * imag)
        return jnp.where(live, real * scale, 0.0), jnp.where(live, sign * imag * scale, 0.0)

    def divide(x, inv):
        return x * inv[0] + lane_roll(x, 64) * inv[1]

    def total(start, tile):
        parts = [raw_ref[start + i, tile : tile + 16, :] for i in range(4)]
        return ((parts[0] + parts[1]) + (parts[2] + parts[3])) * (1.0 / 64.0)

    inv_own = inverse(raw_ref[0, 16 + PY : 17 + PY, :])
    inv_low = inverse(raw_ref[0, 32 + PY : 33 + PY, :])
    inv_high = inverse(raw_ref[NS - 1, 32 + PY : 33 + PY, :])
    inv = [inv_low, inv_low] + [inv_own] * 4 + [inv_high, inv_high]
    rhs = [total(4, 32), total(0, 32)] + [total(4 * i, 16) for i in range(4)] + [total(12, 32), total(8, 32)]
    e = [divide(x, i) for x, i in zip(rhs, inv)]
    low = jnp.where(low_side_open(g), 1.0, 0.0)
    for margin in (1, 2):
        new = list(e)
        for i in range(margin, 8 - margin):
            beside = coarse_sum(e[i]) + (e[i - 1] + e[i + 1])
            new[i] = (1.0 - omega_coarse) * e[i] + divide(rhs[i] + beside * (1.0 / 16.0), inv[i])
        new[1] = new[1] * low
        e = new
    for i in range(4):
        coarse_ref[i] = e[2 + i]
    grown = []
    for q in range(SLOTS):
        patch = jnp.maximum(patch_ref[q], 0)
        rows = []
        for i in range(4):
            plane = jnp.where(odd, 3 - i, i)
            one = coarse_ref[plane, pl.ds(patch // PZ, 1), :]
            rows.append(jnp.broadcast_to(one, (4, LANES)))
        grown.append(pltpu.roll(jnp.concatenate(rows, 0), LANES - 4 * (patch % PZ), 1))
    grown = jnp.concatenate(grown, 0)
    wide = (LANES, 2 * CELLS)
    widen = (coarse_lane(wide, 1) == iota(wide, 0)).astype(F32)
    grown = jnp.dot(grown, widen, precision=HI, preferred_element_type=F32)
    for i in range(EDGE):
        s = jnp.where(odd, EDGE - 1 - i, i)
        for q in range(SLOTS):
            for part in range(2):
                for h in range(2):
                    c = 4 * q + 2 * part + h
                    smooth_ref[2 * q + part, i : i + 1, LANES * h : LANES * (h + 1)] = raw_ref[s, c : c + 1, :]
    for q in range(SLOTS):
        held = patch_ref[q] >= 0
        for part in range(2):
            extra = grown[EDGE * q : EDGE * (q + 1), CELLS * part : CELLS * (part + 1)]
            out_ref[q, part] = jnp.where(held, smooth_ref[2 * q + part] + extra, 0.0)


def swap_pairs(groups, subs):
    pairs = []
    for s in subs:
        for g in range(0 if s >= NS // 2 else 1, groups - 1, 2):
            a, b = g * NS + s, (g + 1) * NS + s
            pairs += [(a, b), (b, a)]
    return pairs


def body(field, source, patch_of_slot, neighbour, wave_index, wave_table):
    groups = lax.axis_size("grp")
    both = ("grp", "sub")
    up = [(i, (i + 1) % NS) for i in range(NS)]
    down = [((i + 1) % NS, i) for i in range(NS)]
    ring = lambda x: (lax.ppermute(x, "sub", up), lax.ppermute(x, "sub", down))
    plane = (PATCHES, CELLS)

    (packed,) = call(pack_body, [(NS, 40, LANES)], [field, source, patch_of_slot, wave_index, wave_table])
    raw = lax.all_to_all(packed, "sub", 0, 0, tiled=True).reshape(NS * 40, LANES)
    own, start, slot = call(place_body, [(5,) + plane, (2,) + plane, (LIVE, LANES)], [raw])
    far = lax.ppermute(own, both, swap_pairs(groups, (0, 1, 2, 13, 14, 15)))
    before, after = ring(start)
    (one,) = call(first_body, [(4,) + plane], [own, before, after, far])
    before, after = ring(one)
    two, sent = call(
        second_body, [(4,) + plane, (4 * LIVE, LANES)], [own, far, before, after, one, slot]
    )
    before, after = ring(two)
    (block,) = call(restrict_body, [(16, LANES)], [own, far, before, after, two, one])
    far_block = lax.ppermute(block, both, swap_pairs(groups, range(NS)))
    (bundle,) = call(bundle_body, [(NS, 48, LANES)], [sent.reshape(NS, 16, LANES), block, far_block])
    back = lax.all_to_all(bundle, "sub", 0, 0, tiled=True)
    (out,) = call(
        correct_body,
        [(SLOTS, 2, EDGE, CELLS)],
        [back, patch_of_slot],
        [(4, 16, LANES), (2 * SLOTS, EDGE, CELLS)],
    )
    return out


def solution(mesh):
    return jax.shard_map(
        body,
        mesh=mesh,
        in_specs=(
            P(("grp", "sub"), None, None, None),
            P(("grp", "sub"), None, None, None),
            P(("grp", "sub")),
            P(("grp", "sub"), None),
            P(("grp", "sub")),
            P(),
        ),
        out_specs=P(("grp", "sub"), None, None, None),
        check_vma=False,
    )
```

profile of v0, /device:TPU:199, one launch (start us, length us, event | category | flops | bytes accessed | tf_op | source)
XLA Modules:
  0.0 93.7 jit_solution(12049948425116131642)
XLA Ops:
  0.0 1.9 %shard_map.55 = f32[16,40,128]{2,1,0:T(8,128)} custom-call(f32[4,2,16,256]{3,2,1,0:T(8,128)} %field_ref.1, f32[4,2,16,256]{3,2,1,0:T(8,128)} %source_ref.1, s32[4]{0:T(128)} %patch_ref.3, s32[4]{0:T(128)} %index_ref.1, f32[16]{0:T(128)} %table_ref.1), custom_call_target="tpu_custom_call" | custom-call | tf_op jit(solution)/shard_map/pallas_call | solution.py:29
  1.9 21.0 %all_to_all.10 = f32[16,40,128]{2,1,0:T(8,128)} all-to-all(f32[16,40,128]{2,1,0:T(8,128)} %shard_map.55), channel_id=1, replica_groups=mesh['grp'=32,'sub'=16] {'sub'}, dimensions={0} | all-to-all | bytes 655360 | tf_op jit(solution)/shard_map/all_to_all | solution.py:361
  22.9 2.1 %shard_map.56 = (f32[5,48,256]{2,1,0:T(8,128)}, f32[2,48,256]{2,1,0:T(8,128)}, f32[64,128]{1,0:T(8,128)}) custom-call(f32[640,128]{1,0:T(8,128)} %bitcast.2), custom_call_target="tpu_custom_call" | custom-call | tf_op jit(solution)/shard_map/pallas_call | solution.py:29
  25.0 5.1 %collective-permute-start = (f32[5,48,256]{2,1,0:T(8,128)}, f32[5,48,256]{2,1,0:T(8,128)S(1)}, u32[]{:S(2)}, u32[]{:S(2)}) collective-permute-start(f32[5,48,256]{2,1,0:T(8,128)} %get-tuple-element.10.own_ref), channel_id=1, source_target_pairs={{16,32},{32,16},{48,64},{64,48},{80,96},{96,80},{112,128},{128,112... | collective-permute-start | bytes 737288 | tf_op jit(solution)/shard_map/ppermute | solution.py:363
  30.1 1.7 %collective-permute-start.1 = (f32[2,48,256]{2,1,0:T(8,128)}, f32[2,48,256]{2,1,0:T(8,128)S(1)}, u32[]{:S(2)}, u32[]{:S(2)}) collective-permute-start(f32[2,48,256]{2,1,0:T(8,128)} %get-tuple-element.11), channel_id=1, source_target_pairs={{0,1},{1,2},{2,3},{3,4},{4,5},{5,6},{6,7},{7,8},{8,9},{9,10},{10,1... | collective-permute-start | bytes 294920 | tf_op jit(solution)/shard_map/ppermute | solution.py:357
  31.8 2.8 %collective-permute-done.2.after_ref = f32[2,48,256]{2,1,0:T(8,128)S(1)} collective-permute-done((f32[2,48,256]{2,1,0:T(8,128)}, f32[2,48,256]{2,1,0:T(8,128)S(1)}, u32[]{:S(2)}, u32[]{:S(2)}) %collective-permute-start.2) | collective-permute-done | bytes 98336 | tf_op jit(solution)/shard_map/ppermute | solution.py:357
  34.6 3.5 %collective-permute-done.far_ref = f32[5,48,256]{2,1,0:T(8,128)S(1)} collective-permute-done((f32[5,48,256]{2,1,0:T(8,128)}, f32[5,48,256]{2,1,0:T(8,128)S(1)}, u32[]{:S(2)}, u32[]{:S(2)}) %collective-permute-start) | collective-permute-done | bytes 245792 | tf_op jit(solution)/shard_map/ppermute | solution.py:363
  38.1 0.7 copy-done
  38.8 2.1 %shard_map.57.mine_ref.one_ref = f32[4,48,256]{2,1,0:T(8,128)} custom-call(f32[5,48,256]{2,1,0:T(8,128)} %get-tuple-element.10.own_ref, f32[2,48,256]{2,1,0:T(8,128)} %copy-done.6, f32[2,48,256]{2,1,0:T(8,128)} %copy-done.5, f32[5,48,256]{2,1,0:T(8,128)} %copy-done), custom_call_target="tpu_custom_call" | custom-call | tf_op jit(solution)/shard_map/pallas_call | solution.py:29
  41.3 1.4 %collective-permute-start.3 = (f32[4,48,256]{2,1,0:T(8,128)}, f32[4,48,256]{2,1,0:T(8,128)S(1)}, u32[]{:S(2)}, u32[]{:S(2)}) collective-permute-start(f32[4,48,256]{2,1,0:T(8,128)} %shard_map.57.mine_ref.one_ref), channel_id=1, source_target_pairs={{0,1},{1,2},{2,3},{3,4},{4,5},{5,6},{6,7},{7,8},{8,9},{9,10},{10,1... | collective-permute-start | bytes 589832 | tf_op jit(solution)/shard_map/ppermute | solution.py:357
  42.6 3.9 %collective-permute-done.4.after_ref = f32[4,48,256]{2,1,0:T(8,128)S(1)} collective-permute-done((f32[4,48,256]{2,1,0:T(8,128)}, f32[4,48,256]{2,1,0:T(8,128)S(1)}, u32[]{:S(2)}, u32[]{:S(2)}) %collective-permute-start.4) | collective-permute-done | bytes 196640 | tf_op jit(solution)/shard_map/ppermute | solution.py:357
  46.5 0.7 copy-done.3
  47.2 2.6 %shard_map.58 = (f32[4,48,256]{2,1,0:T(8,128)}, f32[256,128]{1,0:T(8,128)}) custom-call(f32[5,48,256]{2,1,0:T(8,128)} %get-tuple-element.10.own_ref, f32[5,48,256]{2,1,0:T(8,128)} %copy-done, f32[4,48,256]{2,1,0:T(8,128)} %copy-done.4, f32[4,48,256]{2,1,0:T(8,128)} %copy-done.3, f32[4,48,256]{2,1,0:T(8,128)} %shard_map.57.mine_ref.one_ref, ...), custom_call_target="tpu_custom_call" | custom-call | tf_op jit(solution)/shard_map/pallas_call | solution.py:29
  49.9 1.2 %collective-permute-start.6 = (f32[4,48,256]{2,1,0:T(8,128)}, f32[4,48,256]{2,1,0:T(8,128)S(1)}, u32[]{:S(2)}, u32[]{:S(2)}) collective-permute-start(f32[4,48,256]{2,1,0:T(8,128)} %get-tuple-element.14.two_ref), channel_id=1, source_target_pairs={{1,0},{2,1},{3,2},{4,3},{5,4},{6,5},{7,6},{8,7},{9,8},{10,9},{11,1... | collective-permute-start | bytes 589832 | tf_op jit(solution)/shard_map/ppermute | solution.py:357
  51.6 3.9 %collective-permute-done.6.after_ref = f32[4,48,256]{2,1,0:T(8,128)S(1)} collective-permute-done((f32[4,48,256]{2,1,0:T(8,128)}, f32[4,48,256]{2,1,0:T(8,128)S(1)}, u32[]{:S(2)}, u32[]{:S(2)}) %collective-permute-start.6) | collective-permute-done | bytes 196640 | tf_op jit(solution)/shard_map/ppermute | solution.py:357
  55.5 0.7 copy-done.1
  56.2 0.7 copy-done.2
  56.8 2.9 %shard_map.59.block_ref = f32[16,128]{1,0:T(8,128)} custom-call(f32[5,48,256]{2,1,0:T(8,128)} %get-tuple-element.10.own_ref, f32[5,48,256]{2,1,0:T(8,128)} %copy-done, f32[4,48,256]{2,1,0:T(8,128)} %copy-done.2, f32[4,48,256]{2,1,0:T(8,128)} %copy-done.1, f32[4,48,256]{2,1,0:T(8,128)} %get-tuple-element.14.two_ref, f32[4,48,256]{2,1,0:T(8,128)} %shard_map.57.mine_ref.one_ref), custom_call_target="tpu_custom_call" | custom-call | tf_op jit(solution)/shard_map/pallas_call | solution.py:29
  59.7 5.1 %collective-permute-start.7 = (f32[16,128]{1,0:T(8,128)}, f32[16,128]{1,0:T(8,128)S(1)}, u32[]{:S(2)}, u32[]{:S(2)}) collective-permute-start(f32[16,128]{1,0:T(8,128)} %shard_map.59.block_ref), channel_id=1, source_target_pairs={{16,32},{32,16},{48,64},{64,48},{80,96},{96,80},{112,128},{128,112... | collective-permute-start | bytes 24584 | tf_op jit(solution)/shard_map/ppermute | solution.py:372
  64.8 2.8 %collective-permute-done.7.far_ref = f32[16,128]{1,0:T(8,128)S(1)} collective-permute-done((f32[16,128]{1,0:T(8,128)}, f32[16,128]{1,0:T(8,128)S(1)}, u32[]{:S(2)}, u32[]{:S(2)}) %collective-permute-start.7) | collective-permute-done | bytes 8224 | tf_op jit(solution)/shard_map/ppermute | solution.py:372
  67.6 0.6 copy-done.7
  68.2 1.7 %shard_map.60 = f32[16,48,128]{2,1,0:T(8,128)} custom-call(f32[16,16,128]{2,1,0:T(8,128)} %bitcast.3, f32[16,128]{1,0:T(8,128)} %shard_map.59.block_ref, f32[16,128]{1,0:T(8,128)} %copy-done.7), custom_call_target="tpu_custom_call" | custom-call | tf_op jit(solution)/shard_map/pallas_call | solution.py:29
  69.9 21.3 %all_to_all.11.raw_ref = f32[16,48,128]{2,1,0:T(8,128)} all-to-all(f32[16,48,128]{2,1,0:T(8,128)} %shard_map.60), channel_id=1, replica_groups=mesh['grp'=32,'sub'=16] {'sub'}, dimensions={0} | all-to-all | bytes 786432 | tf_op jit(solution)/shard_map/all_to_all | solution.py:374
  91.2 2.6 %shard_map.61 = f32[4,2,16,256]{3,2,1,0:T(8,128)} custom-call(f32[16,48,128]{2,1,0:T(8,128)} %all_to_all.11.raw_ref, s32[4]{0:T(128)} %patch_ref.3), custom_call_target="tpu_custom_call" | custom-call | tf_op jit(solution)/shard_map/pallas_call | solution.py:29
  (17 shorter events, 1.0 us)
Async XLA Ops:
  25.0 13.2 %collective-permute-start = (f32[5,48,256]{2,1,0:T(8,128)}, f32[5,48,256]{2,1,0:T(8,128)S(1)}, u32[]{:S(2)}, u32[]{:S(2)}) collective-permute-start(f32[5,48,256]{2,1,0:T(8,128)} %get-tuple-element.10.own_ref), channel_id=1, source_target_pairs={{16,32},{32,16},{48,64},{64,48},{80,96},{96,80},{112,128},{128,112... | collective-permute-start | bytes 737288 | tf_op jit(solution)/shard_map/ppermute | solution.py:363
  30.1 4.6 %collective-permute-start.2 = (f32[2,48,256]{2,1,0:T(8,128)}, f32[2,48,256]{2,1,0:T(8,128)S(1)}, u32[]{:S(2)}, u32[]{:S(2)}) collective-permute-start(f32[2,48,256]{2,1,0:T(8,128)} %get-tuple-element.11), channel_id=1, source_target_pairs={{1,0},{2,1},{3,2},{4,3},{5,4},{6,5},{7,6},{8,7},{9,8},{10,9},{11,1... | collective-permute-start | bytes 294920 | tf_op jit(solution)/shard_map/ppermute | solution.py:357
  30.1 4.5 %collective-permute-start.1 = (f32[2,48,256]{2,1,0:T(8,128)}, f32[2,48,256]{2,1,0:T(8,128)S(1)}, u32[]{:S(2)}, u32[]{:S(2)}) collective-permute-start(f32[2,48,256]{2,1,0:T(8,128)} %get-tuple-element.11), channel_id=1, source_target_pairs={{0,1},{1,2},{2,3},{3,4},{4,5},{5,6},{6,7},{7,8},{8,9},{9,10},{10,1... | collective-permute-start | bytes 294920 | tf_op jit(solution)/shard_map/ppermute | solution.py:357
  34.6 3.5 %copy-start.5 = (f32[2,48,256]{2,1,0:T(8,128)}, f32[2,48,256]{2,1,0:T(8,128)S(1)}, u32[]{:S(2)}) copy-start(f32[2,48,256]{2,1,0:T(8,128)S(1)} %collective-permute-done.2.after_ref) | copy-start | bytes 294916
  34.6 3.5 %copy-start.6 = (f32[2,48,256]{2,1,0:T(8,128)}, f32[2,48,256]{2,1,0:T(8,128)S(1)}, u32[]{:S(2)}) copy-start(f32[2,48,256]{2,1,0:T(8,128)S(1)} %collective-permute-done.1.before_ref) | copy-start | bytes 294916
  38.1 0.7 copy-start
  40.9 5.6 %collective-permute-start.4 = (f32[4,48,256]{2,1,0:T(8,128)}, f32[4,48,256]{2,1,0:T(8,128)S(1)}, u32[]{:S(2)}, u32[]{:S(2)}) collective-permute-start(f32[4,48,256]{2,1,0:T(8,128)} %shard_map.57.mine_ref.one_ref), channel_id=1, source_target_pairs={{1,0},{2,1},{3,2},{4,3},{5,4},{6,5},{7,6},{8,7},{9,8},{10,9},{11,1... | collective-permute-start | bytes 589832 | tf_op jit(solution)/shard_map/ppermute | solution.py:357
  41.3 5.2 %collective-permute-start.3 = (f32[4,48,256]{2,1,0:T(8,128)}, f32[4,48,256]{2,1,0:T(8,128)S(1)}, u32[]{:S(2)}, u32[]{:S(2)}) collective-permute-start(f32[4,48,256]{2,1,0:T(8,128)} %shard_map.57.mine_ref.one_ref), channel_id=1, source_target_pairs={{0,1},{1,2},{2,3},{3,4},{4,5},{5,6},{6,7},{7,8},{8,9},{9,10},{10,1... | collective-permute-start | bytes 589832 | tf_op jit(solution)/shard_map/ppermute | solution.py:357
  46.5 0.7 copy-start.3
  46.5 0.8 copy-start.4
  49.9 5.6 %collective-permute-start.6 = (f32[4,48,256]{2,1,0:T(8,128)}, f32[4,48,256]{2,1,0:T(8,128)S(1)}, u32[]{:S(2)}, u32[]{:S(2)}) collective-permute-start(f32[4,48,256]{2,1,0:T(8,128)} %get-tuple-element.14.two_ref), channel_id=1, source_target_pairs={{1,0},{2,1},{3,2},{4,3},{5,4},{6,5},{7,6},{8,7},{9,8},{10,9},{11,1... | collective-permute-start | bytes 589832 | tf_op jit(solution)/shard_map/ppermute | solution.py:357
  51.1 4.4 %collective-permute-start.5 = (f32[4,48,256]{2,1,0:T(8,128)}, f32[4,48,256]{2,1,0:T(8,128)S(1)}, u32[]{:S(2)}, u32[]{:S(2)}) collective-permute-start(f32[4,48,256]{2,1,0:T(8,128)} %get-tuple-element.14.two_ref), channel_id=1, source_target_pairs={{0,1},{1,2},{2,3},{3,4},{4,5},{5,6},{6,7},{7,8},{8,9},{9,10},{10,1... | collective-permute-start | bytes 589832 | tf_op jit(solution)/shard_map/ppermute | solution.py:357
  55.5 0.7 copy-start.1
  56.2 0.7 copy-start.2
  59.7 7.9 %collective-permute-start.7 = (f32[16,128]{1,0:T(8,128)}, f32[16,128]{1,0:T(8,128)S(1)}, u32[]{:S(2)}, u32[]{:S(2)}) collective-permute-start(f32[16,128]{1,0:T(8,128)} %shard_map.59.block_ref), channel_id=1, source_target_pairs={{16,32},{32,16},{48,64},{64,48},{80,96},{96,80},{112,128},{128,112... | collective-permute-start | bytes 24584 | tf_op jit(solution)/shard_map/ppermute | solution.py:372
  67.6 0.6 copy-start.7
where the time goes:
time: 94.2 us; the launch traced here: 93.7 us
  blocking collectives  42.2 us (45%)
  waiting for transfers between devices  16.8 us (18%)
  Pallas kernels  15.8 us (17%)
  starting transfers between devices  15.5 us (16%)
  local copies, waits for them, and re-layouts  3.42 us (4%)
    all_to_all x1, blocking collectives, body(): back = lax.all_to_all(bundle, 'sub', 0, 0, tiled=True)  21.3 us
    all_to_all x1, blocking collectives, body(): lax.all_to_all(packed, 'sub', 0, 0, tiled=True).reshape(NS * 40, LANES)  21 us
    pallas_call x7, Pallas kernels, call(): pl.pallas_call(body, out_shape=[jax.ShapeDtypeStruct(shape, F32) for shap...  15.8 us
    ppermute x6, waiting for transfers between devices, body(): ring = lambda x: (lax.ppermute(x, 'sub', up), lax.ppermute(x, 'sub', down))  10.5 us
    ppermute x6, starting transfers between devices, body(): ring = lambda x: (lax.ppermute(x, 'sub', up), lax.ppermute(x, 'sub', down))  5.24 us
    ppermute x1, starting transfers between devices, body(): far = lax.ppermute(own, both, swap_pairs(groups, (0, 1, 2, 13, 14, 15)))  5.11 us
    ppermute x1, starting transfers between devices, body(): far_block = lax.ppermute(block, both, swap_pairs(groups, range(NS)))  5.11 us
    ppermute x1, waiting for transfers between devices, body(): far = lax.ppermute(own, both, swap_pairs(groups, (0, 1, 2, 13, 14, 15)))  3.47 us
  transfers between devices with their start and end apart: 8, of which 5 were waited for; matrix products, arithmetic and copies ran while one was open for 0% of the time, Pallas kernels for 0%

commit v1 on v0

--- a/solution.py
+++ b/solution.py
@@ -32,6 +32,7 @@
         in_specs=[SM if a.dtype == jnp.int32 or a.ndim == 1 else VM for a in ins],
         out_specs=[VM] * len(outs),
         scratch_shapes=[pltpu.VMEM(shape, F32) for shape in scratch],
+        compiler_params=pltpu.CompilerParams(vmem_limit_bytes=16 << 20),
     )(*ins)
 
 

time: 94.2 us -> 81.7 us (0.87)
  Pallas kernels: 15.8 us -> 5.05 us
  blocking collectives: 42.2 us -> 41 us
    pallas_call x7, Pallas kernels: 15.8 us -> 5.05 us  [call(): pl.pallas_call(body, out_shape=[jax.ShapeDtypeStruct(shape, F32) for shap...]
    unnamed x16 -> x12, local copies, waits for them, and re-layouts: 3.42 us -> 3.78 us
where the time goes in v1:
time: 81.7 us; the launch traced here: 81.4 us
  blocking collectives  41 us (50%)
  waiting for transfers between devices  15.9 us (19%)
  starting transfers between devices  15.5 us (19%)
  Pallas kernels  5.05 us (6%)
  local copies, waits for them, and re-layouts  3.78 us (5%)
    all_to_all x1, blocking collectives, body(): lax.all_to_all(packed, 'sub', 0, 0, tiled=True).reshape(NS * 40, LANES)  20.6 us
    all_to_all x1, blocking collectives, body(): back = lax.all_to_all(bundle, 'sub', 0, 0, tiled=True)  20.4 us
    ppermute x6, waiting for transfers between devices, body(): ring = lambda x: (lax.ppermute(x, 'sub', up), lax.ppermute(x, 'sub', down))  9.88 us
    ppermute x6, starting transfers between devices, body(): ring = lambda x: (lax.ppermute(x, 'sub', up), lax.ppermute(x, 'sub', down))  5.27 us
    ppermute x1, starting transfers between devices, body(): far_block = lax.ppermute(block, both, swap_pairs(groups, range(NS)))  5.13 us
    ppermute x1, starting transfers between devices, body(): far = lax.ppermute(own, both, swap_pairs(groups, (0, 1, 2, 13, 14, 15)))  5.12 us
    pallas_call x7, Pallas kernels, call(): pl.pallas_call(body, out_shape=[jax.ShapeDtypeStruct(shape, F32) for shap...  5.05 us
    unnamed x12, local copies, waits for them, and re-layouts  3.78 us
  transfers between devices with their start and end apart: 8, of which 5 were waited for; matrix products, arithmetic and copies ran while one was open for 0% of the time, Pallas kernels for 0%

profile of v1, /device:TPU:199, one launch (start us, length us, event | category | flops | bytes accessed | tf_op | source)
XLA Modules:
  0.0 81.4 jit_solution(7387078420682475420)
XLA Ops:
  0.0 0.9 %copy-done = f32[4,2,16,256]{3,2,1,0:T(8,128)S(1)} copy-done((f32[4,2,16,256]{3,2,1,0:T(8,128)S(1)}, f32[4,2,16,256]{3,2,1,0:T(8,128)}, u32[]{:S(2)}) %copy-start) | copy-done | bytes 131096
  0.9 0.9 %copy-done.1 = f32[4,2,16,256]{3,2,1,0:T(8,128)S(1)} copy-done((f32[4,2,16,256]{3,2,1,0:T(8,128)S(1)}, f32[4,2,16,256]{3,2,1,0:T(8,128)}, u32[]{:S(2)}) %copy-start.1) | copy-done | bytes 131096
  1.8 0.7 copy-done.2
  2.5 0.7 copy-done.4
  3.1 0.7 copy-done.5
  3.8 0.8 shard_map.55
  4.6 20.6 %all_to_all.10 = f32[16,40,128]{2,1,0:T(8,128)S(1)} all-to-all(f32[16,40,128]{2,1,0:T(8,128)S(1)} %shard_map.55), channel_id=1, replica_groups=mesh['grp'=32,'sub'=16] {'sub'}, dimensions={0} | all-to-all | bytes 655360 | tf_op jit(solution)/shard_map/all_to_all | solution.py:362
  25.2 0.4 shard_map.56
  25.6 5.1 %collective-permute-start = (f32[5,48,256]{2,1,0:T(8,128)S(1)}, f32[5,48,256]{2,1,0:T(8,128)S(1)}, u32[]{:S(2)}, u32[]{:S(2)}) collective-permute-start(f32[5,48,256]{2,1,0:T(8,128)S(1)} %get-tuple-element.10.own_ref), channel_id=1, source_target_pairs={{16,32},{32,16},{48,64},{64,48},{80,96},{96,80},{112,128},{128,112... | collective-permute-start | bytes 737288 | tf_op jit(solution)/shard_map/ppermute | solution.py:364
  30.8 1.7 %collective-permute-start.1 = (f32[2,48,256]{2,1,0:T(8,128)S(1)}, f32[2,48,256]{2,1,0:T(8,128)S(1)}, u32[]{:S(2)}, u32[]{:S(2)}) collective-permute-start(f32[2,48,256]{2,1,0:T(8,128)S(1)} %get-tuple-element.11), channel_id=1, source_target_pairs={{0,1},{1,2},{2,3},{3,4},{4,5},{5,6},{6,7},{7,8},{8,9},{9,10},{10,1... | collective-permute-start | bytes 294920 | tf_op jit(solution)/shard_map/ppermute | solution.py:358
  32.5 2.6 %collective-permute-done.2.after_ref = f32[2,48,256]{2,1,0:T(8,128)S(1)} collective-permute-done((f32[2,48,256]{2,1,0:T(8,128)S(1)}, f32[2,48,256]{2,1,0:T(8,128)S(1)}, u32[]{:S(2)}, u32[]{:S(2)}) %collective-permute-start.2) | collective-permute-done | bytes 98336 | tf_op jit(solution)/shard_map/ppermute | solution.py:358
  35.1 3.5 %collective-permute-done.far_ref = f32[5,48,256]{2,1,0:T(8,128)S(1)} collective-permute-done((f32[5,48,256]{2,1,0:T(8,128)S(1)}, f32[5,48,256]{2,1,0:T(8,128)S(1)}, u32[]{:S(2)}, u32[]{:S(2)}) %collective-permute-start) | collective-permute-done | bytes 245792 | tf_op jit(solution)/shard_map/ppermute | solution.py:364
  38.8 0.4 collective-permute-start.4
  39.2 1.4 %collective-permute-start.3 = (f32[4,48,256]{2,1,0:T(8,128)S(1)}, f32[4,48,256]{2,1,0:T(8,128)S(1)}, u32[]{:S(2)}, u32[]{:S(2)}) collective-permute-start(f32[4,48,256]{2,1,0:T(8,128)S(1)} %shard_map.57.mine_ref.one_ref), channel_id=1, source_target_pairs={{0,1},{1,2},{2,3},{3,4},{4,5},{5,6},{6,7},{7,8},{8,9},{9,10},{10,1... | collective-permute-start | bytes 589832 | tf_op jit(solution)/shard_map/ppermute | solution.py:358
  40.6 3.6 %collective-permute-done.4.after_ref = f32[4,48,256]{2,1,0:T(8,128)S(1)} collective-permute-done((f32[4,48,256]{2,1,0:T(8,128)S(1)}, f32[4,48,256]{2,1,0:T(8,128)S(1)}, u32[]{:S(2)}, u32[]{:S(2)}) %collective-permute-start.4) | collective-permute-done | bytes 196640 | tf_op jit(solution)/shard_map/ppermute | solution.py:358
  44.2 0.6 shard_map.58
  44.9 1.3 %collective-permute-start.6 = (f32[4,48,256]{2,1,0:T(8,128)S(1)}, f32[4,48,256]{2,1,0:T(8,128)S(1)}, u32[]{:S(2)}, u32[]{:S(2)}) collective-permute-start(f32[4,48,256]{2,1,0:T(8,128)S(1)} %get-tuple-element.14.two_ref), channel_id=1, source_target_pairs={{1,0},{2,1},{3,2},{4,3},{5,4},{6,5},{7,6},{8,7},{9,8},{10,9},{11,1... | collective-permute-start | bytes 589832 | tf_op jit(solution)/shard_map/ppermute | solution.py:358
  46.2 0.4 collective-permute-start.5
  46.6 3.6 %collective-permute-done.6.after_ref = f32[4,48,256]{2,1,0:T(8,128)S(1)} collective-permute-done((f32[4,48,256]{2,1,0:T(8,128)S(1)}, f32[4,48,256]{2,1,0:T(8,128)S(1)}, u32[]{:S(2)}, u32[]{:S(2)}) %collective-permute-start.6) | collective-permute-done | bytes 196640 | tf_op jit(solution)/shard_map/ppermute | solution.py:358
  50.3 0.9 %shard_map.59.block_ref = f32[16,128]{1,0:T(8,128)S(1)} custom-call(f32[5,48,256]{2,1,0:T(8,128)S(1)} %get-tuple-element.10.own_ref, f32[5,48,256]{2,1,0:T(8,128)S(1)} %collective-permute-done.far_ref, f32[4,48,256]{2,1,0:T(8,128)S(1)} %collective-permute-done.5.before_ref, f32[4,48,256]{2,1,0:T(8,128)S(1)} %collective-permute-done.6.after_ref, ...), custom_call_target="tpu_custom_call" | custom-call | tf_op jit(solution)/shard_map/pallas_call | solution.py:29
  51.2 5.1 %collective-permute-start.7 = (f32[16,128]{1,0:T(8,128)S(1)}, f32[16,128]{1,0:T(8,128)S(1)}, u32[]{:S(2)}, u32[]{:S(2)}) collective-permute-start(f32[16,128]{1,0:T(8,128)S(1)} %shard_map.59.block_ref), channel_id=1, source_target_pairs={{16,32},{32,16},{48,64},{64,48},{80,96},{96,80},{112,128},{128,112... | collective-permute-start | bytes 24584 | tf_op jit(solution)/shard_map/ppermute | solution.py:373
  56.3 2.6 %collective-permute-done.7.far_ref = f32[16,128]{1,0:T(8,128)S(1)} collective-permute-done((f32[16,128]{1,0:T(8,128)S(1)}, f32[16,128]{1,0:T(8,128)S(1)}, u32[]{:S(2)}, u32[]{:S(2)}) %collective-permute-start.7) | collective-permute-done | bytes 8224 | tf_op jit(solution)/shard_map/ppermute | solution.py:373
  58.9 20.4 %all_to_all.11.raw_ref = f32[16,48,128]{2,1,0:T(8,128)S(1)} all-to-all(f32[16,48,128]{2,1,0:T(8,128)S(1)} %shard_map.60), channel_id=1, replica_groups=mesh['grp'=32,'sub'=16] {'sub'}, dimensions={0} | all-to-all | bytes 786432 | tf_op jit(solution)/shard_map/all_to_all | solution.py:375
  79.3 2.1 %shard_map.61 = f32[4,2,16,256]{3,2,1,0:T(8,128)} custom-call(f32[16,48,128]{2,1,0:T(8,128)S(1)} %all_to_all.11.raw_ref, s32[4]{0:T(128)S(1)} %copy-done.3), custom_call_target="tpu_custom_call" | custom-call | tf_op jit(solution)/shard_map/pallas_call | solution.py:29
  (13 shorter events, 0.3 us)
Async XLA Ops:
  0.0 0.9 %copy-start = (f32[4,2,16,256]{3,2,1,0:T(8,128)S(1)}, f32[4,2,16,256]{3,2,1,0:T(8,128)}, u32[]{:S(2)}) copy-start(f32[4,2,16,256]{3,2,1,0:T(8,128)} %field_ref.1) | copy-start | bytes 393220
  0.9 0.9 %copy-start.1 = (f32[4,2,16,256]{3,2,1,0:T(8,128)S(1)}, f32[4,2,16,256]{3,2,1,0:T(8,128)}, u32[]{:S(2)}) copy-start(f32[4,2,16,256]{3,2,1,0:T(8,128)} %source_ref.1) | copy-start | bytes 393220
  1.8 0.7 copy-start.2
  2.5 0.7 copy-start.4
  3.1 0.7 copy-start.5
  25.6 13.0 %collective-permute-start = (f32[5,48,256]{2,1,0:T(8,128)S(1)}, f32[5,48,256]{2,1,0:T(8,128)S(1)}, u32[]{:S(2)}, u32[]{:S(2)}) collective-permute-start(f32[5,48,256]{2,1,0:T(8,128)S(1)} %get-tuple-element.10.own_ref), channel_id=1, source_target_pairs={{16,32},{32,16},{48,64},{64,48},{80,96},{96,80},{112,128},{128,112... | collective-permute-start | bytes 737288 | tf_op jit(solution)/shard_map/ppermute | solution.py:364
  30.8 4.3 %collective-permute-start.2 = (f32[2,48,256]{2,1,0:T(8,128)S(1)}, f32[2,48,256]{2,1,0:T(8,128)S(1)}, u32[]{:S(2)}, u32[]{:S(2)}) collective-permute-start(f32[2,48,256]{2,1,0:T(8,128)S(1)} %get-tuple-element.11), channel_id=1, source_target_pairs={{1,0},{2,1},{3,2},{4,3},{5,4},{6,5},{7,6},{8,7},{9,8},{10,9},{11,1... | collective-permute-start | bytes 294920 | tf_op jit(solution)/shard_map/ppermute | solution.py:358
  30.8 4.3 %collective-permute-start.1 = (f32[2,48,256]{2,1,0:T(8,128)S(1)}, f32[2,48,256]{2,1,0:T(8,128)S(1)}, u32[]{:S(2)}, u32[]{:S(2)}) collective-permute-start(f32[2,48,256]{2,1,0:T(8,128)S(1)} %get-tuple-element.11), channel_id=1, source_target_pairs={{0,1},{1,2},{2,3},{3,4},{4,5},{5,6},{6,7},{7,8},{8,9},{9,10},{10,1... | collective-permute-start | bytes 294920 | tf_op jit(solution)/shard_map/ppermute | solution.py:358
  38.8 5.4 %collective-permute-start.4 = (f32[4,48,256]{2,1,0:T(8,128)S(1)}, f32[4,48,256]{2,1,0:T(8,128)S(1)}, u32[]{:S(2)}, u32[]{:S(2)}) collective-permute-start(f32[4,48,256]{2,1,0:T(8,128)S(1)} %shard_map.57.mine_ref.one_ref), channel_id=1, source_target_pairs={{1,0},{2,1},{3,2},{4,3},{5,4},{6,5},{7,6},{8,7},{9,8},{10,9},{11,1... | collective-permute-start | bytes 589832 | tf_op jit(solution)/shard_map/ppermute | solution.py:358
  39.2 5.0 %collective-permute-start.3 = (f32[4,48,256]{2,1,0:T(8,128)S(1)}, f32[4,48,256]{2,1,0:T(8,128)S(1)}, u32[]{:S(2)}, u32[]{:S(2)}) collective-permute-start(f32[4,48,256]{2,1,0:T(8,128)S(1)} %shard_map.57.mine_ref.one_ref), channel_id=1, source_target_pairs={{0,1},{1,2},{2,3},{3,4},{4,5},{5,6},{6,7},{7,8},{8,9},{9,10},{10,1... | collective-permute-start | bytes 589832 | tf_op jit(solution)/shard_map/ppermute | solution.py:358
  44.9 5.4 %collective-permute-start.6 = (f32[4,48,256]{2,1,0:T(8,128)S(1)}, f32[4,48,256]{2,1,0:T(8,128)S(1)}, u32[]{:S(2)}, u32[]{:S(2)}) collective-permute-start(f32[4,48,256]{2,1,0:T(8,128)S(1)} %get-tuple-element.14.two_ref), channel_id=1, source_target_pairs={{1,0},{2,1},{3,2},{4,3},{5,4},{6,5},{7,6},{8,7},{9,8},{10,9},{11,1... | collective-permute-start | bytes 589832 | tf_op jit(solution)/shard_map/ppermute | solution.py:358
  46.2 4.1 %collective-permute-start.5 = (f32[4,48,256]{2,1,0:T(8,128)S(1)}, f32[4,48,256]{2,1,0:T(8,128)S(1)}, u32[]{:S(2)}, u32[]{:S(2)}) collective-permute-start(f32[4,48,256]{2,1,0:T(8,128)S(1)} %get-tuple-element.14.two_ref), channel_id=1, source_target_pairs={{0,1},{1,2},{2,3},{3,4},{4,5},{5,6},{6,7},{7,8},{8,9},{9,10},{10,1... | collective-permute-start | bytes 589832 | tf_op jit(solution)/shard_map/ppermute | solution.py:358
  51.2 7.7 %collective-permute-start.7 = (f32[16,128]{1,0:T(8,128)S(1)}, f32[16,128]{1,0:T(8,128)S(1)}, u32[]{:S(2)}, u32[]{:S(2)}) collective-permute-start(f32[16,128]{1,0:T(8,128)S(1)} %shard_map.59.block_ref), channel_id=1, source_target_pairs={{16,32},{32,16},{48,64},{64,48},{80,96},{96,80},{112,128},{128,112... | collective-permute-start | bytes 24584 | tf_op jit(solution)/shard_map/ppermute | solution.py:373
  58.9 20.4 %copy-start.3 = (s32[4]{0:T(128)S(1)}, s32[4]{0:T(128)}, u32[]{:S(2)}) copy-start(s32[4]{0:T(128)} %patch_ref.3) | copy-start | bytes 52

commit v2 on v0

v2 whole, which is shorter than its diff:
```python
import jax
import jax.numpy as jnp
from jax import lax
from jax.experimental import pallas as pl
from jax.experimental.pallas import tpu as pltpu
from jax.sharding import PartitionSpec as P

PZ = 4
PY = 12
PATCHES = PY * PZ
EDGE = 16
CELLS = EDGE * EDGE
SLOTS = 4
NS = 16
LIVE = NS * SLOTS
LANES = 128

omega_fine = 0.7
omega_coarse = 0.6
shift_imag = 0.5

F32 = jnp.float32
VM = pl.BlockSpec(memory_space=pltpu.VMEM)
SM = pl.BlockSpec(memory_space=pltpu.SMEM)


def call(body, outs, ins, scratch=(), specs=None, limit=16):
    return pl.pallas_call(
        body,
        out_shape=[jax.ShapeDtypeStruct(shape, F32) for shape in outs],
        in_specs=specs or [SM if a.dtype == jnp.int32 else VM for a in ins],
        out_specs=[VM] * len(outs),
        scratch_shapes=[pltpu.VMEM(s, F32) if isinstance(s, tuple) else s for s in scratch],
        compiler_params=pltpu.CompilerParams(vmem_limit_bytes=limit << 20),
    )(*ins)


def select(picks, x):
    picks = picks.astype(jnp.bfloat16)
    out = None
    for _ in range(3):
        piece = x.astype(jnp.bfloat16)
        x = x - piece.astype(F32)
        term = jnp.dot(picks, piece, preferred_element_type=F32)
        out = term if out is None else out + term
    return out


def select_lanes(x, picks):
    picks = picks.astype(jnp.bfloat16)
    out = None
    for _ in range(3):
        piece = x.astype(jnp.bfloat16)
        x = x - piece.astype(F32)
        term = jnp.dot(piece, picks, preferred_element_type=F32)
        out = term if out is None else out + term
    return out


def iota(shape, dim):
    return lax.broadcasted_iota(jnp.int32, shape, dim)


def lane_roll(x, shift):
    return pltpu.roll(x, shift % x.shape[1], 1)


def row_roll(x, shift):
    return pltpu.roll(x, shift % x.shape[0], 0)


def in_plane(u):
    shape = u[0].shape
    lane = iota(shape, 1)
    patch = iota(shape, 0)
    k = lane % EDGE
    col = patch % PZ
    not_last, not_first = k < EDGE - 1, k > 0
    has_next, has_prev = col < PZ - 1, col > 0
    out = []
    ahead = [lane_roll(t, -EDGE) for t in u]
    behind = [lane_roll(t, EDGE) for t in u]
    low, high = lane >= EDGE, lane < LANES - EDGE
    y_next = [
        jnp.where(high, ahead[0], ahead[1]),
        jnp.where(high, ahead[1], jnp.where(patch < PATCHES - PZ, row_roll(ahead[0], -PZ), 0.0)),
    ]
    y_prev = [
        jnp.where(low, behind[0], jnp.where(patch >= PZ, row_roll(behind[1], PZ), 0.0)),
        jnp.where(low, behind[1], behind[0]),
    ]
    for h in range(2):
        t = u[h]
        z_next = jnp.where(
            not_last,
            lane_roll(t, -1),
            jnp.where(has_next, row_roll(lane_roll(t, EDGE - 1), -1), 0.0),
        )
        z_prev = jnp.where(
            not_first,
            lane_roll(t, 1),
            jnp.where(has_prev, row_roll(lane_roll(t, 1 - EDGE), 1), 0.0),
        )
        out.append((z_next + z_prev) + (y_next[h] + y_prev[h]))
    return out


def halves(ref, index):
    return [ref[index, :, :LANES], ref[index, :, LANES:]]


def put(ref, index, pair):
    ref[index, :, :LANES] = pair[0]
    ref[index, :, LANES:] = pair[1]


def field_of(ref, first):
    return [halves(ref, first), halves(ref, first + 1)]


def choose(flag, a, b):
    return [[jnp.where(flag, x, y) for x, y in zip(p, q)] for p, q in zip(a, b)]


def around(u, before, after):
    return [
        [n + (x + y) for n, x, y in zip(in_plane(u[part]), before[part], after[part])]
        for part in range(2)
    ]


def diagonal(wave):
    real, imag = 6.0 - wave, shift_imag * wave
    return real, imag


def smooth(u, total, rights, wave):
    real, imag = diagonal(wave)
    scale = omega_fine / (real * real + imag * imag)
    real, imag = real * scale, imag * scale
    keep = 1.0 - omega_fine
    out_re, out_im = [], []
    for h in range(2):
        a = rights[0][h] + total[0][h]
        b = rights[1][h] + total[1][h]
        out_re.append(keep * u[0][h] + (a * real - b * imag))
        out_im.append(keep * u[1][h] + (a * imag + b * real))
    return [out_re, out_im]


def residual(u, total, rights, wave):
    real, imag = diagonal(wave)
    out_re, out_im = [], []
    for h in range(2):
        out_re.append(rights[0][h] + total[0][h] - (real * u[0][h] + imag * u[1][h]))
        out_im.append(rights[1][h] + total[1][h] - (real * u[1][h] - imag * u[0][h]))
    return [out_re, out_im]


def position():
    return lax.axis_index("grp"), lax.axis_index("sub")


def low_side_open(g):
    last = lax.axis_size("grp") - 1
    beyond = jnp.where(g % 2 == 0, g - 1, g + 1)
    return (beyond >= 0) & (beyond <= last)


def pack_body(
    field_hbm, source_hbm, patch_hbm, index_hbm, table_hbm, out_ref,
    field_ref, source_ref, patch_ref, index_ref, table_ref, sems,
):
    pairs = (
        (field_hbm, field_ref),
        (source_hbm, source_ref),
        (patch_hbm, patch_ref),
        (index_hbm, index_ref),
        (table_hbm, table_ref),
    )
    copies = [pltpu.make_async_copy(a, b, sems.at[i]) for i, (a, b) in enumerate(pairs)]
    for copy in copies:
        copy.start()
    for copy in copies:
        copy.wait()
    g, _ = position()
    odd = g % 2 == 1
    for q in range(SLOTS):
        patch = jnp.full((1, LANES), patch_ref[q].astype(F32), F32)
        wave = jnp.full((1, LANES), table_ref[index_ref[q]], F32)
        for s in range(NS):
            out_ref[s, 10 * q + 8 : 10 * q + 9, :] = patch
            out_ref[s, 10 * q + 9 : 10 * q + 10, :] = wave
    for s in range(NS):
        layer = jnp.where(odd, EDGE - 1 - s, s)
        for q in range(SLOTS):
            for a, ref in enumerate((field_ref, source_ref)):
                for part in range(2):
                    row = 10 * q + 4 * a + 2 * part
                    cells = ref[q, part, pl.ds(layer, 1), :]
                    out_ref[s, row : row + 1, :] = cells[:, :LANES]
                    out_ref[s, row + 1 : row + 2, :] = cells[:, LANES:]


def place_body(raw_ref, plane_ref, field_ref, slot_ref):
    patches = raw_ref[pl.ds(8, LIVE, stride=10), :]
    held = (patches == iota((LIVE, LANES), 1).astype(F32)).astype(F32)
    slot_ref[...] = held
    pick = held.T[:PATCHES]
    order = (0, 1, 2, 3, 4, 5, 6, 7, 9)
    rows = jnp.concatenate([raw_ref[pl.ds(c, LIVE, stride=10), :] for c in order], 1)
    placed = select(pick, rows)
    for c in range(4):
        pair = [placed[:, CELLS * c : CELLS * c + LANES], placed[:, CELLS * c + LANES : CELLS * (c + 1)]]
        put(plane_ref, c, pair)
        if c < 2:
            put(field_ref, c, pair)
    put(plane_ref, 4, [placed[:, 4 * CELLS :]] * 2)


def first_body(own_ref, before_ref, after_ref, far_ref, out_ref):
    _, s = position()
    u = field_of(own_ref, 0)
    v = field_of(far_ref, 0)
    before = choose(s == 0, v, field_of(before_ref, 0))
    after = choose(s == NS - 1, v, field_of(after_ref, 0))
    new = smooth(u, around(u, before, after), field_of(own_ref, 2), own_ref[4, :, :LANES])
    for part in range(2):
        put(out_ref, part, new[part])
        put(out_ref, 2 + part, v[part])


def open_factor():
    g, s = position()
    return jnp.where((s >= NS // 2) | low_side_open(g), 1.0, 0.0)


def window_lane(shape, dim):
    cell = iota(shape, dim)
    part, inside = cell // CELLS, cell % CELLS
    return part * 64 + (inside // (4 * EDGE) + 2) * 8 + (inside % EDGE) // 4 + 2


def second_body(own_ref, far_ref, before_ref, after_ref, mine_ref, field_ref, sums_ref, values_ref):
    _, s = position()
    first, last = s == 0, s == NS - 1
    u = field_of(own_ref, 0)
    v = field_of(far_ref, 0)
    one = field_of(mine_ref, 0)
    rights = field_of(own_ref, 2)
    wave = own_ref[4, :, :LANES]
    v_before = choose(first, u, field_of(before_ref, 2))
    v_after = choose(last, u, field_of(after_ref, 2))
    v_one = smooth(v, around(v, v_before, v_after), field_of(far_ref, 2), far_ref[4, :, :LANES])
    factor = open_factor()
    v_one = [[x * factor for x in pair] for pair in v_one]
    before = choose(first, v_one, field_of(before_ref, 0))
    after = choose(last, v_one, field_of(after_ref, 0))
    two = smooth(one, around(one, before, after), rights, wave)
    for part in range(2):
        put(field_ref, part, two[part])
    r = residual(two, [in_plane(two[0]), in_plane(two[1])], rights, wave)
    rows = jnp.concatenate(
        [jnp.concatenate(r[0] + r[1], 1), jnp.concatenate(two[0] + two[1], 1)], 0
    )
    shape = (2 * CELLS, LANES)
    gather = jnp.where(window_lane(shape, 0) == iota(shape, 1), 1.0, 0.0)
    sums = select_lanes(rows, gather)
    lane = iota((PATCHES, LANES), 1)
    sums_ref[...] = jnp.where(lane == 0, wave, sums[:PATCHES])
    values_ref[...] = sums[PATCHES:]


def join_body(sums_ref, values_ref, before_ref, after_ref, out_ref):
    _, s = position()
    before = jnp.where(s == 0, 0.0, before_ref[...])
    after = jnp.where(s == NS - 1, 0.0, after_ref[...])
    out_ref[0] = sums_ref[...] + (before + after)
    out_ref[1] = values_ref[...]


def sides(x, patch, col):
    return (
        jnp.where(patch >= PZ, row_roll(x, PZ), 0.0),
        jnp.where(patch < PATCHES - PZ, row_roll(x, -PZ), 0.0),
        jnp.where(col > 0, row_roll(x, 1), 0.0),
        jnp.where(col < PZ - 1, row_roll(x, -1), 0.0),
    )


def windows(x):
    patch, lane = iota(x.shape, 0), iota(x.shape, 1)
    col = patch % PZ
    a, b = (lane // 8) % 8, lane % 8
    x = jnp.where((a >= 2) & (a < 6) & (b >= 2) & (b < 6), x, 0.0)
    _, _, low, high = sides(x, patch, col)
    x = x + jnp.where(b < 2, lane_roll(low, -4), 0.0) + jnp.where(b >= 6, lane_roll(high, 4), 0.0)
    low, high, _, _ = sides(x, patch, col)
    return x + jnp.where(a < 2, lane_roll(low, -32), 0.0) + jnp.where(a >= 6, lane_roll(high, 32), 0.0)


def slots_body(field_ref, own_ref, slot_ref, out_ref, wave_ref, patch_ref):
    _, s = position()
    rows = [half for c in range(2) for half in halves(field_ref, c)]
    out_ref[...] = select(slot_ref[:, :PATCHES], jnp.concatenate(rows, 1))
    wave = own_ref[4, :, :LANES]
    patch, lane = iota(wave.shape, 0), iota(wave.shape, 1)
    col = patch % PZ
    a, b = (lane // 8) % 8, lane % 8
    _, _, low, high = sides(wave, patch, col)
    wave = jnp.where(b < 2, low, jnp.where(b >= 6, high, wave))
    low, high, _, _ = sides(wave, patch, col)
    wave = jnp.where(a < 2, low, jnp.where(a >= 6, high, wave))
    mine = slot_ref[pl.ds(SLOTS * s, SLOTS), :]
    wave_ref[...] = select(mine[:, :PATCHES], wave)
    index = iota(mine.shape, 1).astype(F32) + 1.0
    patch_ref[...] = jnp.broadcast_to(jnp.sum(mine * index, 1, keepdims=True) - 1.0, mine.shape)


def bundle_body(sent_ref, block_ref, far_ref, slot_ref, out_ref):
    _, s = position()
    factor = open_factor()
    edge = jnp.where((s == 0) | (s == NS - 1), 1.0, 0.0)
    own = windows(block_ref[0] + edge * far_ref[1])
    far = windows(factor * (far_ref[0] + edge * block_ref[1]))
    patch, lane = iota(far.shape, 0), iota(far.shape, 1)
    wave = jnp.broadcast_to(far_ref[0, :, 0:1], far.shape)
    beside = (wave,) + sides(wave, patch, patch % PZ)
    for i, x in enumerate(beside):
        far = jnp.where(lane == i, x, far)
    placed = select(slot_ref[:, :PATCHES], jnp.concatenate([own, far], 1))
    for c in range(4):
        out_ref[pl.ds(c, LIVE, stride=6), :] = sent_ref[:, LANES * c : LANES * (c + 1)]
    for c in range(2):
        out_ref[pl.ds(4 + c, LIVE, stride=6), :] = placed[:, LANES * c : LANES * (c + 1)]


def coarse_sum(e):
    return (lane_roll(e, -1) + lane_roll(e, 1)) + (lane_roll(e, -8) + lane_roll(e, 8))


def correct_body(raw_ref, wave_ref, patch_ref, out_ref, grown_ref, smooth_ref):
    g, _ = position()
    odd = g % 2 == 1
    rows = 24
    shape = (SLOTS, LANES)

    def slot_rows(s, c):
        return raw_ref[pl.ds(rows * s + c, SLOTS, stride=6), :]

    def total(start, c):
        parts = [slot_rows(start + i, c) for i in range(4)]
        return ((parts[0] + parts[1]) + (parts[2] + parts[3])) * (1.0 / 64.0)

    lane = iota((LANES, LANES), 1)
    a, b = (lane // 8) % 8, lane % 8
    region = jnp.where(a < 2, 1, jnp.where(a >= 6, 2, jnp.where(b < 2, 3, jnp.where(b >= 6, 4, 0))))
    spread = jnp.where(iota((LANES, LANES), 0) == region, 1.0, 0.0)
    ends = jnp.concatenate([slot_rows(0, 5), slot_rows(NS - 1, 5)], 0)
    ends = select_lanes(ends, spread)
    low, high = ends[:SLOTS], ends[SLOTS:]
    own = wave_ref[...]
    wave = jnp.concatenate([low, low, own, own, own, own, high, high], 0)
    rhs = jnp.concatenate(
        [total(4, 5), total(0, 5)] + [total(4 * i, 4) for i in range(4)] + [total(12, 5), total(8, 5)], 0
    )
    lane = iota(shape, 1)
    a, b = (lane // 8) % 8, lane % 8
    patch = patch_ref[...].astype(jnp.int32)
    line, col = patch // PZ, patch % PZ
    y, z = 4 * line + a - 2, 4 * col + b - 2
    inside = jnp.where((y >= 0) & (y < 4 * PY) & (z >= 0) & (z < 4 * PZ), 1.0, 0.0)
    lower = jnp.where(low_side_open(g), inside, 0.0)
    inside = jnp.concatenate([lower, lower] + [inside] * 6, 0) > 0.0
    part_sign = jnp.where(iota(wave.shape, 1) < 64, -1.0, 1.0)
    real, imag = 6.0 / 16.0 - wave, shift_imag * wave
    scale = omega_coarse / (real * real + imag * imag)
    real, imag = real * scale, part_sign * imag * scale

    def divide(x):
        return jnp.where(inside, x * real + lane_roll(x, 64) * imag, 0.0)

    e = divide(rhs)
    for _ in range(2):
        beside = coarse_sum(e) + (row_roll(e, SLOTS) + row_roll(e, -SLOTS))
        e = (1.0 - omega_coarse) * e + divide(rhs + beside * (1.0 / 16.0))
    wide = (LANES, 2 * CELLS)
    widen = jnp.where(window_lane(wide, 1) == iota(wide, 0), 1.0, 0.0)
    grown_ref[...] = select_lanes(e[2 * SLOTS : 6 * SLOTS], widen)
    for i in range(EDGE):
        s = jnp.where(odd, EDGE - 1 - i, i)
        for q in range(SLOTS):
            for part in range(2):
                for h in range(2):
                    row = raw_ref[pl.ds(rows * s + 6 * q + 2 * part + h, 1), :]
                    smooth_ref[2 * q + part, i : i + 1, LANES * h : LANES * (h + 1)] = row
    for q in range(SLOTS):
        held = jnp.broadcast_to(patch_ref[q : q + 1, 0:1] >= 0.0, (4, CELLS))
        for i in range(4):
            plane = jnp.where(odd, 3 - i, i)
            line = grown_ref[pl.ds(SLOTS * plane + q, 1), :]
            for part in range(2):
                extra = jnp.broadcast_to(line[:, CELLS * part : CELLS * (part + 1)], (4, CELLS))
                value = smooth_ref[2 * q + part, 4 * i : 4 * i + 4] + extra
                out_ref[q, part, 4 * i : 4 * i + 4] = jnp.where(held, value, 0.0)


def swap_pairs(groups, subs):
    pairs = []
    for s in subs:
        for g in range(0 if s >= NS // 2 else 1, groups - 1, 2):
            a, b = g * NS + s, (g + 1) * NS + s
            pairs += [(a, b), (b, a)]
    return pairs


def body(field, source, patch_of_slot, neighbour, wave_index, wave_table):
    groups = lax.axis_size("grp")
    both = ("grp", "sub")
    up = [(i, (i + 1) % NS) for i in range(NS)]
    down = [((i + 1) % NS, i) for i in range(NS)]
    ring = lambda x: (lax.ppermute(x, "sub", up), lax.ppermute(x, "sub", down))
    plane = (PATCHES, CELLS)

    hbm = pl.BlockSpec(memory_space=pltpu.HBM)
    (packed,) = call(
        pack_body,
        [(NS, 40, LANES)],
        [field, source, patch_of_slot, wave_index, wave_table],
        [
            field.shape,
            source.shape,
            pltpu.SMEM(patch_of_slot.shape, jnp.int32),
            pltpu.SMEM(wave_index.shape, jnp.int32),
            pltpu.SMEM(wave_table.shape, F32),
            pltpu.SemaphoreType.DMA((5,)),
        ],
        [hbm] * 5,
        60,
    )
    raw = lax.all_to_all(packed, "sub", 0, 0, tiled=True).reshape(NS * 40, LANES)
    own, start, slot = call(place_body, [(5,) + plane, (2,) + plane, (LIVE, LANES)], [raw])
    far = lax.ppermute(own, both, swap_pairs(groups, (0, 1, 14, 15)))
    before, after = ring(start)
    (one,) = call(first_body, [(4,) + plane], [own, before, after, far])
    before, after = ring(one)
    row = (PATCHES, LANES)
    two, sums, values = call(
        second_body, [(2,) + plane, row, row], [own, far, before, after, one]
    )
    before, after = ring(values)
    mine = (SLOTS, LANES)
    sent, wave, patch = call(slots_body, [(LIVE, 2 * CELLS), mine, mine], [two, own, slot])
    (block,) = call(join_body, [(2,) + row], [sums, values, before, after])
    far_block = lax.ppermute(block, both, swap_pairs(groups, range(NS)))
    (bundle,) = call(bundle_body, [(LIVE * 6, LANES)], [sent, block, far_block, slot])
    back = lax.all_to_all(bundle.reshape(NS, 24, LANES), "sub", 0, 0, tiled=True)
    (out,) = call(
        correct_body,
        [(SLOTS, 2, EDGE, CELLS)],
        [back.reshape(NS * 24, LANES), wave, patch],
        [(EDGE, 2 * CELLS), (2 * SLOTS, EDGE, CELLS)],
    )
    return out


def solution(mesh):
    return jax.shard_map(
        body,
        mesh=mesh,
        in_specs=(
            P(("grp", "sub"), None, None, None),
            P(("grp", "sub"), None, None, None),
            P(("grp", "sub")),
            P(("grp", "sub"), None),
            P(("grp", "sub")),
            P(),
        ),
        out_specs=P(("grp", "sub"), None, None, None),
        check_vma=False,
    )
```

time: 94.2 us -> 72.5 us (0.77)
  Pallas kernels: 15.8 us -> 5.26 us
  blocking collectives: 42.2 us -> 37.4 us
  local copies, waits for them, and re-layouts: 3.42 us -> 0 us
  waiting for transfers between devices: 16.8 us -> 14.1 us
    pallas_call x7 -> x8, Pallas kernels: 15.8 us -> 5.26 us  [call(): pl.pallas_call(body, out_shape=[jax.ShapeDtypeStruct(shape, F32) for shap...]
    all_to_all x1, blocking collectives: 21.3 us -> 16.5 us  [body(): lax.all_to_all(bundle.reshape(NS, 24, LANES), 'sub', 0, 0, tiled=True)]
    unnamed x16 -> x0, local copies, waits for them, and re-layouts: 3.42 us -> none
    ppermute x6, waiting for transfers between devices: 10.5 us -> 7.75 us  [body(): ring = lambda x: (lax.ppermute(x, 'sub', up), lax.ppermute(x, 'sub', down))]
where the time goes in v2:
time: 72.5 us; the launch traced here: 72.3 us
  blocking collectives  37.4 us (52%)
  starting transfers between devices  15.5 us (21%)
  waiting for transfers between devices  14.1 us (19%)
  Pallas kernels  5.26 us (7%)
    all_to_all x1, blocking collectives, body(): lax.all_to_all(packed, 'sub', 0, 0, tiled=True).reshape(NS * 40, LANES)  20.9 us
    all_to_all x1, blocking collectives, body(): lax.all_to_all(bundle.reshape(NS, 24, LANES), 'sub', 0, 0, tiled=True)  16.5 us
    ppermute x6, waiting for transfers between devices, body(): ring = lambda x: (lax.ppermute(x, 'sub', up), lax.ppermute(x, 'sub', down))  7.75 us
    ppermute x6, starting transfers between devices, body(): ring = lambda x: (lax.ppermute(x, 'sub', up), lax.ppermute(x, 'sub', down))  5.27 us
    pallas_call x8, Pallas kernels, call(): pl.pallas_call(body, out_shape=[jax.ShapeDtypeStruct(shape, F32) for shap...  5.26 us
    ppermute x1, starting transfers between devices, body(): far = lax.ppermute(own, both, swap_pairs(groups, (0, 1, 14, 15)))  5.12 us
    ppermute x1, starting transfers between devices, body(): far_block = lax.ppermute(block, both, swap_pairs(groups, range(NS)))  5.12 us
    ppermute x1, waiting for transfers between devices, body(): far = lax.ppermute(own, both, swap_pairs(groups, (0, 1, 14, 15)))  3.48 us
  transfers between devices with their start and end apart: 8, of which 5 were waited for; matrix products, arithmetic and copies ran while one was open for 0% of the time, Pallas kernels for 0%

profile of v2, /device:TPU:199, one launch (start us, length us, event | category | flops | bytes accessed | tf_op | source)
XLA Modules:
  0.0 72.3 jit_solution(14252740831359965455)
XLA Ops:
  0.0 2.0 %shard_map.55 = f32[16,40,128]{2,1,0:T(8,128)} custom-call(f32[4,2,16,256]{3,2,1,0:T(8,128)} %field_hbm.1, f32[4,2,16,256]{3,2,1,0:T(8,128)} %source_hbm.1, s32[4]{0:T(128)} %patch_hbm.1, s32[4]{0:T(128)} %index_hbm.1, f32[16]{0:T(128)} %table_hbm.1), custom_call_target="tpu_custom_call" | custom-call | tf_op jit(solution)/shard_map/pallas_call | solution.py:28
  2.0 20.9 %all_to_all.10 = f32[16,40,128]{2,1,0:T(8,128)S(1)} all-to-all(f32[16,40,128]{2,1,0:T(8,128)} %shard_map.55), channel_id=1, replica_groups=mesh['grp'=32,'sub'=16] {'sub'}, dimensions={0} | all-to-all | bytes 655360 | tf_op jit(solution)/shard_map/all_to_all | solution.py:441
  22.9 0.3 shard_map.56
  23.2 5.1 %collective-permute-start = (f32[5,48,256]{2,1,0:T(8,128)S(1)}, f32[5,48,256]{2,1,0:T(8,128)S(1)}, u32[]{:S(2)}, u32[]{:S(2)}) collective-permute-start(f32[5,48,256]{2,1,0:T(8,128)S(1)} %get-tuple-element.14.own_ref), channel_id=1, source_target_pairs={{16,32},{32,16},{48,64},{64,48},{80,96},{96,80},{112,128},{128,112... | collective-permute-start | bytes 737288 | tf_op jit(solution)/shard_map/ppermute | solution.py:443
  28.3 0.0 collective-permute-start.2
  28.3 1.7 %collective-permute-start.1 = (f32[2,48,256]{2,1,0:T(8,128)S(1)}, f32[2,48,256]{2,1,0:T(8,128)S(1)}, u32[]{:S(2)}, u32[]{:S(2)}) collective-permute-start(f32[2,48,256]{2,1,0:T(8,128)S(1)} %get-tuple-element.15), channel_id=1, source_target_pairs={{0,1},{1,2},{2,3},{3,4},{4,5},{5,6},{6,7},{7,8},{8,9},{9,10},{10,1... | collective-permute-start | bytes 294920 | tf_op jit(solution)/shard_map/ppermute | solution.py:422
  30.1 2.6 %collective-permute-done.2.after_ref = f32[2,48,256]{2,1,0:T(8,128)S(1)} collective-permute-done((f32[2,48,256]{2,1,0:T(8,128)S(1)}, f32[2,48,256]{2,1,0:T(8,128)S(1)}, u32[]{:S(2)}, u32[]{:S(2)}) %collective-permute-start.2) | collective-permute-done | bytes 98336 | tf_op jit(solution)/shard_map/ppermute | solution.py:422
  32.7 0.0 collective-permute-done.1.before_ref
  32.7 3.5 %collective-permute-done.far_ref = f32[5,48,256]{2,1,0:T(8,128)S(1)} collective-permute-done((f32[5,48,256]{2,1,0:T(8,128)S(1)}, f32[5,48,256]{2,1,0:T(8,128)S(1)}, u32[]{:S(2)}, u32[]{:S(2)}) %collective-permute-start) | collective-permute-done | bytes 245792 | tf_op jit(solution)/shard_map/ppermute | solution.py:443
  36.1 0.2 shard_map.57.mine_ref
  36.4 0.4 collective-permute-start.4
  36.8 1.4 %collective-permute-start.3 = (f32[4,48,256]{2,1,0:T(8,128)S(1)}, f32[4,48,256]{2,1,0:T(8,128)S(1)}, u32[]{:S(2)}, u32[]{:S(2)}) collective-permute-start(f32[4,48,256]{2,1,0:T(8,128)S(1)} %shard_map.57.mine_ref), channel_id=1, source_target_pairs={{0,1},{1,2},{2,3},{3,4},{4,5},{5,6},{6,7},{7,8},{8,9},{9,10},{10,1... | collective-permute-start | bytes 589832 | tf_op jit(solution)/shard_map/ppermute | solution.py:422
  38.1 3.6 %collective-permute-done.4.after_ref = f32[4,48,256]{2,1,0:T(8,128)S(1)} collective-permute-done((f32[4,48,256]{2,1,0:T(8,128)S(1)}, f32[4,48,256]{2,1,0:T(8,128)S(1)}, u32[]{:S(2)}, u32[]{:S(2)}) %collective-permute-start.4) | collective-permute-done | bytes 196640 | tf_op jit(solution)/shard_map/ppermute | solution.py:422
  41.8 0.9 %shard_map.58 = (f32[2,48,256]{2,1,0:T(8,128)S(1)}, f32[48,128]{1,0:T(8,128)S(1)}, f32[48,128]{1,0:T(8,128)S(1)}) custom-call(f32[5,48,256]{2,1,0:T(8,128)S(1)} %get-tuple-element.14.own_ref, f32[5,48,256]{2,1,0:T(8,128)S(1)} %collective-permute-done.far_ref, f32[4,48,256]{2,1,0:T(8,128)S(1)} %collective-permute-done.3.before_ref, ...), custom_call_target="tpu_custom_call" | custom-call | tf_op jit(solution)/shard_map/pallas_call | solution.py:28
  42.7 1.3 %collective-permute-start.6 = (f32[48,128]{1,0:T(8,128)S(1)}, f32[48,128]{1,0:T(8,128)S(1)}, u32[]{:S(2)}, u32[]{:S(2)}) collective-permute-start(f32[48,128]{1,0:T(8,128)S(1)} %get-tuple-element.20.values_ref), channel_id=1, source_target_pairs={{1,0},{2,1},{3,2},{4,3},{5,4},{6,5},{7,6},{8,7},{9,8},{10,9},{11,1... | collective-permute-start | bytes 73736 | tf_op jit(solution)/shard_map/ppermute | solution.py:422
  44.0 0.4 collective-permute-start.5
  44.4 1.5 %collective-permute-done.6.after_ref = f32[48,128]{1,0:T(8,128)S(1)} collective-permute-done((f32[48,128]{1,0:T(8,128)S(1)}, f32[48,128]{1,0:T(8,128)S(1)}, u32[]{:S(2)}, u32[]{:S(2)}) %collective-permute-start.6) | collective-permute-done | bytes 24608 | tf_op jit(solution)/shard_map/ppermute | solution.py:422
  45.9 0.0 collective-permute-done.5.before_ref
  45.9 5.1 %collective-permute-start.7 = (f32[2,48,128]{2,1,0:T(8,128)S(1)}, f32[2,48,128]{2,1,0:T(8,128)S(1)}, u32[]{:S(2)}, u32[]{:S(2)}) collective-permute-start(f32[2,48,128]{2,1,0:T(8,128)S(1)} %shard_map.60.block_ref), channel_id=1, source_target_pairs={{16,32},{32,16},{48,64},{64,48},{80,96},{96,80},{112,128},{128,112... | collective-permute-start | bytes 147464 | tf_op jit(solution)/shard_map/ppermute | solution.py:455
  51.1 0.2 shard_map.59
  51.3 2.8 %collective-permute-done.7.far_ref = f32[2,48,128]{2,1,0:T(8,128)S(1)} collective-permute-done((f32[2,48,128]{2,1,0:T(8,128)S(1)}, f32[2,48,128]{2,1,0:T(8,128)S(1)}, u32[]{:S(2)}, u32[]{:S(2)}) %collective-permute-start.7) | collective-permute-done | bytes 49184 | tf_op jit(solution)/shard_map/ppermute | solution.py:455
  54.1 0.3 shard_map.61
  54.4 16.5 %all_to_all.11 = f32[16,24,128]{2,1,0:T(8,128)S(1)} all-to-all(f32[16,24,128]{2,1,0:T(8,128)S(1)} %bitcast.4), channel_id=1, replica_groups=mesh['grp'=32,'sub'=16] {'sub'}, dimensions={0} | all-to-all | bytes 393216 | tf_op jit(solution)/shard_map/all_to_all | solution.py:457
  70.9 1.3 %shard_map.62 = f32[4,2,16,256]{3,2,1,0:T(8,128)} custom-call(f32[384,128]{1,0:T(8,128)S(1)} %bitcast.5, f32[4,128]{1,0:T(4,128)S(1)} %get-tuple-element.21.wave_ref, f32[4,128]{1,0:T(4,128)S(1)} %get-tuple-element.22.patch_ref), custom_call_target="tpu_custom_call" | custom-call | tf_op jit(solution)/shard_map/pallas_call | solution.py:28
  (2 shorter events, 0.0 us)
Async XLA Ops:
  23.2 13.0 %collective-permute-start = (f32[5,48,256]{2,1,0:T(8,128)S(1)}, f32[5,48,256]{2,1,0:T(8,128)S(1)}, u32[]{:S(2)}, u32[]{:S(2)}) collective-permute-start(f32[5,48,256]{2,1,0:T(8,128)S(1)} %get-tuple-element.14.own_ref), channel_id=1, source_target_pairs={{16,32},{32,16},{48,64},{64,48},{80,96},{96,80},{112,128},{128,112... | collective-permute-start | bytes 737288 | tf_op jit(solution)/shard_map/ppermute | solution.py:443
  28.3 4.3 %collective-permute-start.2 = (f32[2,48,256]{2,1,0:T(8,128)S(1)}, f32[2,48,256]{2,1,0:T(8,128)S(1)}, u32[]{:S(2)}, u32[]{:S(2)}) collective-permute-start(f32[2,48,256]{2,1,0:T(8,128)S(1)} %get-tuple-element.15), channel_id=1, source_target_pairs={{1,0},{2,1},{3,2},{4,3},{5,4},{6,5},{7,6},{8,7},{9,8},{10,9},{11,1... | collective-permute-start | bytes 294920 | tf_op jit(solution)/shard_map/ppermute | solution.py:422
  28.3 4.3 %collective-permute-start.1 = (f32[2,48,256]{2,1,0:T(8,128)S(1)}, f32[2,48,256]{2,1,0:T(8,128)S(1)}, u32[]{:S(2)}, u32[]{:S(2)}) collective-permute-start(f32[2,48,256]{2,1,0:T(8,128)S(1)} %get-tuple-element.15), channel_id=1, source_target_pairs={{0,1},{1,2},{2,3},{3,4},{4,5},{5,6},{6,7},{7,8},{8,9},{9,10},{10,1... | collective-permute-start | bytes 294920 | tf_op jit(solution)/shard_map/ppermute | solution.py:422
  36.4 5.4 %collective-permute-start.4 = (f32[4,48,256]{2,1,0:T(8,128)S(1)}, f32[4,48,256]{2,1,0:T(8,128)S(1)}, u32[]{:S(2)}, u32[]{:S(2)}) collective-permute-start(f32[4,48,256]{2,1,0:T(8,128)S(1)} %shard_map.57.mine_ref), channel_id=1, source_target_pairs={{1,0},{2,1},{3,2},{4,3},{5,4},{6,5},{7,6},{8,7},{9,8},{10,9},{11,1... | collective-permute-start | bytes 589832 | tf_op jit(solution)/shard_map/ppermute | solution.py:422
  36.8 5.0 %collective-permute-start.3 = (f32[4,48,256]{2,1,0:T(8,128)S(1)}, f32[4,48,256]{2,1,0:T(8,128)S(1)}, u32[]{:S(2)}, u32[]{:S(2)}) collective-permute-start(f32[4,48,256]{2,1,0:T(8,128)S(1)} %shard_map.57.mine_ref), channel_id=1, source_target_pairs={{0,1},{1,2},{2,3},{3,4},{4,5},{5,6},{6,7},{7,8},{8,9},{9,10},{10,1... | collective-permute-start | bytes 589832 | tf_op jit(solution)/shard_map/ppermute | solution.py:422
  42.7 3.3 %collective-permute-start.6 = (f32[48,128]{1,0:T(8,128)S(1)}, f32[48,128]{1,0:T(8,128)S(1)}, u32[]{:S(2)}, u32[]{:S(2)}) collective-permute-start(f32[48,128]{1,0:T(8,128)S(1)} %get-tuple-element.20.values_ref), channel_id=1, source_target_pairs={{1,0},{2,1},{3,2},{4,3},{5,4},{6,5},{7,6},{8,7},{9,8},{10,9},{11,1... | collective-permute-start | bytes 73736 | tf_op jit(solution)/shard_map/ppermute | solution.py:422
  44.0 1.9 %collective-permute-start.5 = (f32[48,128]{1,0:T(8,128)S(1)}, f32[48,128]{1,0:T(8,128)S(1)}, u32[]{:S(2)}, u32[]{:S(2)}) collective-permute-start(f32[48,128]{1,0:T(8,128)S(1)} %get-tuple-element.20.values_ref), channel_id=1, source_target_pairs={{0,1},{1,2},{2,3},{3,4},{4,5},{5,6},{6,7},{7,8},{8,9},{9,10},{10,1... | collective-permute-start | bytes 73736 | tf_op jit(solution)/shard_map/ppermute | solution.py:422
  45.9 8.2 %collective-permute-start.7 = (f32[2,48,128]{2,1,0:T(8,128)S(1)}, f32[2,48,128]{2,1,0:T(8,128)S(1)}, u32[]{:S(2)}, u32[]{:S(2)}) collective-permute-start(f32[2,48,128]{2,1,0:T(8,128)S(1)} %shard_map.60.block_ref), channel_id=1, source_target_pairs={{16,32},{32,16},{48,64},{64,48},{80,96},{96,80},{112,128},{128,112... | collective-permute-start | bytes 147464 | tf_op jit(solution)/shard_map/ppermute | solution.py:455

commit v3 on v2

--- a/solution.py
+++ b/solution.py
@@ -158,7 +158,11 @@
 
 
 def position():
-    return lax.axis_index("grp"), lax.axis_index("sub")
+    return lax.axis_index("grp"), (lax.axis_index("sub") + NS - 1) % NS
+
+
+def device_at(place):
+    return (place + 1) % NS
 
 
 def low_side_open(g):
@@ -192,7 +196,8 @@
             out_ref[s, 10 * q + 8 : 10 * q + 9, :] = patch
             out_ref[s, 10 * q + 9 : 10 * q + 10, :] = wave
     for s in range(NS):
-        layer = jnp.where(odd, EDGE - 1 - s, s)
+        place = (s + NS - 1) % NS
+        layer = jnp.where(odd, EDGE - 1 - place, place)
         for q in range(SLOTS):
             for a, ref in enumerate((field_ref, source_ref)):
                 for part in range(2):
@@ -221,7 +226,8 @@
 def first_body(own_ref, before_ref, after_ref, far_ref, out_ref):
     _, s = position()
     u = field_of(own_ref, 0)
-    v = field_of(far_ref, 0)
+    factor = open_factor()
+    v = [[x * factor for x in pair] for pair in field_of(far_ref.at[other()], 0)]
     before = choose(s == 0, v, field_of(before_ref, 0))
     after = choose(s == NS - 1, v, field_of(after_ref, 0))
     new = smooth(u, around(u, before, after), field_of(own_ref, 2), own_ref[4, :, :LANES])
@@ -230,6 +236,11 @@
         put(out_ref, 2 + part, v[part])
 
 
+def other():
+    g, s = position()
+    return jnp.where((g % 2 == 0) == (s >= NS // 2), 1, 0)
+
+
 def open_factor():
     g, s = position()
     return jnp.where((s >= NS // 2) | low_side_open(g), 1.0, 0.0)
@@ -245,14 +256,15 @@
     _, s = position()
     first, last = s == 0, s == NS - 1
     u = field_of(own_ref, 0)
-    v = field_of(far_ref, 0)
+    far_ref = far_ref.at[other()]
+    factor = open_factor()
+    v = [[x * factor for x in pair] for pair in field_of(far_ref, 0)]
     one = field_of(mine_ref, 0)
     rights = field_of(own_ref, 2)
     wave = own_ref[4, :, :LANES]
     v_before = choose(first, u, field_of(before_ref, 2))
     v_after = choose(last, u, field_of(after_ref, 2))
     v_one = smooth(v, around(v, v_before, v_after), field_of(far_ref, 2), far_ref[4, :, :LANES])
-    factor = open_factor()
     v_one = [[x * factor for x in pair] for pair in v_one]
     before = choose(first, v_one, field_of(before_ref, 0))
     after = choose(last, v_one, field_of(after_ref, 0))
@@ -267,16 +279,18 @@
     gather = jnp.where(window_lane(shape, 0) == iota(shape, 1), 1.0, 0.0)
     sums = select_lanes(rows, gather)
     lane = iota((PATCHES, LANES), 1)
-    sums_ref[...] = jnp.where(lane == 0, wave, sums[:PATCHES])
-    values_ref[...] = sums[PATCHES:]
-
-
-def join_body(sums_ref, values_ref, before_ref, after_ref, out_ref):
+    values = sums[PATCHES:]
+    beside = jnp.where((s % 4 == 0) | (s % 4 == 3), 1.0, 2.0)
+    sums_ref[...] = jnp.where(lane == 0, wave, sums[:PATCHES] + beside * values)
+    values_ref[...] = values
+
+
+def join_body(sums_ref, pair_ref, out_ref):
     _, s = position()
-    before = jnp.where(s == 0, 0.0, before_ref[...])
-    after = jnp.where(s == NS - 1, 0.0, after_ref[...])
-    out_ref[0] = sums_ref[...] + (before + after)
-    out_ref[1] = values_ref[...]
+    core = lax.axis_index("sub") % 2
+    meets = ((s % 4 == 0) | (s % 4 == 3)) & (s > 0) & (s < NS - 1)
+    out_ref[0] = sums_ref[...] + jnp.where(meets, pair_ref[1 - core], 0.0)
+    out_ref[1] = pair_ref[core]
 
 
 def sides(x, patch, col):
@@ -311,7 +325,7 @@
     wave = jnp.where(b < 2, low, jnp.where(b >= 6, high, wave))
     low, high, _, _ = sides(wave, patch, col)
     wave = jnp.where(a < 2, low, jnp.where(a >= 6, high, wave))
-    mine = slot_ref[pl.ds(SLOTS * s, SLOTS), :]
+    mine = slot_ref[pl.ds(SLOTS * device_at(s), SLOTS), :]
     wave_ref[...] = select(mine[:, :PATCHES], wave)
     index = iota(mine.shape, 1).astype(F32) + 1.0
     patch_ref[...] = jnp.broadcast_to(jnp.sum(mine * index, 1, keepdims=True) - 1.0, mine.shape)
@@ -320,8 +334,9 @@
 def bundle_body(sent_ref, block_ref, far_ref, slot_ref, out_ref):
     _, s = position()
     factor = open_factor()
+    far_ref = far_ref.at[other()]
     edge = jnp.where((s == 0) | (s == NS - 1), 1.0, 0.0)
-    own = windows(block_ref[0] + edge * far_ref[1])
+    own = windows(block_ref[0] + (edge * factor) * far_ref[1])
     far = windows(factor * (far_ref[0] + edge * block_ref[1]))
     patch, lane = iota(far.shape, 0), iota(far.shape, 1)
     wave = jnp.broadcast_to(far_ref[0, :, 0:1], far.shape)
@@ -349,14 +364,14 @@
         return raw_ref[pl.ds(rows * s + c, SLOTS, stride=6), :]
 
     def total(start, c):
-        parts = [slot_rows(start + i, c) for i in range(4)]
+        parts = [slot_rows(device_at(start + i), c) for i in range(4)]
         return ((parts[0] + parts[1]) + (parts[2] + parts[3])) * (1.0 / 64.0)
 
     lane = iota((LANES, LANES), 1)
     a, b = (lane // 8) % 8, lane % 8
     region = jnp.where(a < 2, 1, jnp.where(a >= 6, 2, jnp.where(b < 2, 3, jnp.where(b >= 6, 4, 0))))
     spread = jnp.where(iota((LANES, LANES), 0) == region, 1.0, 0.0)
-    ends = jnp.concatenate([slot_rows(0, 5), slot_rows(NS - 1, 5)], 0)
+    ends = jnp.concatenate([slot_rows(device_at(0), 5), slot_rows(device_at(NS - 1), 5)], 0)
     ends = select_lanes(ends, spread)
     low, high = ends[:SLOTS], ends[SLOTS:]
     own = wave_ref[...]
@@ -388,7 +403,7 @@
     widen = jnp.where(window_lane(wide, 1) == iota(wide, 0), 1.0, 0.0)
     grown_ref[...] = select_lanes(e[2 * SLOTS : 6 * SLOTS], widen)
     for i in range(EDGE):
-        s = jnp.where(odd, EDGE - 1 - i, i)
+        s = device_at(jnp.where(odd, EDGE - 1 - i, i))
         for q in range(SLOTS):
             for part in range(2):
                 for h in range(2):
@@ -405,12 +420,19 @@
                 out_ref[q, part, 4 * i : 4 * i + 4] = jnp.where(held, value, 0.0)
 
 
-def swap_pairs(groups, subs):
-    pairs = []
-    for s in subs:
-        for g in range(0 if s >= NS // 2 else 1, groups - 1, 2):
-            a, b = g * NS + s, (g + 1) * NS + s
-            pairs += [(a, b), (b, a)]
+def facing(groups, reach):
+    pairs, met = [], set()
+    for place in [i for i in range(NS) if i < reach or i >= NS - reach]:
+        s = device_at(place)
+        for g in range(0 if place >= NS // 2 else 1, groups - 1, 2):
+            pairs.append([g * NS + s, (g + 1) * NS + s])
+            met.update(pairs[-1])
+    for g in range(groups):
+        rest = [g * NS + s for s in range(NS) if g * NS + s not in met]
+        whole = [i for i in rest if i ^ 1 in rest]
+        rest = [i for i in rest if i ^ 1 not in rest]
+        pairs += [whole[i : i + 2] for i in range(0, len(whole), 2)]
+        pairs += [rest[i : i + 2] for i in range(0, len(rest), 2)]
     return pairs
 
 
@@ -440,7 +462,7 @@
     )
     raw = lax.all_to_all(packed, "sub", 0, 0, tiled=True).reshape(NS * 40, LANES)
     own, start, slot = call(place_body, [(5,) + plane, (2,) + plane, (LIVE, LANES)], [raw])
-    far = lax.ppermute(own, both, swap_pairs(groups, (0, 1, 14, 15)))
+    far = lax.all_gather(own, both, axis_index_groups=facing(groups, 2))
     before, after = ring(start)
     (one,) = call(first_body, [(4,) + plane], [own, before, after, far])
     before, after = ring(one)
@@ -448,11 +470,12 @@
     two, sums, values = call(
         second_body, [(2,) + plane, row, row], [own, far, before, after, one]
     )
-    before, after = ring(values)
+    chips = [[i, i + 1] for i in range(0, NS, 2)]
+    pair = lax.all_gather(values, "sub", axis_index_groups=chips)
     mine = (SLOTS, LANES)
     sent, wave, patch = call(slots_body, [(LIVE, 2 * CELLS), mine, mine], [two, own, slot])
-    (block,) = call(join_body, [(2,) + row], [sums, values, before, after])
-    far_block = lax.ppermute(block, both, swap_pairs(groups, range(NS)))
+    (block,) = call(join_body, [(2,) + row], [sums, pair])
+    far_block = lax.all_gather(block, both, axis_index_groups=facing(groups, NS // 2))
     (bundle,) = call(bundle_body, [(LIVE * 6, LANES)], [sent, block, far_block, slot])
     back = lax.all_to_all(bundle.reshape(NS, 24, LANES), "sub", 0, 0, tiled=True)
     (out,) = call(

time: 72.5 us -> 65.8 us (0.908)
  blocking collectives: 37.4 us -> 53.4 us
  starting transfers between devices: 15.5 us -> 3.5 us
  waiting for transfers between devices: 14.1 us -> 3.36 us
    all_gather x0 -> x3, blocking collectives: none -> 17.8 us  [the longest x1 9.03 us: body(): far = lax.all_gather(own, both, axis_index_groups=facing(groups, 2))]
    ppermute x2 -> x0, starting transfers between devices: 10.2 us -> none  [the longest x1 5.12 us: body(): far = lax.ppermute(own, both, swap_pairs(groups, (0, 1, 14, 15)))]
    ppermute x2 -> x0, waiting for transfers between devices: 6.31 us -> none  [the longest x1 3.48 us: body(): far = lax.ppermute(own, both, swap_pairs(groups, (0, 1, 14, 15)))]
    ppermute x6 -> x4, waiting for transfers between devices: 7.75 us -> 3.36 us  [body(): ring = lambda x: (lax.ppermute(x, 'sub', up), lax.ppermute(x, 'sub', down))]
    all_to_all x1, blocking collectives: 16.5 us -> 14.7 us  [body(): lax.all_to_all(bundle.reshape(NS, 24, LANES), 'sub', 0, 0, tiled=True)]
    ppermute x6 -> x4, starting transfers between devices: 5.27 us -> 3.5 us  [body(): ring = lambda x: (lax.ppermute(x, 'sub', up), lax.ppermute(x, 'sub', down))]
  transfers between devices with their start and end apart: 8 -> 4, of which waited for: 5 -> 1; matrix products, arithmetic and copies ran while one was open for 0% -> 0% of each run, Pallas kernels for 0% -> 0%
where the time goes in v3:
time: 65.8 us; the launch traced here: 65.6 us
  blocking collectives  53.4 us (81%)
  Pallas kernels  5.28 us (8%)
  starting transfers between devices  3.5 us (5%)
  waiting for transfers between devices  3.36 us (5%)
    all_to_all x1, blocking collectives, body(): lax.all_to_all(packed, 'sub', 0, 0, tiled=True).reshape(NS * 40, LANES)  20.9 us
    all_to_all x1, blocking collectives, body(): lax.all_to_all(bundle.reshape(NS, 24, LANES), 'sub', 0, 0, tiled=True)  14.7 us
    all_gather x1, blocking collectives, body(): far = lax.all_gather(own, both, axis_index_groups=facing(groups, 2))  9.03 us
    all_gather x1, blocking collectives, body(): lax.all_gather(block, both, axis_index_groups=facing(groups, NS // 2))  6.94 us
    pallas_call x8, Pallas kernels, call(): pl.pallas_call(body, out_shape=[jax.ShapeDtypeStruct(shape, F32) for shap...  5.28 us
    ppermute x4, starting transfers between devices, body(): ring = lambda x: (lax.ppermute(x, 'sub', up), lax.ppermute(x, 'sub', down))  3.5 us
    ppermute x4, waiting for transfers between devices, body(): ring = lambda x: (lax.ppermute(x, 'sub', up), lax.ppermute(x, 'sub', down))  3.36 us
    all_gather x1, blocking collectives, body(): pair = lax.all_gather(values, 'sub', axis_index_groups=chips)  1.84 us
  transfers between devices with their start and end apart: 4, of which 1 were waited for; matrix products, arithmetic and copies ran while one was open for 0% of the time, Pallas kernels for 0%

profile of v3, /device:TPU:199, one launch (start us, length us, event | category | flops | bytes accessed | tf_op | source)
XLA Modules:
  0.0 65.6 jit_solution(7402927156560640611)
XLA Ops:
  0.0 2.0 %shard_map.55 = f32[16,40,128]{2,1,0:T(8,128)} custom-call(f32[4,2,16,256]{3,2,1,0:T(8,128)} %field_hbm.1, f32[4,2,16,256]{3,2,1,0:T(8,128)} %source_hbm.1, s32[4]{0:T(128)} %patch_hbm.1, s32[4]{0:T(128)} %index_hbm.1, f32[16]{0:T(128)} %table_hbm.1), custom_call_target="tpu_custom_call" | custom-call | tf_op jit(solution)/shard_map/pallas_call | solution.py:28
  2.0 20.9 %all_to_all.10 = f32[16,40,128]{2,1,0:T(8,128)S(1)} all-to-all(f32[16,40,128]{2,1,0:T(8,128)} %shard_map.55), channel_id=1, replica_groups=mesh['grp'=32,'sub'=16] {'sub'}, dimensions={0} | all-to-all | bytes 655360 | tf_op jit(solution)/shard_map/all_to_all | solution.py:463
  22.9 0.3 shard_map.56
  23.2 0.0 collective-permute-start.1
  23.2 1.7 %collective-permute-start = (f32[2,48,256]{2,1,0:T(8,128)S(1)}, f32[2,48,256]{2,1,0:T(8,128)S(1)}, u32[]{:S(2)}, u32[]{:S(2)}) collective-permute-start(f32[2,48,256]{2,1,0:T(8,128)S(1)} %get-tuple-element.15), channel_id=1, source_target_pairs={{0,1},{1,2},{2,3},{3,4},{4,5},{5,6},{6,7},{7,8},{8,9},{9,10},{10,1... | collective-permute-start | bytes 294920 | tf_op jit(solution)/shard_map/ppermute | solution.py:444
  25.0 9.0 %all-gather = f32[10,48,256]{2,1,0:T(8,128)S(1)} all-gather(f32[5,48,256]{2,1,0:T(8,128)S(1)} %get-tuple-element.14.own_ref), channel_id=2, replica_groups={{17,33},{49,65},{81,97},{113,129},{145,161},{177,193},{209,225},{241,25..., dimensions={0}, use_global_device_ids=true | all-gather | bytes 737280 | tf_op jit(solution)/shard_map/all_gather | solution.py:465
  34.0 0.0 collective-permute-done.1.after_ref
  34.0 0.0 collective-permute-done.before_ref
  34.0 0.2 shard_map.57.mine_ref
  34.2 0.0 collective-permute-start.3
  34.3 1.7 %collective-permute-start.2 = (f32[4,48,256]{2,1,0:T(8,128)S(1)}, f32[4,48,256]{2,1,0:T(8,128)S(1)}, u32[]{:S(2)}, u32[]{:S(2)}) collective-permute-start(f32[4,48,256]{2,1,0:T(8,128)S(1)} %shard_map.57.mine_ref), channel_id=1, source_target_pairs={{0,1},{1,2},{2,3},{3,4},{4,5},{5,6},{6,7},{7,8},{8,9},{9,10},{10,1... | collective-permute-start | bytes 589832 | tf_op jit(solution)/shard_map/ppermute | solution.py:444
  36.0 3.3 %collective-permute-done.3.after_ref = f32[4,48,256]{2,1,0:T(8,128)S(1)} collective-permute-done((f32[4,48,256]{2,1,0:T(8,128)S(1)}, f32[4,48,256]{2,1,0:T(8,128)S(1)}, u32[]{:S(2)}, u32[]{:S(2)}) %collective-permute-start.3) | collective-permute-done | bytes 196640 | tf_op jit(solution)/shard_map/ppermute | solution.py:444
  39.3 0.0 collective-permute-done.2.before_ref
  39.3 0.9 %shard_map.58 = (f32[2,48,256]{2,1,0:T(8,128)S(1)}, f32[48,128]{1,0:T(8,128)S(1)}, f32[48,128]{1,0:T(8,128)S(1)}) custom-call(f32[5,48,256]{2,1,0:T(8,128)S(1)} %get-tuple-element.14.own_ref, f32[2,5,48,256]{3,2,1,0:T(8,128)S(1)} %bitcast.7, f32[4,48,256]{2,1,0:T(8,128)S(1)} %collective-permute-done.2.before_ref, ...), custom_call_target="tpu_custom_call" | custom-call | tf_op jit(solution)/shard_map/pallas_call | solution.py:28
  40.2 1.8 %all-gather.1 = f32[96,128]{1,0:T(8,128)S(1)} all-gather(f32[48,128]{1,0:T(8,128)S(1)} %get-tuple-element.20), channel_id=3, replica_groups={{0,1},{2,3},{4,5},{6,7},{8,9},{10,11},{12,13},{14,15},{16,17},{18,19},{..., dimensions={0}, use_global_device_ids=true | all-gather | bytes 73728 | tf_op jit(solution)/shard_map/all_gather | solution.py:474
  42.1 6.9 %all-gather.2 = f32[4,48,128]{2,1,0:T(8,128)S(1)} all-gather(f32[2,48,128]{2,1,0:T(8,128)S(1)} %shard_map.60.block_ref), channel_id=4, replica_groups={{17,33},{49,65},{81,97},{113,129},{145,161},{177,193},{209,225},{241,25..., dimensions={0}, use_global_device_ids=true | all-gather | bytes 147456 | tf_op jit(solution)/shard_map/all_gather | solution.py:478
  49.0 0.2 shard_map.59
  49.2 0.3 shard_map.61
  49.5 14.7 %all_to_all.11 = f32[16,24,128]{2,1,0:T(8,128)S(1)} all-to-all(f32[16,24,128]{2,1,0:T(8,128)S(1)} %bitcast.9), channel_id=1, replica_groups=mesh['grp'=32,'sub'=16] {'sub'}, dimensions={0} | all-to-all | bytes 393216 | tf_op jit(solution)/shard_map/all_to_all | solution.py:480
  64.2 1.3 %shard_map.62 = f32[4,2,16,256]{3,2,1,0:T(8,128)} custom-call(f32[384,128]{1,0:T(8,128)S(1)} %bitcast.10, f32[4,128]{1,0:T(4,128)S(1)} %get-tuple-element.21.wave_ref, f32[4,128]{1,0:T(4,128)S(1)} %get-tuple-element.22.patch_ref), custom_call_target="tpu_custom_call" | custom-call | tf_op jit(solution)/shard_map/pallas_call | solution.py:28
  (1 shorter events, 0.0 us)
Async XLA Ops:
  23.2 10.8 %collective-permute-start.1 = (f32[2,48,256]{2,1,0:T(8,128)S(1)}, f32[2,48,256]{2,1,0:T(8,128)S(1)}, u32[]{:S(2)}, u32[]{:S(2)}) collective-permute-start(f32[2,48,256]{2,1,0:T(8,128)S(1)} %get-tuple-element.15), channel_id=1, source_target_pairs={{1,0},{2,1},{3,2},{4,3},{5,4},{6,5},{7,6},{8,7},{9,8},{10,9},{11,1... | collective-permute-start | bytes 294920 | tf_op jit(solution)/shard_map/ppermute | solution.py:444
  23.2 10.8 %collective-permute-start = (f32[2,48,256]{2,1,0:T(8,128)S(1)}, f32[2,48,256]{2,1,0:T(8,128)S(1)}, u32[]{:S(2)}, u32[]{:S(2)}) collective-permute-start(f32[2,48,256]{2,1,0:T(8,128)S(1)} %get-tuple-element.15), channel_id=1, source_target_pairs={{0,1},{1,2},{2,3},{3,4},{4,5},{5,6},{6,7},{7,8},{8,9},{9,10},{10,1... | collective-permute-start | bytes 294920 | tf_op jit(solution)/shard_map/ppermute | solution.py:444
  34.2 5.1 %collective-permute-start.3 = (f32[4,48,256]{2,1,0:T(8,128)S(1)}, f32[4,48,256]{2,1,0:T(8,128)S(1)}, u32[]{:S(2)}, u32[]{:S(2)}) collective-permute-start(f32[4,48,256]{2,1,0:T(8,128)S(1)} %shard_map.57.mine_ref), channel_id=1, source_target_pairs={{1,0},{2,1},{3,2},{4,3},{5,4},{6,5},{7,6},{8,7},{9,8},{10,9},{11,1... | collective-permute-start | bytes 589832 | tf_op jit(solution)/shard_map/ppermute | solution.py:444
  34.3 5.1 %collective-permute-start.2 = (f32[4,48,256]{2,1,0:T(8,128)S(1)}, f32[4,48,256]{2,1,0:T(8,128)S(1)}, u32[]{:S(2)}, u32[]{:S(2)}) collective-permute-start(f32[4,48,256]{2,1,0:T(8,128)S(1)} %shard_map.57.mine_ref), channel_id=1, source_target_pairs={{0,1},{1,2},{2,3},{3,4},{4,5},{5,6},{6,7},{7,8},{8,9},{9,10},{10,1... | collective-permute-start | bytes 589832 | tf_op jit(solution)/shard_map/ppermute | solution.py:444

commit v4 on v3

--- a/solution.py
+++ b/solution.py
@@ -118,6 +118,23 @@
     return [halves(ref, first), halves(ref, first + 1)]
 
 
+def rows_of(ref, first):
+    return [
+        [ref[PATCHES * c : PATCHES * (c + 1), :LANES], ref[PATCHES * c : PATCHES * (c + 1), LANES:]]
+        for c in (first, first + 1)
+    ]
+
+
+def wave_row(wave):
+    return jnp.sum(jnp.where(iota(wave.shape, 0) == iota(wave.shape, 1), wave, 0.0), 0, keepdims=True)
+
+
+def wave_rows(row):
+    shape = (PATCHES, LANES)
+    own = jnp.where(iota(shape, 0) == iota(shape, 1), jnp.broadcast_to(row, shape), 0.0)
+    return jnp.broadcast_to(jnp.sum(own, 1, keepdims=True), shape)
+
+
 def choose(flag, a, b):
     return [[jnp.where(flag, x, y) for x, y in zip(p, q)] for p, q in zip(a, b)]
 
@@ -207,7 +224,7 @@
                     out_ref[s, row + 1 : row + 2, :] = cells[:, LANES:]
 
 
-def place_body(raw_ref, plane_ref, field_ref, slot_ref):
+def place_body(raw_ref, plane_ref, field_ref, slot_ref, wave_ref):
     patches = raw_ref[pl.ds(8, LIVE, stride=10), :]
     held = (patches == iota((LIVE, LANES), 1).astype(F32)).astype(F32)
     slot_ref[...] = held
@@ -217,20 +234,25 @@
     placed = select(pick, rows)
     for c in range(4):
         pair = [placed[:, CELLS * c : CELLS * c + LANES], placed[:, CELLS * c + LANES : CELLS * (c + 1)]]
-        put(plane_ref, c, pair)
+        plane_ref[PATCHES * c : PATCHES * (c + 1), :LANES] = pair[0]
+        plane_ref[PATCHES * c : PATCHES * (c + 1), LANES:] = pair[1]
         if c < 2:
             put(field_ref, c, pair)
-    put(plane_ref, 4, [placed[:, 4 * CELLS :]] * 2)
-
-
-def first_body(own_ref, before_ref, after_ref, far_ref, out_ref):
+    wave = placed[:, 4 * CELLS :]
+    wave_ref[...] = wave
+    row = jnp.broadcast_to(wave_row(wave), (8, LANES))
+    plane_ref[4 * PATCHES :, :LANES] = row
+    plane_ref[4 * PATCHES :, LANES:] = row
+
+
+def first_body(own_ref, wave_ref, before_ref, after_ref, far_ref, out_ref):
     _, s = position()
-    u = field_of(own_ref, 0)
+    u = rows_of(own_ref, 0)
     factor = open_factor()
-    v = [[x * factor for x in pair] for pair in field_of(far_ref.at[other()], 0)]
+    v = [[x * factor for x in pair] for pair in rows_of(far_ref.at[other()], 0)]
     before = choose(s == 0, v, field_of(before_ref, 0))
     after = choose(s == NS - 1, v, field_of(after_ref, 0))
-    new = smooth(u, around(u, before, after), field_of(own_ref, 2), own_ref[4, :, :LANES])
+    new = smooth(u, around(u, before, after), rows_of(own_ref, 2), wave_ref[...])
     for part in range(2):
         put(out_ref, part, new[part])
         put(out_ref, 2 + part, v[part])
@@ -252,19 +274,20 @@
     return part * 64 + (inside // (4 * EDGE) + 2) * 8 + (inside % EDGE) // 4 + 2
 
 
-def second_body(own_ref, far_ref, before_ref, after_ref, mine_ref, field_ref, sums_ref, values_ref):
+def second_body(own_ref, wave_ref, far_ref, before_ref, after_ref, mine_ref, field_ref, sums_ref, values_ref):
     _, s = position()
     first, last = s == 0, s == NS - 1
-    u = field_of(own_ref, 0)
+    u = rows_of(own_ref, 0)
     far_ref = far_ref.at[other()]
     factor = open_factor()
-    v = [[x * factor for x in pair] for pair in field_of(far_ref, 0)]
+    v = [[x * factor for x in pair] for pair in rows_of(far_ref, 0)]
     one = field_of(mine_ref, 0)
-    rights = field_of(own_ref, 2)
-    wave = own_ref[4, :, :LANES]
+    rights = rows_of(own_ref, 2)
+    wave = wave_ref[...]
+    far_wave = wave_rows(far_ref[4 * PATCHES : 4 * PATCHES + 1, :LANES])
     v_before = choose(first, u, field_of(before_ref, 2))
     v_after = choose(last, u, field_of(after_ref, 2))
-    v_one = smooth(v, around(v, v_before, v_after), field_of(far_ref, 2), far_ref[4, :, :LANES])
+    v_one = smooth(v, around(v, v_before, v_after), rows_of(far_ref, 2), far_wave)
     v_one = [[x * factor for x in pair] for pair in v_one]
     before = choose(first, v_one, field_of(before_ref, 0))
     after = choose(last, v_one, field_of(after_ref, 0))
@@ -289,8 +312,9 @@
     _, s = position()
     core = lax.axis_index("sub") % 2
     meets = ((s % 4 == 0) | (s % 4 == 3)) & (s > 0) & (s < NS - 1)
-    out_ref[0] = sums_ref[...] + jnp.where(meets, pair_ref[1 - core], 0.0)
-    out_ref[1] = pair_ref[core]
+    out_ref[...] = sums_ref[...] + (
+        jnp.where(meets, pair_ref[1 - core], 0.0) + lane_roll(pair_ref[core], 4)
+    )
 
 
 def sides(x, patch, col):
@@ -313,11 +337,11 @@
     return x + jnp.where(a < 2, lane_roll(low, -32), 0.0) + jnp.where(a >= 6, lane_roll(high, 32), 0.0)
 
 
-def slots_body(field_ref, own_ref, slot_ref, out_ref, wave_ref, patch_ref):
+def slots_body(field_ref, own_wave_ref, slot_ref, out_ref, wave_ref, patch_ref):
     _, s = position()
     rows = [half for c in range(2) for half in halves(field_ref, c)]
     out_ref[...] = select(slot_ref[:, :PATCHES], jnp.concatenate(rows, 1))
-    wave = own_ref[4, :, :LANES]
+    wave = own_wave_ref[...]
     patch, lane = iota(wave.shape, 0), iota(wave.shape, 1)
     col = patch % PZ
     a, b = (lane // 8) % 8, lane % 8
@@ -336,10 +360,11 @@
     factor = open_factor()
     far_ref = far_ref.at[other()]
     edge = jnp.where((s == 0) | (s == NS - 1), 1.0, 0.0)
-    own = windows(block_ref[0] + (edge * factor) * far_ref[1])
-    far = windows(factor * (far_ref[0] + edge * block_ref[1]))
+    block, far_block = block_ref[...], far_ref[...]
+    own = windows(block + (edge * factor) * lane_roll(far_block, -4))
+    far = windows(factor * (far_block + edge * lane_roll(block, -4)))
     patch, lane = iota(far.shape, 0), iota(far.shape, 1)
-    wave = jnp.broadcast_to(far_ref[0, :, 0:1], far.shape)
+    wave = jnp.broadcast_to(far_block[:, 0:1], far.shape)
     beside = (wave,) + sides(wave, patch, patch % PZ)
     for i, x in enumerate(beside):
         far = jnp.where(lane == i, x, far)
@@ -448,7 +473,10 @@
     (packed,) = call(
         pack_body,
         [(NS, 40, LANES)],
-        [field, source, patch_of_slot, wave_index, wave_table],
+        [
+            pltpu.with_memory_space_constraint(x, pltpu.HBM)
+            for x in (field, source, patch_of_slot, wave_index, wave_table)
+        ],
         [
             field.shape,
             source.shape,
@@ -458,23 +486,24 @@
             pltpu.SemaphoreType.DMA((5,)),
         ],
         [hbm] * 5,
-        60,
+        16,
     )
     raw = lax.all_to_all(packed, "sub", 0, 0, tiled=True).reshape(NS * 40, LANES)
-    own, start, slot = call(place_body, [(5,) + plane, (2,) + plane, (LIVE, LANES)], [raw])
+    row = (PATCHES, LANES)
+    stacked = (4 * PATCHES + 8, CELLS)
+    own, start, slot, own_wave = call(place_body, [stacked, (2,) + plane, (LIVE, LANES), row], [raw])
     far = lax.all_gather(own, both, axis_index_groups=facing(groups, 2))
     before, after = ring(start)
-    (one,) = call(first_body, [(4,) + plane], [own, before, after, far])
+    (one,) = call(first_body, [(4,) + plane], [own, own_wave, before, after, far])
     before, after = ring(one)
-    row = (PATCHES, LANES)
     two, sums, values = call(
-        second_body, [(2,) + plane, row, row], [own, far, before, after, one]
+        second_body, [(2,) + plane, row, row], [own, own_wave, far, before, after, one]
     )
     chips = [[i, i + 1] for i in range(0, NS, 2)]
     pair = lax.all_gather(values, "sub", axis_index_groups=chips)
     mine = (SLOTS, LANES)
-    sent, wave, patch = call(slots_body, [(LIVE, 2 * CELLS), mine, mine], [two, own, slot])
-    (block,) = call(join_body, [(2,) + row], [sums, pair])
+    sent, wave, patch = call(slots_body, [(LIVE, 2 * CELLS), mine, mine], [two, own_wave, slot])
+    (block,) = call(join_body, [row], [sums, pair])
     far_block = lax.all_gather(block, both, axis_index_groups=facing(groups, NS // 2))
     (bundle,) = call(bundle_body, [(LIVE * 6, LANES)], [sent, block, far_block, slot])
     back = lax.all_to_all(bundle.reshape(NS, 24, LANES), "sub", 0, 0, tiled=True)

time: 65.8 us -> 64.3 us (0.977)
  the two profiles are of different devices: /device:TPU:199 before, /device:TPU:257 now
where the time goes in v4:
time: 64.3 us; the launch traced here: 64.1 us
  blocking collectives  52.4 us (81%)
  Pallas kernels  4.69 us (7%)
  starting transfers between devices  3.5 us (5%)
  waiting for transfers between devices  3.36 us (5%)
    all_to_all x1, blocking collectives, body(): lax.all_to_all(packed, 'sub', 0, 0, tiled=True).reshape(NS * 40, LANES)  20.6 us
    all_to_all x1, blocking collectives, body(): lax.all_to_all(bundle.reshape(NS, 24, LANES), 'sub', 0, 0, tiled=True)  14.7 us
    all_gather x1, blocking collectives, body(): far = lax.all_gather(own, both, axis_index_groups=facing(groups, 2))  8.59 us
    all_gather x1, blocking collectives, body(): lax.all_gather(block, both, axis_index_groups=facing(groups, NS // 2))  6.66 us
    pallas_call x8, Pallas kernels, call(): pl.pallas_call(body, out_shape=[jax.ShapeDtypeStruct(shape, F32) for shap...  4.69 us
    ppermute x4, starting transfers between devices, body(): ring = lambda x: (lax.ppermute(x, 'sub', up), lax.ppermute(x, 'sub', down))  3.5 us
    ppermute x4, waiting for transfers between devices, body(): ring = lambda x: (lax.ppermute(x, 'sub', up), lax.ppermute(x, 'sub', down))  3.36 us
    all_gather x1, blocking collectives, body(): pair = lax.all_gather(values, 'sub', axis_index_groups=chips)  1.84 us
  transfers between devices with their start and end apart: 4, of which 1 were waited for; matrix products, arithmetic and copies ran while one was open for 0% of the time, Pallas kernels for 0%

profile of v4, /device:TPU:257, one launch (start us, length us, event | category | flops | bytes accessed | tf_op | source)
XLA Modules:
  0.0 64.1 jit_solution(11787232678409093655)
XLA Ops:
  0.0 1.3 %shard_map.55 = f32[16,40,128]{2,1,0:T(8,128)S(1)} custom-call(f32[4,2,16,256]{3,2,1,0:T(8,128)} %field_hbm.1, f32[4,2,16,256]{3,2,1,0:T(8,128)} %source_hbm.1, s32[4]{0:T(128)} %patch_hbm.1, s32[4]{0:T(128)} %index_hbm.1, f32[16]{0:T(128)} %table_hbm.1), custom_call_target="tpu_custom_call" | custom-call | tf_op jit(solution)/shard_map/pallas_call | solution.py:28
  1.3 20.6 %all_to_all.10 = f32[16,40,128]{2,1,0:T(8,128)S(1)} all-to-all(f32[16,40,128]{2,1,0:T(8,128)S(1)} %shard_map.55), channel_id=1, replica_groups=mesh['grp'=32,'sub'=16] {'sub'}, dimensions={0} | all-to-all | bytes 655360 | tf_op jit(solution)/shard_map/all_to_all | solution.py:491
  21.9 0.3 shard_map.56
  22.3 0.0 collective-permute-start.1
  22.3 1.7 %collective-permute-start = (f32[2,48,256]{2,1,0:T(8,128)S(1)}, f32[2,48,256]{2,1,0:T(8,128)S(1)}, u32[]{:S(2)}, u32[]{:S(2)}) collective-permute-start(f32[2,48,256]{2,1,0:T(8,128)S(1)} %get-tuple-element.17), channel_id=1, source_target_pairs={{0,1},{1,2},{2,3},{3,4},{4,5},{5,6},{6,7},{7,8},{8,9},{9,10},{10,1... | collective-permute-start | bytes 294920 | tf_op jit(solution)/shard_map/ppermute | solution.py:469
  24.0 8.6 %all-gather = f32[400,256]{1,0:T(8,128)S(1)} all-gather(f32[200,256]{1,0:T(8,128)S(1)} %get-tuple-element.15.own_ref), channel_id=2, replica_groups={{17,33},{49,65},{81,97},{113,129},{145,161},{177,193},{209,225},{241,25..., dimensions={0}, use_global_device_ids=true | all-gather | bytes 614400 | tf_op jit(solution)/shard_map/all_gather | solution.py:495
  32.6 0.0 collective-permute-done.1.after_ref
  32.6 0.0 collective-permute-done.before_ref
  32.6 0.2 shard_map.57.mine_ref
  32.9 0.0 collective-permute-start.3
  32.9 1.7 %collective-permute-start.2 = (f32[4,48,256]{2,1,0:T(8,128)S(1)}, f32[4,48,256]{2,1,0:T(8,128)S(1)}, u32[]{:S(2)}, u32[]{:S(2)}) collective-permute-start(f32[4,48,256]{2,1,0:T(8,128)S(1)} %shard_map.57.mine_ref), channel_id=1, source_target_pairs={{0,1},{1,2},{2,3},{3,4},{4,5},{5,6},{6,7},{7,8},{8,9},{9,10},{10,1... | collective-permute-start | bytes 589832 | tf_op jit(solution)/shard_map/ppermute | solution.py:469
  34.6 3.3 %collective-permute-done.3.after_ref = f32[4,48,256]{2,1,0:T(8,128)S(1)} collective-permute-done((f32[4,48,256]{2,1,0:T(8,128)S(1)}, f32[4,48,256]{2,1,0:T(8,128)S(1)}, u32[]{:S(2)}, u32[]{:S(2)}) %collective-permute-start.3) | collective-permute-done | bytes 196640 | tf_op jit(solution)/shard_map/ppermute | solution.py:469
  38.0 0.0 collective-permute-done.2.before_ref
  38.0 0.9 %shard_map.58 = (f32[2,48,256]{2,1,0:T(8,128)S(1)}, f32[48,128]{1,0:T(8,128)S(1)}, f32[48,128]{1,0:T(8,128)S(1)}) custom-call(f32[200,256]{1,0:T(8,128)S(1)} %get-tuple-element.15.own_ref, f32[48,128]{1,0:T(8,128)S(1)} %get-tuple-element.16.wave_ref.own_wave_ref, f32[2,200,256]{2,1,0:T(8,128)S(1)} %bitcast.7, ...), custom_call_target="tpu_custom_call" | custom-call | tf_op jit(solution)/shard_map/pallas_call | solution.py:28
  38.8 1.8 %all-gather.1 = f32[96,128]{1,0:T(8,128)S(1)} all-gather(f32[48,128]{1,0:T(8,128)S(1)} %get-tuple-element.22), channel_id=3, replica_groups={{0,1},{2,3},{4,5},{6,7},{8,9},{10,11},{12,13},{14,15},{16,17},{18,19},{..., dimensions={0}, use_global_device_ids=true | all-gather | bytes 73728 | tf_op jit(solution)/shard_map/all_gather | solution.py:503
  40.7 0.1 shard_map.60.block_ref
  40.8 6.7 %all-gather.2 = f32[96,128]{1,0:T(8,128)S(1)} all-gather(f32[48,128]{1,0:T(8,128)S(1)} %shard_map.60.block_ref), channel_id=4, replica_groups={{17,33},{49,65},{81,97},{113,129},{145,161},{177,193},{209,225},{241,25..., dimensions={0}, use_global_device_ids=true | all-gather | bytes 73728 | tf_op jit(solution)/shard_map/all_gather | solution.py:507
  47.4 0.2 shard_map.59
  47.6 0.4 shard_map.61
  48.0 14.7 %all_to_all.11 = f32[16,24,128]{2,1,0:T(8,128)S(1)} all-to-all(f32[16,24,128]{2,1,0:T(8,128)S(1)} %bitcast.9), channel_id=1, replica_groups=mesh['grp'=32,'sub'=16] {'sub'}, dimensions={0} | all-to-all | bytes 393216 | tf_op jit(solution)/shard_map/all_to_all | solution.py:509
  62.7 1.3 %shard_map.62 = f32[4,2,16,256]{3,2,1,0:T(8,128)} custom-call(f32[384,128]{1,0:T(8,128)S(1)} %bitcast.10, f32[4,128]{1,0:T(4,128)S(1)} %get-tuple-element.23.wave_ref, f32[4,128]{1,0:T(4,128)S(1)} %get-tuple-element.24.patch_ref), custom_call_target="tpu_custom_call" | custom-call | tf_op jit(solution)/shard_map/pallas_call | solution.py:28
Async XLA Ops:
  22.3 10.4 %collective-permute-start.1 = (f32[2,48,256]{2,1,0:T(8,128)S(1)}, f32[2,48,256]{2,1,0:T(8,128)S(1)}, u32[]{:S(2)}, u32[]{:S(2)}) collective-permute-start(f32[2,48,256]{2,1,0:T(8,128)S(1)} %get-tuple-element.17), channel_id=1, source_target_pairs={{1,0},{2,1},{3,2},{4,3},{5,4},{6,5},{7,6},{8,7},{9,8},{10,9},{11,1... | collective-permute-start | bytes 294920 | tf_op jit(solution)/shard_map/ppermute | solution.py:469
  22.3 10.3 %collective-permute-start = (f32[2,48,256]{2,1,0:T(8,128)S(1)}, f32[2,48,256]{2,1,0:T(8,128)S(1)}, u32[]{:S(2)}, u32[]{:S(2)}) collective-permute-start(f32[2,48,256]{2,1,0:T(8,128)S(1)} %get-tuple-element.17), channel_id=1, source_target_pairs={{0,1},{1,2},{2,3},{3,4},{4,5},{5,6},{6,7},{7,8},{8,9},{9,10},{10,1... | collective-permute-start | bytes 294920 | tf_op jit(solution)/shard_map/ppermute | solution.py:469
  32.9 5.1 %collective-permute-start.3 = (f32[4,48,256]{2,1,0:T(8,128)S(1)}, f32[4,48,256]{2,1,0:T(8,128)S(1)}, u32[]{:S(2)}, u32[]{:S(2)}) collective-permute-start(f32[4,48,256]{2,1,0:T(8,128)S(1)} %shard_map.57.mine_ref), channel_id=1, source_target_pairs={{1,0},{2,1},{3,2},{4,3},{5,4},{6,5},{7,6},{8,7},{9,8},{10,9},{11,1... | collective-permute-start | bytes 589832 | tf_op jit(solution)/shard_map/ppermute | solution.py:469
  32.9 5.1 %collective-permute-start.2 = (f32[4,48,256]{2,1,0:T(8,128)S(1)}, f32[4,48,256]{2,1,0:T(8,128)S(1)}, u32[]{:S(2)}, u32[]{:S(2)}) collective-permute-start(f32[4,48,256]{2,1,0:T(8,128)S(1)} %shard_map.57.mine_ref), channel_id=1, source_target_pairs={{0,1},{1,2},{2,3},{3,4},{4,5},{5,6},{6,7},{7,8},{8,9},{9,10},{10,1... | collective-permute-start | bytes 589832 | tf_op jit(solution)/shard_map/ppermute | solution.py:469

commit v5 on v4

--- a/solution.py
+++ b/solution.py
@@ -245,7 +245,7 @@
     plane_ref[4 * PATCHES :, LANES:] = row
 
 
-def first_body(own_ref, wave_ref, before_ref, after_ref, far_ref, out_ref):
+def first_body(own_ref, wave_ref, before_ref, after_ref, far_ref, out_ref, up_ref, down_ref):
     _, s = position()
     u = rows_of(own_ref, 0)
     factor = open_factor()
@@ -253,9 +253,17 @@
     before = choose(s == 0, v, field_of(before_ref, 0))
     after = choose(s == NS - 1, v, field_of(after_ref, 0))
     new = smooth(u, around(u, before, after), rows_of(own_ref, 2), wave_ref[...])
+    real, imag = diagonal(wave_rows(far_ref[other(), 4 * PATCHES : 4 * PATCHES + 1, :LANES]))
+    scale = omega_fine / (real * real + imag * imag)
+    real, imag = real * scale, imag * scale
+    more = [
+        [a * real - b * imag for a, b in zip(v[0], v[1])],
+        [a * imag + b * real for a, b in zip(v[0], v[1])],
+    ]
     for part in range(2):
         put(out_ref, part, new[part])
-        put(out_ref, 2 + part, v[part])
+        put(up_ref, part, [x + jnp.where(s == NS - 2, y, 0.0) for x, y in zip(new[part], more[part])])
+        put(down_ref, part, [x + jnp.where(s == 1, y, 0.0) for x, y in zip(new[part], more[part])])
 
 
 def other():
@@ -285,9 +293,7 @@
     rights = rows_of(own_ref, 2)
     wave = wave_ref[...]
     far_wave = wave_rows(far_ref[4 * PATCHES : 4 * PATCHES + 1, :LANES])
-    v_before = choose(first, u, field_of(before_ref, 2))
-    v_after = choose(last, u, field_of(after_ref, 2))
-    v_one = smooth(v, around(v, v_before, v_after), rows_of(far_ref, 2), far_wave)
+    v_one = smooth(v, [[x + y for x, y in zip(in_plane(p), q)] for p, q in zip(v, u)], rows_of(far_ref, 2), far_wave)
     v_one = [[x * factor for x in pair] for pair in v_one]
     before = choose(first, v_one, field_of(before_ref, 0))
     after = choose(last, v_one, field_of(after_ref, 0))
@@ -494,8 +500,11 @@
     own, start, slot, own_wave = call(place_body, [stacked, (2,) + plane, (LIVE, LANES), row], [raw])
     far = lax.all_gather(own, both, axis_index_groups=facing(groups, 2))
     before, after = ring(start)
-    (one,) = call(first_body, [(4,) + plane], [own, own_wave, before, after, far])
-    before, after = ring(one)
+    one, rising, falling = call(
+        first_body, [(2,) + plane] * 3, [own, own_wave, before, after, far]
+    )
+    before = lax.ppermute(rising, "sub", up)
+    after = lax.ppermute(falling, "sub", down)
     two, sums, values = call(
         second_body, [(2,) + plane, row, row], [own, own_wave, far, before, after, one]
     )

time: 64.3 us -> 62.9 us (0.978)
  the two profiles are of different devices: /device:TPU:257 before, /device:TPU:1 now
where the time goes in v5:
time: 62.9 us; the launch traced here: 62.7 us
  blocking collectives  52.1 us (83%)
  Pallas kernels  4.73 us (8%)
  waiting for transfers between devices  3.56 us (6%)
  starting transfers between devices  2.27 us (4%)
    all_to_all x1, blocking collectives, body(): lax.all_to_all(packed, 'sub', 0, 0, tiled=True).reshape(NS * 40, LANES)  22.3 us
    all_to_all x1, blocking collectives, body(): lax.all_to_all(bundle.reshape(NS, 24, LANES), 'sub', 0, 0, tiled=True)  13 us
    all_gather x1, blocking collectives, body(): lax.all_gather(block, both, axis_index_groups=facing(groups, NS // 2))  7.83 us
    all_gather x1, blocking collectives, body(): far = lax.all_gather(own, both, axis_index_groups=facing(groups, 2))  7.06 us
    pallas_call x8, Pallas kernels, call(): pl.pallas_call(body, out_shape=[jax.ShapeDtypeStruct(shape, F32) for shap...  4.73 us
    ppermute x1, waiting for transfers between devices, body(): after = lax.ppermute(falling, 'sub', down)  2.42 us
    all_gather x1, blocking collectives, body(): pair = lax.all_gather(values, 'sub', axis_index_groups=chips)  1.84 us
    ppermute x2, starting transfers between devices, body(): ring = lambda x: (lax.ppermute(x, 'sub', up), lax.ppermute(x, 'sub', down))  1.75 us
  transfers between devices with their start and end apart: 4, of which 2 were waited for; matrix products, arithmetic and copies ran while one was open for 0% of the time, Pallas kernels for 0%

profile of v5, /device:TPU:1, one launch (start us, length us, event | category | flops | bytes accessed | tf_op | source)
XLA Modules:
  0.0 62.7 jit_solution(10973181589713472857)
XLA Ops:
  0.0 1.3 %shard_map.55 = f32[16,40,128]{2,1,0:T(8,128)S(1)} custom-call(f32[4,2,16,256]{3,2,1,0:T(8,128)} %field_hbm.1, f32[4,2,16,256]{3,2,1,0:T(8,128)} %source_hbm.1, s32[4]{0:T(128)} %patch_hbm.1, s32[4]{0:T(128)} %index_hbm.1, f32[16]{0:T(128)} %table_hbm.1), custom_call_target="tpu_custom_call" | custom-call | tf_op jit(solution)/shard_map/pallas_call | solution.py:28
  1.3 22.3 %all_to_all.10 = f32[16,40,128]{2,1,0:T(8,128)S(1)} all-to-all(f32[16,40,128]{2,1,0:T(8,128)S(1)} %shard_map.55), channel_id=1, replica_groups=mesh['grp'=32,'sub'=16] {'sub'}, dimensions={0} | all-to-all | bytes 655360 | tf_op jit(solution)/shard_map/all_to_all | solution.py:497
  23.6 0.3 shard_map.56
  23.9 0.0 collective-permute-start.1
  24.0 1.7 %collective-permute-start = (f32[2,48,256]{2,1,0:T(8,128)S(1)}, f32[2,48,256]{2,1,0:T(8,128)S(1)}, u32[]{:S(2)}, u32[]{:S(2)}) collective-permute-start(f32[2,48,256]{2,1,0:T(8,128)S(1)} %get-tuple-element.20), channel_id=1, source_target_pairs={{0,1},{1,2},{2,3},{3,4},{4,5},{5,6},{6,7},{7,8},{8,9},{9,10},{10,1... | collective-permute-start | bytes 294920 | tf_op jit(solution)/shard_map/ppermute | solution.py:475
  25.7 7.1 %all-gather = f32[400,256]{1,0:T(8,128)S(1)} all-gather(f32[200,256]{1,0:T(8,128)S(1)} %get-tuple-element.18.own_ref), channel_id=2, replica_groups={{17,33},{49,65},{81,97},{113,129},{145,161},{177,193},{209,225},{241,25..., dimensions={0}, use_global_device_ids=true | all-gather | bytes 614400 | tf_op jit(solution)/shard_map/all_gather | solution.py:501
  32.8 0.0 collective-permute-done.1.after_ref
  32.8 0.0 collective-permute-done.before_ref
  32.8 0.3 shard_map.57
  33.0 0.0 collective-permute-start.2
  33.1 0.5 collective-permute-start.3
  33.6 1.1 %collective-permute-done.2.before_ref = f32[2,48,256]{2,1,0:T(8,128)S(1)} collective-permute-done((f32[2,48,256]{2,1,0:T(8,128)S(1)}, f32[2,48,256]{2,1,0:T(8,128)S(1)}, u32[]{:S(2)}, u32[]{:S(2)}) %collective-permute-start.2) | collective-permute-done | bytes 98336 | tf_op jit(solution)/shard_map/ppermute | solution.py:506
  34.7 2.4 %collective-permute-done.3.after_ref = f32[2,48,256]{2,1,0:T(8,128)S(1)} collective-permute-done((f32[2,48,256]{2,1,0:T(8,128)S(1)}, f32[2,48,256]{2,1,0:T(8,128)S(1)}, u32[]{:S(2)}, u32[]{:S(2)}) %collective-permute-start.3) | collective-permute-done | bytes 98336 | tf_op jit(solution)/shard_map/ppermute | solution.py:507
  37.1 0.9 %shard_map.58 = (f32[2,48,256]{2,1,0:T(8,128)S(1)}, f32[48,128]{1,0:T(8,128)S(1)}, f32[48,128]{1,0:T(8,128)S(1)}) custom-call(f32[200,256]{1,0:T(8,128)S(1)} %get-tuple-element.18.own_ref, f32[48,128]{1,0:T(8,128)S(1)} %get-tuple-element.19.wave_ref.own_wave_ref, f32[2,200,256]{2,1,0:T(8,128)S(1)} %bitcast.7, ...), custom_call_target="tpu_custom_call" | custom-call | tf_op jit(solution)/shard_map/pallas_call | solution.py:28
  38.0 1.8 %all-gather.1 = f32[96,128]{1,0:T(8,128)S(1)} all-gather(f32[48,128]{1,0:T(8,128)S(1)} %get-tuple-element.28), channel_id=3, replica_groups={{0,1},{2,3},{4,5},{6,7},{8,9},{10,11},{12,13},{14,15},{16,17},{18,19},{..., dimensions={0}, use_global_device_ids=true | all-gather | bytes 73728 | tf_op jit(solution)/shard_map/all_gather | solution.py:512
  39.8 0.1 shard_map.60.block_ref
  39.9 7.8 %all-gather.2 = f32[96,128]{1,0:T(8,128)S(1)} all-gather(f32[48,128]{1,0:T(8,128)S(1)} %shard_map.60.block_ref), channel_id=4, replica_groups={{17,33},{49,65},{81,97},{113,129},{145,161},{177,193},{209,225},{241,25..., dimensions={0}, use_global_device_ids=true | all-gather | bytes 73728 | tf_op jit(solution)/shard_map/all_gather | solution.py:516
  47.7 0.2 shard_map.59
  47.9 0.4 shard_map.61
  48.3 13.0 %all_to_all.11 = f32[16,24,128]{2,1,0:T(8,128)S(1)} all-to-all(f32[16,24,128]{2,1,0:T(8,128)S(1)} %bitcast.9), channel_id=1, replica_groups=mesh['grp'=32,'sub'=16] {'sub'}, dimensions={0} | all-to-all | bytes 393216 | tf_op jit(solution)/shard_map/all_to_all | solution.py:518
  61.4 1.3 %shard_map.62 = f32[4,2,16,256]{3,2,1,0:T(8,128)} custom-call(f32[384,128]{1,0:T(8,128)S(1)} %bitcast.10, f32[4,128]{1,0:T(4,128)S(1)} %get-tuple-element.29.wave_ref, f32[4,128]{1,0:T(4,128)S(1)} %get-tuple-element.30.patch_ref), custom_call_target="tpu_custom_call" | custom-call | tf_op jit(solution)/shard_map/pallas_call | solution.py:28
Async XLA Ops:
  23.9 8.8 %collective-permute-start.1 = (f32[2,48,256]{2,1,0:T(8,128)S(1)}, f32[2,48,256]{2,1,0:T(8,128)S(1)}, u32[]{:S(2)}, u32[]{:S(2)}) collective-permute-start(f32[2,48,256]{2,1,0:T(8,128)S(1)} %get-tuple-element.20), channel_id=1, source_target_pairs={{1,0},{2,1},{3,2},{4,3},{5,4},{6,5},{7,6},{8,7},{9,8},{10,9},{11,1... | collective-permute-start | bytes 294920 | tf_op jit(solution)/shard_map/ppermute | solution.py:475
  24.0 8.8 %collective-permute-start = (f32[2,48,256]{2,1,0:T(8,128)S(1)}, f32[2,48,256]{2,1,0:T(8,128)S(1)}, u32[]{:S(2)}, u32[]{:S(2)}) collective-permute-start(f32[2,48,256]{2,1,0:T(8,128)S(1)} %get-tuple-element.20), channel_id=1, source_target_pairs={{0,1},{1,2},{2,3},{3,4},{4,5},{5,6},{6,7},{7,8},{8,9},{9,10},{10,1... | collective-permute-start | bytes 294920 | tf_op jit(solution)/shard_map/ppermute | solution.py:475
  33.0 1.7 %collective-permute-start.2 = (f32[2,48,256]{2,1,0:T(8,128)S(1)}, f32[2,48,256]{2,1,0:T(8,128)S(1)}, u32[]{:S(2)}, u32[]{:S(2)}) collective-permute-start(f32[2,48,256]{2,1,0:T(8,128)S(1)} %get-tuple-element.21), channel_id=1, source_target_pairs={{0,1},{1,2},{2,3},{3,4},{4,5},{5,6},{6,7},{7,8},{8,9},{9,10},{10,1... | collective-permute-start | bytes 294920 | tf_op jit(solution)/shard_map/ppermute | solution.py:506
  33.1 4.1 %collective-permute-start.3 = (f32[2,48,256]{2,1,0:T(8,128)S(1)}, f32[2,48,256]{2,1,0:T(8,128)S(1)}, u32[]{:S(2)}, u32[]{:S(2)}) collective-permute-start(f32[2,48,256]{2,1,0:T(8,128)S(1)} %get-tuple-element.22), channel_id=1, source_target_pairs={{1,0},{2,1},{3,2},{4,3},{5,4},{6,5},{7,6},{8,7},{9,8},{10,9},{11,1... | collective-permute-start | bytes 294920 | tf_op jit(solution)/shard_map/ppermute | solution.py:507

commit v6 on v5

--- a/solution.py
+++ b/solution.py
@@ -314,13 +314,8 @@
     values_ref[...] = values
 
 
-def join_body(sums_ref, pair_ref, out_ref):
-    _, s = position()
-    core = lax.axis_index("sub") % 2
-    meets = ((s % 4 == 0) | (s % 4 == 3)) & (s > 0) & (s < NS - 1)
-    out_ref[...] = sums_ref[...] + (
-        jnp.where(meets, pair_ref[1 - core], 0.0) + lane_roll(pair_ref[core], 4)
-    )
+def join_body(sums_ref, values_ref, pair_ref, out_ref):
+    out_ref[...] = sums_ref[...] + (pair_ref[...] + lane_roll(values_ref[...], 4))
 
 
 def sides(x, patch, col):
@@ -460,8 +455,8 @@
             met.update(pairs[-1])
     for g in range(groups):
         rest = [g * NS + s for s in range(NS) if g * NS + s not in met]
-        whole = [i for i in rest if i ^ 1 in rest]
-        rest = [i for i in rest if i ^ 1 not in rest]
+        whole = [i for i in rest if i ^ 1 in rest and 2 * reach < NS]
+        rest = [i for i in rest if i not in whole]
         pairs += [whole[i : i + 2] for i in range(0, len(whole), 2)]
         pairs += [rest[i : i + 2] for i in range(0, len(rest), 2)]
     return pairs
@@ -508,11 +503,11 @@
     two, sums, values = call(
         second_body, [(2,) + plane, row, row], [own, own_wave, far, before, after, one]
     )
-    chips = [[i, i + 1] for i in range(0, NS, 2)]
-    pair = lax.all_gather(values, "sub", axis_index_groups=chips)
+    edges = [device_at(4 * i + 3) for i in range(NS // 4 - 1)]
+    pair = lax.ppermute(values, "sub", [(i, i + 1) for i in edges] + [(i + 1, i) for i in edges])
     mine = (SLOTS, LANES)
     sent, wave, patch = call(slots_body, [(LIVE, 2 * CELLS), mine, mine], [two, own_wave, slot])
-    (block,) = call(join_body, [row], [sums, pair])
+    (block,) = call(join_body, [row], [sums, values, pair])
     far_block = lax.all_gather(block, both, axis_index_groups=facing(groups, NS // 2))
     (bundle,) = call(bundle_body, [(LIVE * 6, LANES)], [sent, block, far_block, slot])
     back = lax.all_to_all(bundle.reshape(NS, 24, LANES), "sub", 0, 0, tiled=True)

time: 62.9 us -> 62.2 us (0.989)
  the two profiles are of different devices: /device:TPU:1 before, /device:TPU:199 now
where the time goes in v6:
time: 62.2 us; the launch traced here: 62 us
  blocking collectives  49.6 us (80%)
  Pallas kernels  4.74 us (8%)
  waiting for transfers between devices  4.05 us (7%)
  starting transfers between devices  3.58 us (6%)
    all_to_all x1, blocking collectives, body(): lax.all_to_all(packed, 'sub', 0, 0, tiled=True).reshape(NS * 40, LANES)  20.6 us
    all_to_all x1, blocking collectives, body(): lax.all_to_all(bundle.reshape(NS, 24, LANES), 'sub', 0, 0, tiled=True)  13.7 us
    all_gather x1, blocking collectives, body(): far = lax.all_gather(own, both, axis_index_groups=facing(groups, 2))  8.59 us
    all_gather x1, blocking collectives, body(): lax.all_gather(block, both, axis_index_groups=facing(groups, NS // 2))  6.66 us
    pallas_call x8, Pallas kernels, call(): pl.pallas_call(body, out_shape=[jax.ShapeDtypeStruct(shape, F32) for shap...  4.74 us
    ppermute x1, waiting for transfers between devices, body(): after = lax.ppermute(falling, 'sub', down)  2.4 us
    ppermute x2, starting transfers between devices, body(): ring = lambda x: (lax.ppermute(x, 'sub', up), lax.ppermute(x, 'sub', down))  1.75 us
    ppermute x1, waiting for transfers between devices, body(): before = lax.ppermute(rising, 'sub', up)  1.64 us
  transfers between devices with their start and end apart: 5, of which 2 were waited for; matrix products, arithmetic and copies ran while one was open for 0% of the time, Pallas kernels for 0%

profile of v6, /device:TPU:199, one launch (start us, length us, event | category | flops | bytes accessed | tf_op | source)
XLA Modules:
  0.0 62.0 jit_solution(5267984941153585601)
XLA Ops:
  0.0 1.3 %shard_map.55 = f32[16,40,128]{2,1,0:T(8,128)S(1)} custom-call(f32[4,2,16,256]{3,2,1,0:T(8,128)} %field_hbm.1, f32[4,2,16,256]{3,2,1,0:T(8,128)} %source_hbm.1, s32[4]{0:T(128)} %patch_hbm.1, s32[4]{0:T(128)} %index_hbm.1, f32[16]{0:T(128)} %table_hbm.1), custom_call_target="tpu_custom_call" | custom-call | tf_op jit(solution)/shard_map/pallas_call | solution.py:28
  1.3 20.6 %all_to_all.10 = f32[16,40,128]{2,1,0:T(8,128)S(1)} all-to-all(f32[16,40,128]{2,1,0:T(8,128)S(1)} %shard_map.55), channel_id=1, replica_groups=mesh['grp'=32,'sub'=16] {'sub'}, dimensions={0} | all-to-all | bytes 655360 | tf_op jit(solution)/shard_map/all_to_all | solution.py:492
  21.9 0.3 shard_map.56
  22.2 0.0 collective-permute-start.1
  22.3 1.7 %collective-permute-start = (f32[2,48,256]{2,1,0:T(8,128)S(1)}, f32[2,48,256]{2,1,0:T(8,128)S(1)}, u32[]{:S(2)}, u32[]{:S(2)}) collective-permute-start(f32[2,48,256]{2,1,0:T(8,128)S(1)} %get-tuple-element.20), channel_id=1, source_target_pairs={{0,1},{1,2},{2,3},{3,4},{4,5},{5,6},{6,7},{7,8},{8,9},{9,10},{10,1... | collective-permute-start | bytes 294920 | tf_op jit(solution)/shard_map/ppermute | solution.py:470
  24.0 8.6 %all-gather = f32[400,256]{1,0:T(8,128)S(1)} all-gather(f32[200,256]{1,0:T(8,128)S(1)} %get-tuple-element.18.own_ref), channel_id=2, replica_groups={{17,33},{49,65},{81,97},{113,129},{145,161},{177,193},{209,225},{241,25..., dimensions={0}, use_global_device_ids=true | all-gather | bytes 614400 | tf_op jit(solution)/shard_map/all_gather | solution.py:496
  32.6 0.0 collective-permute-done.1.after_ref
  32.6 0.0 collective-permute-done.before_ref
  32.6 0.3 shard_map.57
  32.9 1.2 %collective-permute-start.2 = (f32[2,48,256]{2,1,0:T(8,128)S(1)}, f32[2,48,256]{2,1,0:T(8,128)S(1)}, u32[]{:S(2)}, u32[]{:S(2)}) collective-permute-start(f32[2,48,256]{2,1,0:T(8,128)S(1)} %get-tuple-element.21), channel_id=1, source_target_pairs={{0,1},{1,2},{2,3},{3,4},{4,5},{5,6},{6,7},{7,8},{8,9},{9,10},{10,1... | collective-permute-start | bytes 294920 | tf_op jit(solution)/shard_map/ppermute | solution.py:501
  34.1 0.0 collective-permute-start.3
  34.1 1.6 %collective-permute-done.2.before_ref = f32[2,48,256]{2,1,0:T(8,128)S(1)} collective-permute-done((f32[2,48,256]{2,1,0:T(8,128)S(1)}, f32[2,48,256]{2,1,0:T(8,128)S(1)}, u32[]{:S(2)}, u32[]{:S(2)}) %collective-permute-start.2) | collective-permute-done | bytes 98336 | tf_op jit(solution)/shard_map/ppermute | solution.py:501
  35.7 2.4 %collective-permute-done.3.after_ref = f32[2,48,256]{2,1,0:T(8,128)S(1)} collective-permute-done((f32[2,48,256]{2,1,0:T(8,128)S(1)}, f32[2,48,256]{2,1,0:T(8,128)S(1)}, u32[]{:S(2)}, u32[]{:S(2)}) %collective-permute-start.3) | collective-permute-done | bytes 98336 | tf_op jit(solution)/shard_map/ppermute | solution.py:502
  38.1 0.9 %shard_map.58 = (f32[2,48,256]{2,1,0:T(8,128)S(1)}, f32[48,128]{1,0:T(8,128)S(1)}, f32[48,128]{1,0:T(8,128)S(1)}) custom-call(f32[200,256]{1,0:T(8,128)S(1)} %get-tuple-element.18.own_ref, f32[48,128]{1,0:T(8,128)S(1)} %get-tuple-element.19.wave_ref.own_wave_ref, f32[2,200,256]{2,1,0:T(8,128)S(1)} %bitcast.6, ...), custom_call_target="tpu_custom_call" | custom-call | tf_op jit(solution)/shard_map/pallas_call | solution.py:28
  39.0 0.7 %collective-permute-start.4 = (f32[48,128]{1,0:T(8,128)S(1)}, f32[48,128]{1,0:T(8,128)S(1)}, u32[]{:S(2)}, u32[]{:S(2)}) collective-permute-start(f32[48,128]{1,0:T(8,128)S(1)} %get-tuple-element.28.values_ref), channel_id=1, source_target_pairs={{4,5},{8,9},{12,13},{5,4},{9,8},{13,12},{20,21},{24,25},{28,29},{2... | collective-permute-start | bytes 73736 | tf_op jit(solution)/shard_map/ppermute | solution.py:507
  39.7 0.2 shard_map.59
  39.9 0.0 collective-permute-done.4.pair_ref
  39.9 0.1 shard_map.60.block_ref
  39.9 6.7 %all-gather.1 = f32[96,128]{1,0:T(8,128)S(1)} all-gather(f32[48,128]{1,0:T(8,128)S(1)} %shard_map.60.block_ref), channel_id=3, replica_groups={{17,33},{49,65},{81,97},{113,129},{145,161},{177,193},{209,225},{241,25..., dimensions={0}, use_global_device_ids=true | all-gather | bytes 73728 | tf_op jit(solution)/shard_map/all_gather | solution.py:511
  46.6 0.4 shard_map.61
  47.0 13.7 %all_to_all.11 = f32[16,24,128]{2,1,0:T(8,128)S(1)} all-to-all(f32[16,24,128]{2,1,0:T(8,128)S(1)} %bitcast.8), channel_id=1, replica_groups=mesh['grp'=32,'sub'=16] {'sub'}, dimensions={0} | all-to-all | bytes 393216 | tf_op jit(solution)/shard_map/all_to_all | solution.py:513
  60.7 1.3 %shard_map.62 = f32[4,2,16,256]{3,2,1,0:T(8,128)} custom-call(f32[384,128]{1,0:T(8,128)S(1)} %bitcast.9, f32[4,128]{1,0:T(4,128)S(1)} %get-tuple-element.29.wave_ref, f32[4,128]{1,0:T(4,128)S(1)} %get-tuple-element.30.patch_ref), custom_call_target="tpu_custom_call" | custom-call | tf_op jit(solution)/shard_map/pallas_call | solution.py:28
Async XLA Ops:
  22.2 10.4 %collective-permute-start.1 = (f32[2,48,256]{2,1,0:T(8,128)S(1)}, f32[2,48,256]{2,1,0:T(8,128)S(1)}, u32[]{:S(2)}, u32[]{:S(2)}) collective-permute-start(f32[2,48,256]{2,1,0:T(8,128)S(1)} %get-tuple-element.20), channel_id=1, source_target_pairs={{1,0},{2,1},{3,2},{4,3},{5,4},{6,5},{7,6},{8,7},{9,8},{10,9},{11,1... | collective-permute-start | bytes 294920 | tf_op jit(solution)/shard_map/ppermute | solution.py:470
  22.3 10.3 %collective-permute-start = (f32[2,48,256]{2,1,0:T(8,128)S(1)}, f32[2,48,256]{2,1,0:T(8,128)S(1)}, u32[]{:S(2)}, u32[]{:S(2)}) collective-permute-start(f32[2,48,256]{2,1,0:T(8,128)S(1)} %get-tuple-element.20), channel_id=1, source_target_pairs={{0,1},{1,2},{2,3},{3,4},{4,5},{5,6},{6,7},{7,8},{8,9},{9,10},{10,1... | collective-permute-start | bytes 294920 | tf_op jit(solution)/shard_map/ppermute | solution.py:470
  32.9 2.8 %collective-permute-start.2 = (f32[2,48,256]{2,1,0:T(8,128)S(1)}, f32[2,48,256]{2,1,0:T(8,128)S(1)}, u32[]{:S(2)}, u32[]{:S(2)}) collective-permute-start(f32[2,48,256]{2,1,0:T(8,128)S(1)} %get-tuple-element.21), channel_id=1, source_target_pairs={{0,1},{1,2},{2,3},{3,4},{4,5},{5,6},{6,7},{7,8},{8,9},{9,10},{10,1... | collective-permute-start | bytes 294920 | tf_op jit(solution)/shard_map/ppermute | solution.py:501
  34.1 4.0 %collective-permute-start.3 = (f32[2,48,256]{2,1,0:T(8,128)S(1)}, f32[2,48,256]{2,1,0:T(8,128)S(1)}, u32[]{:S(2)}, u32[]{:S(2)}) collective-permute-start(f32[2,48,256]{2,1,0:T(8,128)S(1)} %get-tuple-element.22), channel_id=1, source_target_pairs={{1,0},{2,1},{3,2},{4,3},{5,4},{6,5},{7,6},{8,7},{9,8},{10,9},{11,1... | collective-permute-start | bytes 294920 | tf_op jit(solution)/shard_map/ppermute | solution.py:502
  39.0 0.9 %collective-permute-start.4 = (f32[48,128]{1,0:T(8,128)S(1)}, f32[48,128]{1,0:T(8,128)S(1)}, u32[]{:S(2)}, u32[]{:S(2)}) collective-permute-start(f32[48,128]{1,0:T(8,128)S(1)} %get-tuple-element.28.values_ref), channel_id=1, source_target_pairs={{4,5},{8,9},{12,13},{5,4},{9,8},{13,12},{20,21},{24,25},{28,29},{2... | collective-permute-start | bytes 73736 | tf_op jit(solution)/shard_map/ppermute | solution.py:507

commit v7 on v6

--- a/solution.py
+++ b/solution.py
@@ -24,12 +24,12 @@
 SM = pl.BlockSpec(memory_space=pltpu.SMEM)
 
 
-def call(body, outs, ins, scratch=(), specs=None, limit=16):
+def call(body, outs, ins, scratch=(), specs=None, limit=16, to=VM):
     return pl.pallas_call(
         body,
         out_shape=[jax.ShapeDtypeStruct(shape, F32) for shape in outs],
         in_specs=specs or [SM if a.dtype == jnp.int32 else VM for a in ins],
-        out_specs=[VM] * len(outs),
+        out_specs=[to] * len(outs),
         scratch_shapes=[pltpu.VMEM(s, F32) if isinstance(s, tuple) else s for s in scratch],
         compiler_params=pltpu.CompilerParams(vmem_limit_bytes=limit << 20),
     )(*ins)
@@ -47,14 +47,15 @@
 
 
 def select_lanes(x, picks):
-    picks = picks.astype(jnp.bfloat16)
-    out = None
+    pieces = []
     for _ in range(3):
-        piece = x.astype(jnp.bfloat16)
-        x = x - piece.astype(F32)
-        term = jnp.dot(piece, picks, preferred_element_type=F32)
-        out = term if out is None else out + term
-    return out
+        piece = x.astype(jnp.bfloat16).astype(F32)
+        x = x - piece
+        pieces.append(piece)
+    n = x.shape[0]
+    stacked = jnp.concatenate(pieces, 0).astype(jnp.bfloat16)
+    out = jnp.dot(stacked, picks.astype(jnp.bfloat16), preferred_element_type=F32)
+    return (out[:n] + out[n : 2 * n]) + out[2 * n :]
 
 
 def iota(shape, dim):
@@ -202,8 +203,8 @@
     copies = [pltpu.make_async_copy(a, b, sems.at[i]) for i, (a, b) in enumerate(pairs)]
     for copy in copies:
         copy.start()
-    for copy in copies:
-        copy.wait()
+    for i in (2, 3, 4):
+        copies[i].wait()
     g, _ = position()
     odd = g % 2 == 1
     for q in range(SLOTS):
@@ -212,11 +213,12 @@
         for s in range(NS):
             out_ref[s, 10 * q + 8 : 10 * q + 9, :] = patch
             out_ref[s, 10 * q + 9 : 10 * q + 10, :] = wave
-    for s in range(NS):
-        place = (s + NS - 1) % NS
-        layer = jnp.where(odd, EDGE - 1 - place, place)
-        for q in range(SLOTS):
-            for a, ref in enumerate((field_ref, source_ref)):
+    for a, ref in enumerate((field_ref, source_ref)):
+        copies[a].wait()
+        for s in range(NS):
+            place = (s + NS - 1) % NS
+            layer = jnp.where(odd, EDGE - 1 - place, place)
+            for q in range(SLOTS):
                 for part in range(2):
                     row = 10 * q + 4 * a + 2 * part
                     cells = ref[q, part, pl.ds(layer, 1), :]
@@ -380,7 +382,7 @@
     return (lane_roll(e, -1) + lane_roll(e, 1)) + (lane_roll(e, -8) + lane_roll(e, 8))
 
 
-def correct_body(raw_ref, wave_ref, patch_ref, out_ref, grown_ref, smooth_ref):
+def correct_body(raw_ref, wave_ref, patch_ref, out_hbm, grown_ref, smooth_ref, sems):
     g, _ = position()
     odd = g % 2 == 1
     rows = 24
@@ -428,22 +430,26 @@
     wide = (LANES, 2 * CELLS)
     widen = jnp.where(window_lane(wide, 1) == iota(wide, 0), 1.0, 0.0)
     grown_ref[...] = select_lanes(e[2 * SLOTS : 6 * SLOTS], widen)
-    for i in range(EDGE):
-        s = device_at(jnp.where(odd, EDGE - 1 - i, i))
-        for q in range(SLOTS):
+    copies = []
+    for q in range(SLOTS):
+        held = jnp.broadcast_to(patch_ref[q : q + 1, 0:1] >= 0.0, (4, CELLS))
+        for i in range(EDGE):
+            s = device_at(jnp.where(odd, EDGE - 1 - i, i))
             for part in range(2):
                 for h in range(2):
                     row = raw_ref[pl.ds(rows * s + 6 * q + 2 * part + h, 1), :]
-                    smooth_ref[2 * q + part, i : i + 1, LANES * h : LANES * (h + 1)] = row
-    for q in range(SLOTS):
-        held = jnp.broadcast_to(patch_ref[q : q + 1, 0:1] >= 0.0, (4, CELLS))
+                    smooth_ref[q, part, i : i + 1, LANES * h : LANES * (h + 1)] = row
         for i in range(4):
             plane = jnp.where(odd, 3 - i, i)
             line = grown_ref[pl.ds(SLOTS * plane + q, 1), :]
             for part in range(2):
                 extra = jnp.broadcast_to(line[:, CELLS * part : CELLS * (part + 1)], (4, CELLS))
-                value = smooth_ref[2 * q + part, 4 * i : 4 * i + 4] + extra
-                out_ref[q, part, 4 * i : 4 * i + 4] = jnp.where(held, value, 0.0)
+                value = smooth_ref[q, part, 4 * i : 4 * i + 4] + extra
+                smooth_ref[q, part, 4 * i : 4 * i + 4] = jnp.where(held, value, 0.0)
+        copies.append(pltpu.make_async_copy(smooth_ref.at[q], out_hbm.at[q], sems.at[q]))
+        copies[q].start()
+    for copy in copies:
+        copy.wait()
 
 
 def facing(groups, reach):
@@ -515,7 +521,8 @@
         correct_body,
         [(SLOTS, 2, EDGE, CELLS)],
         [back.reshape(NS * 24, LANES), wave, patch],
-        [(EDGE, 2 * CELLS), (2 * SLOTS, EDGE, CELLS)],
+        [(EDGE, 2 * CELLS), (SLOTS, 2, EDGE, CELLS), pltpu.SemaphoreType.DMA((SLOTS,))],
+        to=hbm,
     )
     return out
 

time: 62.2 us -> 62.1 us (level)
  no operation moved by 1% of the time
where the time goes in v7:
time: 62.1 us; the launch traced here: 61.9 us
  blocking collectives  49.6 us (80%)
  Pallas kernels  4.6 us (7%)
  waiting for transfers between devices  4.05 us (7%)
  starting transfers between devices  3.58 us (6%)
    all_to_all x1, blocking collectives, body(): lax.all_to_all(packed, 'sub', 0, 0, tiled=True).reshape(NS * 40, LANES)  20.6 us
    all_to_all x1, blocking collectives, body(): lax.all_to_all(bundle.reshape(NS, 24, LANES), 'sub', 0, 0, tiled=True)  13.7 us
    all_gather x1, blocking collectives, body(): far = lax.all_gather(own, both, axis_index_groups=facing(groups, 2))  8.59 us
    all_gather x1, blocking collectives, body(): lax.all_gather(block, both, axis_index_groups=facing(groups, NS // 2))  6.66 us
    pallas_call x8, Pallas kernels, call(): pl.pallas_call(body, out_shape=[jax.ShapeDtypeStruct(shape, F32) for shap...  4.6 us
    ppermute x1, waiting for transfers between devices, body(): after = lax.ppermute(falling, 'sub', down)  2.4 us
    ppermute x2, starting transfers between devices, body(): ring = lambda x: (lax.ppermute(x, 'sub', up), lax.ppermute(x, 'sub', down))  1.75 us
    ppermute x1, waiting for transfers between devices, body(): before = lax.ppermute(rising, 'sub', up)  1.64 us
  transfers between devices with their start and end apart: 5, of which 2 were waited for; matrix products, arithmetic and copies ran while one was open for 0% of the time, Pallas kernels for 0%

profile of v7, /device:TPU:199, one launch (start us, length us, event | category | flops | bytes accessed | tf_op | source)
XLA Modules:
  0.0 61.9 jit_solution(14069087356526196144)
XLA Ops:
  0.0 1.2 %shard_map.55 = f32[16,40,128]{2,1,0:T(8,128)S(1)} custom-call(f32[4,2,16,256]{3,2,1,0:T(8,128)} %field_hbm.1, f32[4,2,16,256]{3,2,1,0:T(8,128)} %source_hbm.1, s32[4]{0:T(128)} %patch_hbm.1, s32[4]{0:T(128)} %index_hbm.1, f32[16]{0:T(128)} %table_hbm.1), custom_call_target="tpu_custom_call" | custom-call | tf_op jit(solution)/shard_map/pallas_call | solution.py:28
  1.2 20.6 %all_to_all.10 = f32[16,40,128]{2,1,0:T(8,128)S(1)} all-to-all(f32[16,40,128]{2,1,0:T(8,128)S(1)} %shard_map.55), channel_id=1, replica_groups=mesh['grp'=32,'sub'=16] {'sub'}, dimensions={0} | all-to-all | bytes 655360 | tf_op jit(solution)/shard_map/all_to_all | solution.py:498
  21.8 0.3 shard_map.56
  22.1 0.0 collective-permute-start.1
  22.2 1.7 %collective-permute-start = (f32[2,48,256]{2,1,0:T(8,128)S(1)}, f32[2,48,256]{2,1,0:T(8,128)S(1)}, u32[]{:S(2)}, u32[]{:S(2)}) collective-permute-start(f32[2,48,256]{2,1,0:T(8,128)S(1)} %get-tuple-element.20), channel_id=1, source_target_pairs={{0,1},{1,2},{2,3},{3,4},{4,5},{5,6},{6,7},{7,8},{8,9},{9,10},{10,1... | collective-permute-start | bytes 294920 | tf_op jit(solution)/shard_map/ppermute | solution.py:476
  23.9 8.6 %all-gather = f32[400,256]{1,0:T(8,128)S(1)} all-gather(f32[200,256]{1,0:T(8,128)S(1)} %get-tuple-element.18.own_ref), channel_id=2, replica_groups={{17,33},{49,65},{81,97},{113,129},{145,161},{177,193},{209,225},{241,25..., dimensions={0}, use_global_device_ids=true | all-gather | bytes 614400 | tf_op jit(solution)/shard_map/all_gather | solution.py:502
  32.5 0.0 collective-permute-done.1.after_ref
  32.5 0.0 collective-permute-done.before_ref
  32.5 0.3 shard_map.57
  32.8 1.2 %collective-permute-start.2 = (f32[2,48,256]{2,1,0:T(8,128)S(1)}, f32[2,48,256]{2,1,0:T(8,128)S(1)}, u32[]{:S(2)}, u32[]{:S(2)}) collective-permute-start(f32[2,48,256]{2,1,0:T(8,128)S(1)} %get-tuple-element.21), channel_id=1, source_target_pairs={{0,1},{1,2},{2,3},{3,4},{4,5},{5,6},{6,7},{7,8},{8,9},{9,10},{10,1... | collective-permute-start | bytes 294920 | tf_op jit(solution)/shard_map/ppermute | solution.py:507
  33.9 0.0 collective-permute-start.3
  33.9 1.6 %collective-permute-done.2.before_ref = f32[2,48,256]{2,1,0:T(8,128)S(1)} collective-permute-done((f32[2,48,256]{2,1,0:T(8,128)S(1)}, f32[2,48,256]{2,1,0:T(8,128)S(1)}, u32[]{:S(2)}, u32[]{:S(2)}) %collective-permute-start.2) | collective-permute-done | bytes 98336 | tf_op jit(solution)/shard_map/ppermute | solution.py:507
  35.6 2.4 %collective-permute-done.3.after_ref = f32[2,48,256]{2,1,0:T(8,128)S(1)} collective-permute-done((f32[2,48,256]{2,1,0:T(8,128)S(1)}, f32[2,48,256]{2,1,0:T(8,128)S(1)}, u32[]{:S(2)}, u32[]{:S(2)}) %collective-permute-start.3) | collective-permute-done | bytes 98336 | tf_op jit(solution)/shard_map/ppermute | solution.py:508
  38.0 0.8 %shard_map.58 = (f32[2,48,256]{2,1,0:T(8,128)S(1)}, f32[48,128]{1,0:T(8,128)S(1)}, f32[48,128]{1,0:T(8,128)S(1)}) custom-call(f32[200,256]{1,0:T(8,128)S(1)} %get-tuple-element.18.own_ref, f32[48,128]{1,0:T(8,128)S(1)} %get-tuple-element.19.wave_ref.own_wave_ref, f32[2,200,256]{2,1,0:T(8,128)S(1)} %bitcast.6, ...), custom_call_target="tpu_custom_call" | custom-call | tf_op jit(solution)/shard_map/pallas_call | solution.py:28
  38.8 0.7 %collective-permute-start.4 = (f32[48,128]{1,0:T(8,128)S(1)}, f32[48,128]{1,0:T(8,128)S(1)}, u32[]{:S(2)}, u32[]{:S(2)}) collective-permute-start(f32[48,128]{1,0:T(8,128)S(1)} %get-tuple-element.28.values_ref), channel_id=1, source_target_pairs={{4,5},{8,9},{12,13},{5,4},{9,8},{13,12},{20,21},{24,25},{28,29},{2... | collective-permute-start | bytes 73736 | tf_op jit(solution)/shard_map/ppermute | solution.py:513
  39.5 0.2 shard_map.59
  39.7 0.0 collective-permute-done.4.pair_ref
  39.7 0.1 shard_map.60.block_ref
  39.8 6.7 %all-gather.1 = f32[96,128]{1,0:T(8,128)S(1)} all-gather(f32[48,128]{1,0:T(8,128)S(1)} %shard_map.60.block_ref), channel_id=3, replica_groups={{17,33},{49,65},{81,97},{113,129},{145,161},{177,193},{209,225},{241,25..., dimensions={0}, use_global_device_ids=true | all-gather | bytes 73728 | tf_op jit(solution)/shard_map/all_gather | solution.py:517
  46.5 0.4 shard_map.61
  46.9 13.7 %all_to_all.11 = f32[16,24,128]{2,1,0:T(8,128)S(1)} all-to-all(f32[16,24,128]{2,1,0:T(8,128)S(1)} %bitcast.8), channel_id=1, replica_groups=mesh['grp'=32,'sub'=16] {'sub'}, dimensions={0} | all-to-all | bytes 393216 | tf_op jit(solution)/shard_map/all_to_all | solution.py:519
  60.5 1.3 %shard_map.62 = f32[4,2,16,256]{3,2,1,0:T(8,128)} custom-call(f32[384,128]{1,0:T(8,128)S(1)} %bitcast.9, f32[4,128]{1,0:T(4,128)S(1)} %get-tuple-element.29.wave_ref, f32[4,128]{1,0:T(4,128)S(1)} %get-tuple-element.30.patch_ref), custom_call_target="tpu_custom_call" | custom-call | tf_op jit(solution)/shard_map/pallas_call | solution.py:28
Async XLA Ops:
  22.1 10.4 %collective-permute-start.1 = (f32[2,48,256]{2,1,0:T(8,128)S(1)}, f32[2,48,256]{2,1,0:T(8,128)S(1)}, u32[]{:S(2)}, u32[]{:S(2)}) collective-permute-start(f32[2,48,256]{2,1,0:T(8,128)S(1)} %get-tuple-element.20), channel_id=1, source_target_pairs={{1,0},{2,1},{3,2},{4,3},{5,4},{6,5},{7,6},{8,7},{9,8},{10,9},{11,1... | collective-permute-start | bytes 294920 | tf_op jit(solution)/shard_map/ppermute | solution.py:476
  22.2 10.3 %collective-permute-start = (f32[2,48,256]{2,1,0:T(8,128)S(1)}, f32[2,48,256]{2,1,0:T(8,128)S(1)}, u32[]{:S(2)}, u32[]{:S(2)}) collective-permute-start(f32[2,48,256]{2,1,0:T(8,128)S(1)} %get-tuple-element.20), channel_id=1, source_target_pairs={{0,1},{1,2},{2,3},{3,4},{4,5},{5,6},{6,7},{7,8},{8,9},{9,10},{10,1... | collective-permute-start | bytes 294920 | tf_op jit(solution)/shard_map/ppermute | solution.py:476
  32.8 2.8 %collective-permute-start.2 = (f32[2,48,256]{2,1,0:T(8,128)S(1)}, f32[2,48,256]{2,1,0:T(8,128)S(1)}, u32[]{:S(2)}, u32[]{:S(2)}) collective-permute-start(f32[2,48,256]{2,1,0:T(8,128)S(1)} %get-tuple-element.21), channel_id=1, source_target_pairs={{0,1},{1,2},{2,3},{3,4},{4,5},{5,6},{6,7},{7,8},{8,9},{9,10},{10,1... | collective-permute-start | bytes 294920 | tf_op jit(solution)/shard_map/ppermute | solution.py:507
  33.9 4.0 %collective-permute-start.3 = (f32[2,48,256]{2,1,0:T(8,128)S(1)}, f32[2,48,256]{2,1,0:T(8,128)S(1)}, u32[]{:S(2)}, u32[]{:S(2)}) collective-permute-start(f32[2,48,256]{2,1,0:T(8,128)S(1)} %get-tuple-element.22), channel_id=1, source_target_pairs={{1,0},{2,1},{3,2},{4,3},{5,4},{6,5},{7,6},{8,7},{9,8},{10,9},{11,1... | collective-permute-start | bytes 294920 | tf_op jit(solution)/shard_map/ppermute | solution.py:508
  38.8 0.9 %collective-permute-start.4 = (f32[48,128]{1,0:T(8,128)S(1)}, f32[48,128]{1,0:T(8,128)S(1)}, u32[]{:S(2)}, u32[]{:S(2)}) collective-permute-start(f32[48,128]{1,0:T(8,128)S(1)} %get-tuple-element.28.values_ref), channel_id=1, source_target_pairs={{4,5},{8,9},{12,13},{5,4},{9,8},{13,12},{20,21},{24,25},{28,29},{2... | collective-permute-start | bytes 73736 | tf_op jit(solution)/shard_map/ppermute | solution.py:513

commit v8 on v7

--- a/solution.py
+++ b/solution.py
@@ -36,14 +36,14 @@
 
 
 def select(picks, x):
-    picks = picks.astype(jnp.bfloat16)
-    out = None
+    pieces = []
     for _ in range(3):
-        piece = x.astype(jnp.bfloat16)
-        x = x - piece.astype(F32)
-        term = jnp.dot(picks, piece, preferred_element_type=F32)
-        out = term if out is None else out + term
-    return out
+        piece = x.astype(jnp.bfloat16).astype(F32)
+        x = x - piece
+        pieces.append(piece)
+    stacked = jnp.concatenate(pieces, 0).astype(jnp.bfloat16)
+    thrice = jnp.concatenate([picks] * 3, 1).astype(jnp.bfloat16)
+    return jnp.dot(thrice, stacked, preferred_element_type=F32)
 
 
 def select_lanes(x, picks):

time: 62.1 us -> 62.1 us (level)
  no operation moved by 1% of the time
where the time goes in v8:
time: 62.1 us; the launch traced here: 61.9 us
  blocking collectives  49.6 us (80%)
  Pallas kernels  4.62 us (7%)
  waiting for transfers between devices  4.05 us (7%)
  starting transfers between devices  3.57 us (6%)
    all_to_all x1, blocking collectives, body(): lax.all_to_all(packed, 'sub', 0, 0, tiled=True).reshape(NS * 40, LANES)  20.6 us
    all_to_all x1, blocking collectives, body(): lax.all_to_all(bundle.reshape(NS, 24, LANES), 'sub', 0, 0, tiled=True)  13.7 us
    all_gather x1, blocking collectives, body(): far = lax.all_gather(own, both, axis_index_groups=facing(groups, 2))  8.59 us
    all_gather x1, blocking collectives, body(): lax.all_gather(block, both, axis_index_groups=facing(groups, NS // 2))  6.67 us
    pallas_call x8, Pallas kernels, call(): pl.pallas_call(body, out_shape=[jax.ShapeDtypeStruct(shape, F32) for shap...  4.62 us
    ppermute x1, waiting for transfers between devices, body(): after = lax.ppermute(falling, 'sub', down)  2.4 us
    ppermute x2, starting transfers between devices, body(): ring = lambda x: (lax.ppermute(x, 'sub', up), lax.ppermute(x, 'sub', down))  1.74 us
    ppermute x1, waiting for transfers between devices, body(): before = lax.ppermute(rising, 'sub', up)  1.64 us
  transfers between devices with their start and end apart: 5, of which 2 were waited for; matrix products, arithmetic and copies ran while one was open for 0% of the time, Pallas kernels for 0%

profile of v8, /device:TPU:199, one launch (start us, length us, event | category | flops | bytes accessed | tf_op | source)
XLA Modules:
  0.0 61.9 jit_solution(933712948508060037)
XLA Ops:
  0.0 1.2 %shard_map.55 = f32[16,40,128]{2,1,0:T(8,128)S(1)} custom-call(f32[4,2,16,256]{3,2,1,0:T(8,128)} %field_hbm.1, f32[4,2,16,256]{3,2,1,0:T(8,128)} %source_hbm.1, s32[4]{0:T(128)} %patch_hbm.1, s32[4]{0:T(128)} %index_hbm.1, f32[16]{0:T(128)} %table_hbm.1), custom_call_target="tpu_custom_call" | custom-call | tf_op jit(solution)/shard_map/pallas_call | solution.py:28
  1.2 20.6 %all_to_all.10 = f32[16,40,128]{2,1,0:T(8,128)S(1)} all-to-all(f32[16,40,128]{2,1,0:T(8,128)S(1)} %shard_map.55), channel_id=1, replica_groups=mesh['grp'=32,'sub'=16] {'sub'}, dimensions={0} | all-to-all | bytes 655360 | tf_op jit(solution)/shard_map/all_to_all | solution.py:498
  21.8 0.3 shard_map.56
  22.2 0.0 collective-permute-start.1
  22.2 1.7 %collective-permute-start = (f32[2,48,256]{2,1,0:T(8,128)S(1)}, f32[2,48,256]{2,1,0:T(8,128)S(1)}, u32[]{:S(2)}, u32[]{:S(2)}) collective-permute-start(f32[2,48,256]{2,1,0:T(8,128)S(1)} %get-tuple-element.20), channel_id=1, source_target_pairs={{0,1},{1,2},{2,3},{3,4},{4,5},{5,6},{6,7},{7,8},{8,9},{9,10},{10,1... | collective-permute-start | bytes 294920 | tf_op jit(solution)/shard_map/ppermute | solution.py:476
  23.9 8.6 %all-gather = f32[400,256]{1,0:T(8,128)S(1)} all-gather(f32[200,256]{1,0:T(8,128)S(1)} %get-tuple-element.18.own_ref), channel_id=2, replica_groups={{17,33},{49,65},{81,97},{113,129},{145,161},{177,193},{209,225},{241,25..., dimensions={0}, use_global_device_ids=true | all-gather | bytes 614400 | tf_op jit(solution)/shard_map/all_gather | solution.py:502
  32.5 0.0 collective-permute-done.1.after_ref
  32.5 0.0 collective-permute-done.before_ref
  32.5 0.3 shard_map.57
  32.8 1.2 %collective-permute-start.2 = (f32[2,48,256]{2,1,0:T(8,128)S(1)}, f32[2,48,256]{2,1,0:T(8,128)S(1)}, u32[]{:S(2)}, u32[]{:S(2)}) collective-permute-start(f32[2,48,256]{2,1,0:T(8,128)S(1)} %get-tuple-element.21), channel_id=1, source_target_pairs={{0,1},{1,2},{2,3},{3,4},{4,5},{5,6},{6,7},{7,8},{8,9},{9,10},{10,1... | collective-permute-start | bytes 294920 | tf_op jit(solution)/shard_map/ppermute | solution.py:507
  34.0 0.0 collective-permute-start.3
  34.0 1.6 %collective-permute-done.2.before_ref = f32[2,48,256]{2,1,0:T(8,128)S(1)} collective-permute-done((f32[2,48,256]{2,1,0:T(8,128)S(1)}, f32[2,48,256]{2,1,0:T(8,128)S(1)}, u32[]{:S(2)}, u32[]{:S(2)}) %collective-permute-start.2) | collective-permute-done | bytes 98336 | tf_op jit(solution)/shard_map/ppermute | solution.py:507
  35.6 2.4 %collective-permute-done.3.after_ref = f32[2,48,256]{2,1,0:T(8,128)S(1)} collective-permute-done((f32[2,48,256]{2,1,0:T(8,128)S(1)}, f32[2,48,256]{2,1,0:T(8,128)S(1)}, u32[]{:S(2)}, u32[]{:S(2)}) %collective-permute-start.3) | collective-permute-done | bytes 98336 | tf_op jit(solution)/shard_map/ppermute | solution.py:508
  38.0 0.8 %shard_map.58 = (f32[2,48,256]{2,1,0:T(8,128)S(1)}, f32[48,128]{1,0:T(8,128)S(1)}, f32[48,128]{1,0:T(8,128)S(1)}) custom-call(f32[200,256]{1,0:T(8,128)S(1)} %get-tuple-element.18.own_ref, f32[48,128]{1,0:T(8,128)S(1)} %get-tuple-element.19.wave_ref.own_wave_ref, f32[2,200,256]{2,1,0:T(8,128)S(1)} %bitcast.6, ...), custom_call_target="tpu_custom_call" | custom-call | tf_op jit(solution)/shard_map/pallas_call | solution.py:28
  38.9 0.7 %collective-permute-start.4 = (f32[48,128]{1,0:T(8,128)S(1)}, f32[48,128]{1,0:T(8,128)S(1)}, u32[]{:S(2)}, u32[]{:S(2)}) collective-permute-start(f32[48,128]{1,0:T(8,128)S(1)} %get-tuple-element.28.values_ref), channel_id=1, source_target_pairs={{4,5},{8,9},{12,13},{5,4},{9,8},{13,12},{20,21},{24,25},{28,29},{2... | collective-permute-start | bytes 73736 | tf_op jit(solution)/shard_map/ppermute | solution.py:513
  39.5 0.2 shard_map.59
  39.7 0.0 collective-permute-done.4.pair_ref
  39.7 0.1 shard_map.60.block_ref
  39.8 6.7 %all-gather.1 = f32[96,128]{1,0:T(8,128)S(1)} all-gather(f32[48,128]{1,0:T(8,128)S(1)} %shard_map.60.block_ref), channel_id=3, replica_groups={{17,33},{49,65},{81,97},{113,129},{145,161},{177,193},{209,225},{241,25..., dimensions={0}, use_global_device_ids=true | all-gather | bytes 73728 | tf_op jit(solution)/shard_map/all_gather | solution.py:517
  46.5 0.4 shard_map.61
  46.9 13.7 %all_to_all.11 = f32[16,24,128]{2,1,0:T(8,128)S(1)} all-to-all(f32[16,24,128]{2,1,0:T(8,128)S(1)} %bitcast.8), channel_id=1, replica_groups=mesh['grp'=32,'sub'=16] {'sub'}, dimensions={0} | all-to-all | bytes 393216 | tf_op jit(solution)/shard_map/all_to_all | solution.py:519
  60.5 1.3 %shard_map.62 = f32[4,2,16,256]{3,2,1,0:T(8,128)} custom-call(f32[384,128]{1,0:T(8,128)S(1)} %bitcast.9, f32[4,128]{1,0:T(4,128)S(1)} %get-tuple-element.29.wave_ref, f32[4,128]{1,0:T(4,128)S(1)} %get-tuple-element.30.patch_ref), custom_call_target="tpu_custom_call" | custom-call | tf_op jit(solution)/shard_map/pallas_call | solution.py:28
Async XLA Ops:
  22.2 10.3 %collective-permute-start.1 = (f32[2,48,256]{2,1,0:T(8,128)S(1)}, f32[2,48,256]{2,1,0:T(8,128)S(1)}, u32[]{:S(2)}, u32[]{:S(2)}) collective-permute-start(f32[2,48,256]{2,1,0:T(8,128)S(1)} %get-tuple-element.20), channel_id=1, source_target_pairs={{1,0},{2,1},{3,2},{4,3},{5,4},{6,5},{7,6},{8,7},{9,8},{10,9},{11,1... | collective-permute-start | bytes 294920 | tf_op jit(solution)/shard_map/ppermute | solution.py:476
  22.2 10.3 %collective-permute-start = (f32[2,48,256]{2,1,0:T(8,128)S(1)}, f32[2,48,256]{2,1,0:T(8,128)S(1)}, u32[]{:S(2)}, u32[]{:S(2)}) collective-permute-start(f32[2,48,256]{2,1,0:T(8,128)S(1)} %get-tuple-element.20), channel_id=1, source_target_pairs={{0,1},{1,2},{2,3},{3,4},{4,5},{5,6},{6,7},{7,8},{8,9},{9,10},{10,1... | collective-permute-start | bytes 294920 | tf_op jit(solution)/shard_map/ppermute | solution.py:476
  32.8 2.8 %collective-permute-start.2 = (f32[2,48,256]{2,1,0:T(8,128)S(1)}, f32[2,48,256]{2,1,0:T(8,128)S(1)}, u32[]{:S(2)}, u32[]{:S(2)}) collective-permute-start(f32[2,48,256]{2,1,0:T(8,128)S(1)} %get-tuple-element.21), channel_id=1, source_target_pairs={{0,1},{1,2},{2,3},{3,4},{4,5},{5,6},{6,7},{7,8},{8,9},{9,10},{10,1... | collective-permute-start | bytes 294920 | tf_op jit(solution)/shard_map/ppermute | solution.py:507
  34.0 4.0 %collective-permute-start.3 = (f32[2,48,256]{2,1,0:T(8,128)S(1)}, f32[2,48,256]{2,1,0:T(8,128)S(1)}, u32[]{:S(2)}, u32[]{:S(2)}) collective-permute-start(f32[2,48,256]{2,1,0:T(8,128)S(1)} %get-tuple-element.22), channel_id=1, source_target_pairs={{1,0},{2,1},{3,2},{4,3},{5,4},{6,5},{7,6},{8,7},{9,8},{10,9},{11,1... | collective-permute-start | bytes 294920 | tf_op jit(solution)/shard_map/ppermute | solution.py:508
  38.9 0.9 %collective-permute-start.4 = (f32[48,128]{1,0:T(8,128)S(1)}, f32[48,128]{1,0:T(8,128)S(1)}, u32[]{:S(2)}, u32[]{:S(2)}) collective-permute-start(f32[48,128]{1,0:T(8,128)S(1)} %get-tuple-element.28.values_ref), channel_id=1, source_target_pairs={{4,5},{8,9},{12,13},{5,4},{9,8},{13,12},{20,21},{24,25},{28,29},{2... | collective-permute-start | bytes 73736 | tf_op jit(solution)/shard_map/ppermute | solution.py:513

commit v9 on v8

--- a/solution.py
+++ b/solution.py
@@ -284,6 +284,20 @@
     return part * 64 + (inside // (4 * EDGE) + 2) * 8 + (inside % EDGE) // 4 + 2
 
 
+def block_sums(u):
+    lane = iota(u[0][0].shape, 1)
+    kept = (lane // EDGE % 4 == 0) & (lane % 4 == 0)
+    out = None
+    for part in range(2):
+        for h in range(2):
+            t = u[part][h]
+            for step in (1, 2, EDGE, 2 * EDGE):
+                t = t + lane_roll(t, -step)
+            t = lane_roll(jnp.where(kept, t, 0.0), 2 * part + h)
+            out = t if out is None else out + t
+    return out
+
+
 def second_body(own_ref, wave_ref, far_ref, before_ref, after_ref, mine_ref, field_ref, sums_ref, values_ref):
     _, s = position()
     first, last = s == 0, s == NS - 1
@@ -303,11 +317,12 @@
     for part in range(2):
         put(field_ref, part, two[part])
     r = residual(two, [in_plane(two[0]), in_plane(two[1])], rights, wave)
-    rows = jnp.concatenate(
-        [jnp.concatenate(r[0] + r[1], 1), jnp.concatenate(two[0] + two[1], 1)], 0
-    )
-    shape = (2 * CELLS, LANES)
-    gather = jnp.where(window_lane(shape, 0) == iota(shape, 1), 1.0, 0.0)
+    rows = jnp.concatenate([block_sums(r), block_sums(two)], 0)
+    shape = (LANES, LANES)
+    source = iota(shape, 0)
+    half, base = source % 4, source - source % 4
+    target = half // 2 * 64 + (half % 2 * 2 + base // 64 + 2) * 8 + base % EDGE // 4 + 2
+    gather = jnp.where((base // EDGE % 4 == 0) & (target == iota(shape, 1)), 1.0, 0.0)
     sums = select_lanes(rows, gather)
     lane = iota((PATCHES, LANES), 1)
     values = sums[PATCHES:]

time: 62.1 us -> 62.4 us (level)
  no operation moved by 1% of the time
where the time goes in v9:
time: 62.4 us; the launch traced here: 62.2 us
  blocking collectives  49.6 us (79%)
  Pallas kernels  4.91 us (8%)
  waiting for transfers between devices  4.05 us (6%)
  starting transfers between devices  3.57 us (6%)
    all_to_all x1, blocking collectives, body(): lax.all_to_all(packed, 'sub', 0, 0, tiled=True).reshape(NS * 40, LANES)  20.6 us
    all_to_all x1, blocking collectives, body(): lax.all_to_all(bundle.reshape(NS, 24, LANES), 'sub', 0, 0, tiled=True)  13.7 us
    all_gather x1, blocking collectives, body(): far = lax.all_gather(own, both, axis_index_groups=facing(groups, 2))  8.59 us
    all_gather x1, blocking collectives, body(): lax.all_gather(block, both, axis_index_groups=facing(groups, NS // 2))  6.67 us
    pallas_call x8, Pallas kernels, call(): pl.pallas_call(body, out_shape=[jax.ShapeDtypeStruct(shape, F32) for shap...  4.91 us
    ppermute x1, waiting for transfers between devices, body(): after = lax.ppermute(falling, 'sub', down)  2.4 us
    ppermute x2, starting transfers between devices, body(): ring = lambda x: (lax.ppermute(x, 'sub', up), lax.ppermute(x, 'sub', down))  1.74 us
    ppermute x1, waiting for transfers between devices, body(): before = lax.ppermute(rising, 'sub', up)  1.64 us
  transfers between devices with their start and end apart: 5, of which 2 were waited for; matrix products, arithmetic and copies ran while one was open for 0% of the time, Pallas kernels for 0%

profile of v9, /device:TPU:199, one launch (start us, length us, event | category | flops | bytes accessed | tf_op | source)
XLA Modules:
  0.0 62.2 jit_solution(3920343635322952534)
XLA Ops:
  0.0 1.2 %shard_map.55 = f32[16,40,128]{2,1,0:T(8,128)S(1)} custom-call(f32[4,2,16,256]{3,2,1,0:T(8,128)} %field_hbm.1, f32[4,2,16,256]{3,2,1,0:T(8,128)} %source_hbm.1, s32[4]{0:T(128)} %patch_hbm.1, s32[4]{0:T(128)} %index_hbm.1, f32[16]{0:T(128)} %table_hbm.1), custom_call_target="tpu_custom_call" | custom-call | tf_op jit(solution)/shard_map/pallas_call | solution.py:28
  1.2 20.6 %all_to_all.10 = f32[16,40,128]{2,1,0:T(8,128)S(1)} all-to-all(f32[16,40,128]{2,1,0:T(8,128)S(1)} %shard_map.55), channel_id=1, replica_groups=mesh['grp'=32,'sub'=16] {'sub'}, dimensions={0} | all-to-all | bytes 655360 | tf_op jit(solution)/shard_map/all_to_all | solution.py:513
  21.8 0.3 shard_map.56
  22.2 0.0 collective-permute-start.1
  22.2 1.7 %collective-permute-start = (f32[2,48,256]{2,1,0:T(8,128)S(1)}, f32[2,48,256]{2,1,0:T(8,128)S(1)}, u32[]{:S(2)}, u32[]{:S(2)}) collective-permute-start(f32[2,48,256]{2,1,0:T(8,128)S(1)} %get-tuple-element.20), channel_id=1, source_target_pairs={{0,1},{1,2},{2,3},{3,4},{4,5},{5,6},{6,7},{7,8},{8,9},{9,10},{10,1... | collective-permute-start | bytes 294920 | tf_op jit(solution)/shard_map/ppermute | solution.py:491
  23.9 8.6 %all-gather = f32[400,256]{1,0:T(8,128)S(1)} all-gather(f32[200,256]{1,0:T(8,128)S(1)} %get-tuple-element.18.own_ref), channel_id=2, replica_groups={{17,33},{49,65},{81,97},{113,129},{145,161},{177,193},{209,225},{241,25..., dimensions={0}, use_global_device_ids=true | all-gather | bytes 614400 | tf_op jit(solution)/shard_map/all_gather | solution.py:517
  32.5 0.0 collective-permute-done.1.after_ref
  32.5 0.0 collective-permute-done.before_ref
  32.5 0.3 shard_map.57
  32.8 1.2 %collective-permute-start.2 = (f32[2,48,256]{2,1,0:T(8,128)S(1)}, f32[2,48,256]{2,1,0:T(8,128)S(1)}, u32[]{:S(2)}, u32[]{:S(2)}) collective-permute-start(f32[2,48,256]{2,1,0:T(8,128)S(1)} %get-tuple-element.21), channel_id=1, source_target_pairs={{0,1},{1,2},{2,3},{3,4},{4,5},{5,6},{6,7},{7,8},{8,9},{9,10},{10,1... | collective-permute-start | bytes 294920 | tf_op jit(solution)/shard_map/ppermute | solution.py:522
  34.0 0.0 collective-permute-start.3
  34.0 1.6 %collective-permute-done.2.before_ref = f32[2,48,256]{2,1,0:T(8,128)S(1)} collective-permute-done((f32[2,48,256]{2,1,0:T(8,128)S(1)}, f32[2,48,256]{2,1,0:T(8,128)S(1)}, u32[]{:S(2)}, u32[]{:S(2)}) %collective-permute-start.2) | collective-permute-done | bytes 98336 | tf_op jit(solution)/shard_map/ppermute | solution.py:522
  35.6 2.4 %collective-permute-done.3.after_ref = f32[2,48,256]{2,1,0:T(8,128)S(1)} collective-permute-done((f32[2,48,256]{2,1,0:T(8,128)S(1)}, f32[2,48,256]{2,1,0:T(8,128)S(1)}, u32[]{:S(2)}, u32[]{:S(2)}) %collective-permute-start.3) | collective-permute-done | bytes 98336 | tf_op jit(solution)/shard_map/ppermute | solution.py:523
  38.0 1.1 %shard_map.58 = (f32[2,48,256]{2,1,0:T(8,128)S(1)}, f32[48,128]{1,0:T(8,128)S(1)}, f32[48,128]{1,0:T(8,128)S(1)}) custom-call(f32[200,256]{1,0:T(8,128)S(1)} %get-tuple-element.18.own_ref, f32[48,128]{1,0:T(8,128)S(1)} %get-tuple-element.19.wave_ref.own_wave_ref, f32[2,200,256]{2,1,0:T(8,128)S(1)} %bitcast.6, ...), custom_call_target="tpu_custom_call" | custom-call | tf_op jit(solution)/shard_map/pallas_call | solution.py:28
  39.1 0.7 %collective-permute-start.4 = (f32[48,128]{1,0:T(8,128)S(1)}, f32[48,128]{1,0:T(8,128)S(1)}, u32[]{:S(2)}, u32[]{:S(2)}) collective-permute-start(f32[48,128]{1,0:T(8,128)S(1)} %get-tuple-element.28.values_ref), channel_id=1, source_target_pairs={{4,5},{8,9},{12,13},{5,4},{9,8},{13,12},{20,21},{24,25},{28,29},{2... | collective-permute-start | bytes 73736 | tf_op jit(solution)/shard_map/ppermute | solution.py:528
  39.8 0.2 shard_map.59
  40.0 0.0 collective-permute-done.4.pair_ref
  40.0 0.1 shard_map.60.block_ref
  40.1 6.7 %all-gather.1 = f32[96,128]{1,0:T(8,128)S(1)} all-gather(f32[48,128]{1,0:T(8,128)S(1)} %shard_map.60.block_ref), channel_id=3, replica_groups={{17,33},{49,65},{81,97},{113,129},{145,161},{177,193},{209,225},{241,25..., dimensions={0}, use_global_device_ids=true | all-gather | bytes 73728 | tf_op jit(solution)/shard_map/all_gather | solution.py:532
  46.8 0.4 shard_map.61
  47.2 13.7 %all_to_all.11 = f32[16,24,128]{2,1,0:T(8,128)S(1)} all-to-all(f32[16,24,128]{2,1,0:T(8,128)S(1)} %bitcast.8), channel_id=1, replica_groups=mesh['grp'=32,'sub'=16] {'sub'}, dimensions={0} | all-to-all | bytes 393216 | tf_op jit(solution)/shard_map/all_to_all | solution.py:534
  60.8 1.3 %shard_map.62 = f32[4,2,16,256]{3,2,1,0:T(8,128)} custom-call(f32[384,128]{1,0:T(8,128)S(1)} %bitcast.9, f32[4,128]{1,0:T(4,128)S(1)} %get-tuple-element.29.wave_ref, f32[4,128]{1,0:T(4,128)S(1)} %get-tuple-element.30.patch_ref), custom_call_target="tpu_custom_call" | custom-call | tf_op jit(solution)/shard_map/pallas_call | solution.py:28
Async XLA Ops:
  22.2 10.3 %collective-permute-start.1 = (f32[2,48,256]{2,1,0:T(8,128)S(1)}, f32[2,48,256]{2,1,0:T(8,128)S(1)}, u32[]{:S(2)}, u32[]{:S(2)}) collective-permute-start(f32[2,48,256]{2,1,0:T(8,128)S(1)} %get-tuple-element.20), channel_id=1, source_target_pairs={{1,0},{2,1},{3,2},{4,3},{5,4},{6,5},{7,6},{8,7},{9,8},{10,9},{11,1... | collective-permute-start | bytes 294920 | tf_op jit(solution)/shard_map/ppermute | solution.py:491
  22.2 10.3 %collective-permute-start = (f32[2,48,256]{2,1,0:T(8,128)S(1)}, f32[2,48,256]{2,1,0:T(8,128)S(1)}, u32[]{:S(2)}, u32[]{:S(2)}) collective-permute-start(f32[2,48,256]{2,1,0:T(8,128)S(1)} %get-tuple-element.20), channel_id=1, source_target_pairs={{0,1},{1,2},{2,3},{3,4},{4,5},{5,6},{6,7},{7,8},{8,9},{9,10},{10,1... | collective-permute-start | bytes 294920 | tf_op jit(solution)/shard_map/ppermute | solution.py:491
  32.8 2.8 %collective-permute-start.2 = (f32[2,48,256]{2,1,0:T(8,128)S(1)}, f32[2,48,256]{2,1,0:T(8,128)S(1)}, u32[]{:S(2)}, u32[]{:S(2)}) collective-permute-start(f32[2,48,256]{2,1,0:T(8,128)S(1)} %get-tuple-element.21), channel_id=1, source_target_pairs={{0,1},{1,2},{2,3},{3,4},{4,5},{5,6},{6,7},{7,8},{8,9},{9,10},{10,1... | collective-permute-start | bytes 294920 | tf_op jit(solution)/shard_map/ppermute | solution.py:522
  34.0 4.0 %collective-permute-start.3 = (f32[2,48,256]{2,1,0:T(8,128)S(1)}, f32[2,48,256]{2,1,0:T(8,128)S(1)}, u32[]{:S(2)}, u32[]{:S(2)}) collective-permute-start(f32[2,48,256]{2,1,0:T(8,128)S(1)} %get-tuple-element.22), channel_id=1, source_target_pairs={{1,0},{2,1},{3,2},{4,3},{5,4},{6,5},{7,6},{8,7},{9,8},{10,9},{11,1... | collective-permute-start | bytes 294920 | tf_op jit(solution)/shard_map/ppermute | solution.py:523
  39.1 0.9 %collective-permute-start.4 = (f32[48,128]{1,0:T(8,128)S(1)}, f32[48,128]{1,0:T(8,128)S(1)}, u32[]{:S(2)}, u32[]{:S(2)}) collective-permute-start(f32[48,128]{1,0:T(8,128)S(1)} %get-tuple-element.28.values_ref), channel_id=1, source_target_pairs={{4,5},{8,9},{12,13},{5,4},{9,8},{13,12},{20,21},{24,25},{28,29},{2... | collective-permute-start | bytes 73736 | tf_op jit(solution)/shard_map/ppermute | solution.py:528
